TPU v7x, 32 devices: a whole 2x2x4 slice. The times are simulated.
32 devices in a mesh: seq: 2 (over core), head: 2 (over y), blk: 8 (over z, x).
Axes of the slice: x: 2, y: 2, z: 4, core: 2. Of those that a mesh axis runs over, the one named last changes fastest.
Arguments:
- stream: bfloat16 [4096, 2048], P(('seq', 'head', 'blk')), may hold values from -6 to 6
- attn_gain: bfloat16 [2048], P(('seq', 'head', 'blk')), may hold values from 0.5 to 1.5
- qkv_weight: bfloat16 [2048, 2560], P(('seq', 'head', 'blk')), may hold values from -0.125 to 0.125
- qkv_adapt: bfloat16 [2048, 256], P(('seq', 'head', 'blk')), may hold values from -0.125 to 0.125
- qkv_expand: bfloat16 [256, 2560], P(('seq', 'head', 'blk')), may hold values from -0.375 to 0.375
- out_weight: bfloat16 [2048, 2048], P(('seq', 'head', 'blk')), may hold values from -1 to 1
- out_adapt: bfloat16 [2048, 256], P(('seq', 'head', 'blk')), may hold values from -1 to 1
- out_expand: bfloat16 [256, 2048], P(('seq', 'head', 'blk')), may hold values from -0.375 to 0.375
- ffn_gain: bfloat16 [2048], P(('seq', 'head', 'blk')), may hold values from 0.5 to 1.5
- gateup_weight: bfloat16 [16384, 2, 2048], P(('seq', 'head', 'blk')), may hold values from -0.125 to 0.125
- gateup_adapt: bfloat16 [2048, 256], P(('seq', 'head', 'blk')), may hold values from -0.125 to 0.125
- gateup_expand: bfloat16 [16384, 2, 256], P(('seq', 'head', 'blk')), may hold values from -0.375 to 0.375
- down_weight: bfloat16 [16384, 2048], P(('seq', 'head', 'blk')), may hold values from -0.046875 to 0.046875
- down_adapt: bfloat16 [16384, 256], P(('seq', 'head', 'blk')), may hold values from -0.046875 to 0.046875
- down_expand: bfloat16 [256, 2048], P(('seq', 'head', 'blk')), may hold values from -0.375 to 0.375
- cotangent: bfloat16 [4096, 2048], P(('seq', 'head', 'blk')), may hold values from -6 to 6
Outputs:
- result: bfloat16 [4096, 2048], P(('seq', 'head', 'blk'))
- stream_grad: float32 [4096, 2048], P(('seq', 'head', 'blk'))
- attngain_grad: float32 [2048], P(('seq', 'head', 'blk'))
- qkvweight_grad: float32 [2048, 2560], P(('seq', 'head', 'blk'))
- qkvadapt_grad: float32 [2048, 256], P(('seq', 'head', 'blk'))
- qkvexpand_grad: float32 [256, 2560], P(('seq', 'head', 'blk'))
- outweight_grad: float32 [2048, 2048], P(('seq', 'head', 'blk'))
- outadapt_grad: float32 [2048, 256], P(('seq', 'head', 'blk'))
- outexpand_grad: float32 [256, 2048], P(('seq', 'head', 'blk'))
- ffngain_grad: float32 [2048], P(('seq', 'head', 'blk'))
- gateweight_grad: float32 [16384, 2, 2048], P(('seq', 'head', 'blk'))
- gateadapt_grad: float32 [2048, 256], P(('seq', 'head', 'blk'))
- gateexpand_grad: float32 [16384, 2, 256], P(('seq', 'head', 'blk'))
- downweight_grad: float32 [16384, 2048], P(('seq', 'head', 'blk'))
- downadapt_grad: float32 [16384, 256], P(('seq', 'head', 'blk'))
- downexpand_grad: float32 [256, 2048], P(('seq', 'head', 'blk'))
- root_means: float32 [3, 4096], P(None, ('seq', 'head', 'blk'))
All inputs are finite; a program needn't handle non-finite values.
Results may differ from a plain program's by a relative error of at most 0.023.
Values may be sent and summed in bfloat16 or wider, within the bound.
No kernel may reach another device: no remote copies, remote signals or barrier semaphores. Data moves between devices by JAX's collectives and lax.ppermute only.
A program may use at most 320 MiB of HBM per device.

v0:
```python
import math

import jax
import jax.numpy as jnp
from jax import lax
from jax.sharding import PartitionSpec as P

D = 2048
H = 8
DH = 256
R = 256
KB = 512


EPSILON = 1e-06
NEGATIVE = -1e30


def product(former, latter):
    return jnp.dot(former, latter, preferred_element_type=jnp.float32)


def product_back(former, latter):
    return lax.dot_general(
        former, latter, (((1,), (1,)), ((), ())), preferred_element_type=jnp.float32
    )


def product_rows(former, latter):
    return lax.dot_general(
        former, latter, (((0,), (0,)), ((), ())), preferred_element_type=jnp.float32
    )


def rope_tables(positions, full_width):
    half_width = full_width // 2
    rates = jnp.exp(
        jnp.arange(half_width, dtype=jnp.float32) * (-2.0 * math.log(10000.0) / full_width)
    )
    angles = positions.astype(jnp.float32)[:, None] * rates[None, :]
    return (jnp.cos(angles), jnp.sin(angles))


def rotate(values, cosine, sine_part):
    half_width = values.shape[-1] // 2
    former = values[..., :half_width]
    latter = values[..., half_width:]
    return jnp.concatenate(
        [former * cosine - latter * sine_part, latter * cosine + former * sine_part], axis=-1
    )


def unit_rows(values):
    inverse = lax.rsqrt(jnp.mean(values * values, axis=-1, keepdims=True) + EPSILON)
    return (values * inverse, inverse)


def norm_back(grad_in, scaled_rows, inverse, gain_row):
    weighted = grad_in * gain_row
    return inverse * (
        weighted - scaled_rows * jnp.mean(weighted * scaled_rows, axis=-1, keepdims=True)
    )


def gated_units(gate_up):
    return jax.nn.gelu(gate_up[:, 0], approximate=True) * gate_up[:, 1]


def gated_back(gate_up, grad_hidden):
    ignored, pullback = jax.vjp(gated_units, gate_up)
    return pullback(grad_hidden)[0]


def root_mean(values):
    return jnp.sqrt(jnp.mean(values * values, axis=-1))


def body(
    stream,
    attn_gain,
    qkv_weight,
    qkv_adapt,
    qkv_expand,
    out_weight,
    out_adapt,
    out_expand,
    ffn_gain,
    gateup_weight,
    gateup_adapt,
    gateup_expand,
    down_weight,
    down_adapt,
    down_expand,
    cotangent,
):
    tokens = stream.shape[0]
    units = gateup_weight.shape[0]
    head_count = lax.axis_size("head")
    block_count = lax.axis_size("blk")
    seq_length = tokens * head_count * block_count
    local_heads = H // head_count
    head_rank = lax.axis_index("head")
    block_rank = lax.axis_index("blk")
    own_start = (head_rank * block_count + block_rank) * tokens
    own_pos = own_start + jnp.arange(tokens, dtype=jnp.int32)
    score_scale = DH ** (-0.5)
    (
        gain_one,
        qkv_full,
        qkv_into,
        qkv_from,
        proj_full,
        proj_into,
        proj_from,
        gain_two,
        ffn_into,
        down_from,
    ) = (
        lax.all_gather(attn_gain, ("seq", "head", "blk"), axis=0, tiled=True),
        lax.all_gather(qkv_weight, ("seq", "head", "blk"), axis=0, tiled=True),
        lax.all_gather(qkv_adapt, ("seq", "head", "blk"), axis=0, tiled=True),
        lax.all_gather(qkv_expand, ("seq", "head", "blk"), axis=0, tiled=True),
        lax.all_gather(out_weight, ("seq", "head", "blk"), axis=0, tiled=True),
        lax.all_gather(out_adapt, ("seq", "head", "blk"), axis=0, tiled=True),
        lax.all_gather(out_expand, ("seq", "head", "blk"), axis=0, tiled=True),
        lax.all_gather(ffn_gain, ("seq", "head", "blk"), axis=0, tiled=True),
        lax.all_gather(gateup_adapt, ("seq", "head", "blk"), axis=0, tiled=True),
        lax.all_gather(down_expand, ("seq", "head", "blk"), axis=0, tiled=True),
    )
    gain_one = gain_one.astype(jnp.float32)
    gain_two = gain_two.astype(jnp.float32)
    residual = stream.astype(jnp.float32)
    unit_one, inverse_one = unit_rows(residual)
    normed_one = (unit_one * gain_one).astype(jnp.bfloat16)
    lowrank_one = product(normed_one, qkv_into).astype(jnp.bfloat16)
    joined = product(normed_one, qkv_full) + product(lowrank_one, qkv_from)
    cosine, sine_part = rope_tables(own_pos, DH)
    queries = rotate(
        joined[:, : H * DH].reshape(tokens, H, DH), cosine[:, None, :], sine_part[:, None, :]
    ).astype(jnp.bfloat16)
    keys = rotate(joined[:, H * DH : H * DH + DH], cosine, sine_part).astype(jnp.bfloat16)
    values = joined[:, H * DH + DH :].astype(jnp.bfloat16)
    keys_all = lax.all_gather(
        jnp.concatenate([keys, values], axis=1), ("head", "blk"), axis=0, tiled=True
    )
    head_rows = lax.all_to_all(queries, "head", split_axis=1, concat_axis=0, tiled=True)
    rows_here = head_rows.shape[0]
    source = jnp.arange(rows_here, dtype=jnp.int32)
    head_pos = (source // tokens * block_count + block_rank) * tokens + source % tokens
    head_blocks = (((head_count - 1) * block_count + block_rank) * tokens + tokens - 1) // KB + 1

    def block_scores(step_index, query_rows, query_pos):
        key_block = lax.dynamic_slice_in_dim(keys_all, step_index * KB, KB, 0)
        key_pos = step_index * KB + jnp.arange(KB, dtype=jnp.int32)
        scores = (
            jnp.einsum(
                "qhe,ke->qhk", query_rows, key_block[:, :DH], preferred_element_type=jnp.float32
            )
            * score_scale
        )
        visible = key_pos[None, None, :] <= query_pos[:, None, None]
        return (key_block, jnp.where(visible, scores, NEGATIVE), visible)

    def find_top(step_index, carried):
        row_top, row_total = carried
        ignored, scores, visible = block_scores(step_index, head_rows, head_pos)
        new_top = jnp.maximum(row_top, jnp.max(scores, axis=-1))
        raised = jnp.where(visible, jnp.exp(scores - new_top[..., None]), 0.0)
        return (new_top, row_total * jnp.exp(row_top - new_top) + jnp.sum(raised, axis=-1))

    start_top = jnp.full((rows_here, local_heads), NEGATIVE, jnp.float32)
    row_top, row_total = lax.fori_loop(
        0, head_blocks, find_top, (start_top, jnp.zeros((rows_here, local_heads), jnp.float32))
    )
    log_total = row_top + jnp.log(row_total)

    def gather_out(step_index, acc_rows):
        key_block, scores, visible = block_scores(step_index, head_rows, head_pos)
        shares = jnp.where(visible, jnp.exp(scores - log_total[..., None]), 0.0).astype(
            jnp.bfloat16
        )
        return acc_rows + jnp.einsum(
            "qhk,ke->qhe", shares, key_block[:, DH:], preferred_element_type=jnp.float32
        )

    attended = lax.fori_loop(
        0, head_blocks, gather_out, jnp.zeros((rows_here, local_heads, DH), jnp.float32)
    )
    attended_tok, log_tok = (
        lax.all_to_all(attended, "head", split_axis=0, concat_axis=1, tiled=True),
        lax.all_to_all(log_total, "head", split_axis=0, concat_axis=1, tiled=True),
    )
    attn_rows = attended_tok.reshape(tokens, H * DH).astype(jnp.bfloat16)
    lowrank_two = product(attn_rows, proj_into).astype(jnp.bfloat16)
    branch_attn = product(attn_rows, proj_full) + product(lowrank_two, proj_from)
    middle = residual + branch_attn
    unit_two, inverse_two = unit_rows(middle)
    normed_two = (unit_two * gain_two).astype(jnp.bfloat16)
    lowrank_three = product(normed_two, ffn_into).astype(jnp.bfloat16)
    group_gate, group_expand, group_down, group_adapt = (
        lax.all_gather(gateup_weight, ("seq", "head"), axis=0, tiled=True),
        lax.all_gather(gateup_expand, ("seq", "head"), axis=0, tiled=True),
        lax.all_gather(down_weight, ("seq", "head"), axis=0, tiled=True),
        lax.all_gather(down_adapt, ("seq", "head"), axis=0, tiled=True),
    )
    rows_group, lowrank_group = (
        lax.all_gather(normed_two, "blk", axis=0, tiled=True),
        lax.all_gather(lowrank_three, "blk", axis=0, tiled=True),
    )
    gate_grid = jnp.einsum(
        "td,nkd->tkn", rows_group, group_gate, preferred_element_type=jnp.float32
    ) + jnp.einsum("tr,nkr->tkn", lowrank_group, group_expand, preferred_element_type=jnp.float32)
    hidden_grid = gated_units(gate_grid).astype(jnp.bfloat16)
    down_group = jnp.concatenate([group_down, group_adapt], axis=1)
    mixed = lax.psum_scatter(
        product(hidden_grid, down_group).astype(jnp.bfloat16),
        "blk",
        scatter_dimension=0,
        tiled=True,
    ).astype(jnp.float32)
    summed = mixed[:, :D]
    lowsum = mixed[:, D:]
    lowrank_four = lowsum.astype(jnp.bfloat16)
    branch_ffn = summed + product(lowrank_four, down_from)
    final = middle + branch_ffn
    result = final.astype(jnp.bfloat16)
    root_means = jnp.stack([root_mean(final), root_mean(branch_attn), root_mean(branch_ffn)])
    grad_final = cotangent.astype(jnp.float32)
    expand_down = product_rows(lowrank_four, cotangent)
    grad_four = product_back(cotangent, down_from).astype(jnp.bfloat16)
    back_group, back_low_group = (
        lax.all_gather(cotangent, "blk", axis=0, tiled=True),
        lax.all_gather(grad_four, "blk", axis=0, tiled=True),
    )
    grad_hidden_grid = product_back(back_group, group_down) + product_back(
        back_low_group, group_adapt
    )
    grad_gate_grid = gated_back(gate_grid, grad_hidden_grid).astype(jnp.bfloat16)
    back_joined = jnp.concatenate([back_group, back_low_group], axis=1)
    parts = lax.psum_scatter(
        jnp.concatenate(
            [
                jnp.einsum(
                    "tkn,nkd->td", grad_gate_grid, group_gate, preferred_element_type=jnp.float32
                ),
                jnp.einsum(
                    "tkn,nkr->tr", grad_gate_grid, group_expand, preferred_element_type=jnp.float32
                ),
            ],
            axis=1,
        ).astype(jnp.bfloat16),
        "blk",
        scatter_dimension=0,
        tiled=True,
    ).astype(jnp.float32)
    grad_rows = parts[:, :D]
    grad_lowsum = parts[:, D:]
    down_part = product_rows(hidden_grid, back_joined)
    gate_part = jnp.einsum(
        "tkn,td->nkd", grad_gate_grid, rows_group, preferred_element_type=jnp.float32
    ).reshape(lax.axis_size(("seq", "head")) * units, 2 * D)
    expand_part = jnp.einsum(
        "tkn,tr->nkr", grad_gate_grid, lowrank_group, preferred_element_type=jnp.float32
    ).reshape(lax.axis_size(("seq", "head")) * units, 2 * R)
    weight_terms = lax.psum_scatter(
        jnp.concatenate([down_part, gate_part, expand_part], axis=1).astype(jnp.bfloat16),
        ("seq", "head"),
        scatter_dimension=0,
        tiled=True,
    ).astype(jnp.float32)
    downweight_grad = weight_terms[:, :D]
    downadapt_grad = weight_terms[:, D : D + R]
    gateweight_grad = weight_terms[:, D + R : 3 * D + R].reshape(units, 2, D)
    gateexpand_grad = weight_terms[:, 3 * D + R :].reshape(units, 2, R)
    grad_three = grad_lowsum.astype(jnp.bfloat16)
    adapt_ffn = product_rows(normed_two, grad_three)
    grad_normed_two = grad_rows + product_back(grad_three, ffn_into)
    gain_two_grad = jnp.sum(grad_normed_two * unit_two, axis=0)
    grad_middle = grad_final + norm_back(grad_normed_two, unit_two, inverse_two, gain_two)
    grad_branch = grad_middle.astype(jnp.bfloat16)
    expand_attn = product_rows(lowrank_two, grad_branch)
    weight_attn = product_rows(attn_rows, grad_branch)
    grad_two = product_back(grad_branch, proj_from).astype(jnp.bfloat16)
    adapt_attn = product_rows(attn_rows, grad_two)
    grad_attn = (
        (product_back(grad_branch, proj_full) + product_back(grad_two, proj_into))
        .astype(jnp.bfloat16)
        .reshape(tokens, H, DH)
    )
    delta = jnp.sum(grad_attn.astype(jnp.float32) * attended_tok, axis=-1)
    own_blocks = (own_start + tokens - 1) // KB + 1

    def back_block(step_index, carried):
        grad_query, key_terms = carried
        key_block, scores, visible = block_scores(step_index, queries, own_pos)
        shares = jnp.where(visible, jnp.exp(scores - log_tok[..., None]), 0.0)
        grad_shares = jnp.einsum(
            "the,ke->thk", grad_attn, key_block[:, DH:], preferred_element_type=jnp.float32
        )
        grad_scores = (shares * (grad_shares - delta[..., None])).astype(jnp.bfloat16)
        grad_query = grad_query + jnp.einsum(
            "thk,ke->the", grad_scores, key_block[:, :DH], preferred_element_type=jnp.float32
        )
        grad_keys = (
            jnp.einsum("thk,the->ke", grad_scores, queries, preferred_element_type=jnp.float32)
            * score_scale
        )
        grad_values = jnp.einsum(
            "thk,the->ke",
            shares.astype(jnp.bfloat16),
            grad_attn,
            preferred_element_type=jnp.float32,
        )
        key_terms = lax.dynamic_update_slice_in_dim(
            key_terms, jnp.concatenate([grad_keys, grad_values], axis=1), step_index * KB, 0
        )
        return (grad_query, key_terms)

    start_grads = (
        jnp.zeros((tokens, H, DH), jnp.float32),
        jnp.zeros((seq_length, 2 * DH), jnp.float32),
    )
    grad_query, key_terms = lax.fori_loop(0, own_blocks, back_block, start_grads)
    key_grads = lax.psum_scatter(key_terms, ("head", "blk"), scatter_dimension=0, tiled=True)
    grad_query = rotate(grad_query * score_scale, cosine[:, None, :], -sine_part[:, None, :])
    grad_key = rotate(key_grads[:, :DH], cosine, -sine_part)
    grad_joined = jnp.concatenate(
        [grad_query.reshape(tokens, H * DH), grad_key, key_grads[:, DH:]], axis=1
    ).astype(jnp.bfloat16)
    expand_qkv = product_rows(lowrank_one, grad_joined)
    weight_qkv = product_rows(normed_one, grad_joined)
    grad_one = product_back(grad_joined, qkv_from).astype(jnp.bfloat16)
    adapt_qkv = product_rows(normed_one, grad_one)
    grad_normed_one = product_back(grad_joined, qkv_full) + product_back(grad_one, qkv_into)
    gain_one_grad = jnp.sum(grad_normed_one * unit_one, axis=0)
    stream_grad = grad_middle + norm_back(grad_normed_one, unit_one, inverse_one, gain_one)
    (
        attngain_grad,
        qkvweight_grad,
        qkvadapt_grad,
        qkvexpand_grad,
        outweight_grad,
        outadapt_grad,
        outexpand_grad,
        ffngain_grad,
        gateadapt_grad,
        downexpand_grad,
    ) = (
        lax.psum_scatter(gain_one_grad, ("seq", "head", "blk"), scatter_dimension=0, tiled=True),
        lax.psum_scatter(weight_qkv, ("seq", "head", "blk"), scatter_dimension=0, tiled=True),
        lax.psum_scatter(adapt_qkv, ("seq", "head", "blk"), scatter_dimension=0, tiled=True),
        lax.psum_scatter(expand_qkv, ("seq", "head", "blk"), scatter_dimension=0, tiled=True),
        lax.psum_scatter(weight_attn, ("seq", "head", "blk"), scatter_dimension=0, tiled=True),
        lax.psum_scatter(adapt_attn, ("seq", "head", "blk"), scatter_dimension=0, tiled=True),
        lax.psum_scatter(expand_attn, ("seq", "head", "blk"), scatter_dimension=0, tiled=True),
        lax.psum_scatter(gain_two_grad, ("seq", "head", "blk"), scatter_dimension=0, tiled=True),
        lax.psum_scatter(adapt_ffn, ("seq", "head", "blk"), scatter_dimension=0, tiled=True),
        lax.psum_scatter(expand_down, ("seq", "head", "blk"), scatter_dimension=0, tiled=True),
    )
    return (
        result,
        stream_grad,
        attngain_grad,
        qkvweight_grad,
        qkvadapt_grad,
        qkvexpand_grad,
        outweight_grad,
        outadapt_grad,
        outexpand_grad,
        ffngain_grad,
        gateweight_grad,
        gateadapt_grad,
        gateexpand_grad,
        downweight_grad,
        downadapt_grad,
        downexpand_grad,
        root_means,
    )


def solution(mesh):
    in_specs = (
        P(("seq", "head", "blk"), None),
        P(("seq", "head", "blk")),
        P(("seq", "head", "blk"), None),
        P(("seq", "head", "blk"), None),
        P(("seq", "head", "blk"), None),
        P(("seq", "head", "blk"), None),
        P(("seq", "head", "blk"), None),
        P(("seq", "head", "blk"), None),
        P(("seq", "head", "blk")),
        P(("seq", "head", "blk"), None, None),
        P(("seq", "head", "blk"), None),
        P(("seq", "head", "blk"), None, None),
        P(("seq", "head", "blk"), None),
        P(("seq", "head", "blk"), None),
        P(("seq", "head", "blk"), None),
        P(("seq", "head", "blk"), None),
    )
    out_specs = (
        P(("seq", "head", "blk"), None),
        P(("seq", "head", "blk"), None),
        P(("seq", "head", "blk")),
        P(("seq", "head", "blk"), None),
        P(("seq", "head", "blk"), None),
        P(("seq", "head", "blk"), None),
        P(("seq", "head", "blk"), None),
        P(("seq", "head", "blk"), None),
        P(("seq", "head", "blk"), None),
        P(("seq", "head", "blk")),
        P(("seq", "head", "blk"), None, None),
        P(("seq", "head", "blk"), None),
        P(("seq", "head", "blk"), None, None),
        P(("seq", "head", "blk"), None),
        P(("seq", "head", "blk"), None),
        P(("seq", "head", "blk"), None),
        P(None, ("seq", "head", "blk")),
    )
    return jax.shard_map(body, mesh=mesh, in_specs=in_specs, out_specs=out_specs, check_vma=False)
```

profile of v0, /device:TPU:0, one launch (start us, length us, event | category | flops | bytes accessed | tf_op | source)
XLA Modules:
  0.0 3274.4 jit_solution(12207656405017130853)
XLA Ops:
  11.2 42.2 %all-reduce.7 = (bf16[2048]{0:T(1024)(128)(2,1)S(1)}, bf16[2048]{0:T(1024)(128)(2,1)S(1)}) all-reduce(bf16[2048]{0:T(1024)(128)(2,1)S(1)} %dynamic-update-slice, bf16[2048]{0:T(1024)(128)(2,1)S(1)} %dynamic-update-slice.1), channel_id=1, replica_groups=mesh['seq'=2,'head'=2,'blk'=8] {'seq','head','blk'}, use_global_device_ids=true, to_apply=%add.2 | all-reduce | flops 4096 | bytes 16384
  54.7 12.8 all-gather.18.cloned.1.call-done
  69.3 87.0 %all-gather.16.cloned.1.call-done = bf16[2048,2560]{1,0:T(8,128)(2,1)} async-done(((bf16[64,2560]{1,0:T(8,128)(2,1)}), bf16[2048,2560]{1,0:T(8,128)(2,1)}) %all-gather.16.cloned.1.call-update) | async-done | bytes 10485776 | tf_op jit(solution)/shard_map/all_gather | solution.py:120
  162.0 50.0 %all-gather.20.cloned.1.call-done = bf16[256,2560]{1,0:T(8,128)(2,1)} async-done(((bf16[8,2560]{1,0:T(8,128)(2,1)}), bf16[256,2560]{1,0:T(8,128)(2,1)}) %all-gather.20.cloned.1.call-update) | async-done | bytes 1310736 | tf_op jit(solution)/shard_map/all_gather | solution.py:122
  232.4 8.7 all-to-all-done
  241.3 34.0 %all-gather.22.cloned.1.call-done = bf16[2048,512]{1,0:T(8,128)(2,1)} async-done(((bf16[128,512]{1,0:T(8,128)(2,1)}), bf16[2048,512]{1,0:T(8,128)(2,1)}) %all-gather.22.cloned.1.call-update) | async-done | bytes 2097168 | tf_op jit(solution)/shard_map/all_gather | solution.py:143
  275.2 6.7 while.37
  282.6 7.5 while.38
  295.7 13.6 all-to-all-done.1
  310.8 19.7 all-gather.26.cloned.1.call-done
  332.1 77.7 %all-gather.24.cloned.1.call-done = bf16[2048,2048]{1,0:T(8,128)(2,1)} async-done(((bf16[64,2048]{1,0:T(8,128)(2,1)}), bf16[2048,2048]{1,0:T(8,128)(2,1)}) %all-gather.24.cloned.1.call-update) | async-done | bytes 8388624 | tf_op jit(solution)/shard_map/all_gather | solution.py:123
  414.4 50.7 %all-gather.28.cloned.1.call-done = bf16[256,2048]{1,0:T(8,128)(2,1)} async-done(((bf16[8,2048]{1,0:T(8,128)(2,1)}), bf16[256,2048]{1,0:T(8,128)(2,1)}) %all-gather.28.cloned.1.call-update) | async-done | bytes 1048592 | tf_op jit(solution)/shard_map/all_gather | solution.py:125
  469.2 51.7 %all-gather.42.cloned.1.call-done = bf16[256,2048]{1,0:T(8,128)(2,1)} async-done(((bf16[8,2048]{1,0:T(8,128)(2,1)}), bf16[256,2048]{1,0:T(8,128)(2,1)}) %all-gather.42.cloned.1.call-update) | async-done | bytes 1048592 | tf_op jit(solution)/shard_map/all_gather | solution.py:128
  522.6 33.0 %all_gather.75 = bf16[1024,256]{1,0:T(8,128)(2,1)S(1)} all-gather(bf16[128,256]{1,0:T(8,128)(2,1)S(1)} %convolution_convert_fusion.5), channel_id=1, replica_groups=mesh['seq'=2,'head'=2,'blk'=8] {'blk'}, dimensions={0}, use_global_device_ids=true | all-gather | bytes 589824 | tf_op jit(solution)/shard_map/all_gather | solution.py:233
  555.6 43.0 %all-gather.44.cloned.1.call-done = bf16[1024,2048]{1,0:T(8,128)(2,1)} async-done(((bf16[128,2048]{1,0:T(8,128)(2,1)}), bf16[1024,2048]{1,0:T(8,128)(2,1)}) %all-gather.44.cloned.1.call-update) | async-done | bytes 4194320 | tf_op jit(solution)/shard_map/all_gather | solution.py:232
  598.6 58.0 %all-gather.38.cloned.1.call-done = bf16[2048,2048]{1,0:T(8,128)(2,1)} async-done(((bf16[512,2048]{1,0:T(8,128)(2,1)}), bf16[2048,2048]{1,0:T(8,128)(2,1)}) %all-gather.38.cloned.1.call-update) | async-done | bytes 8388624 | tf_op jit(solution)/shard_map/all_gather | solution.py:203
  656.6 14.6 fusion.113
  671.2 42.1 %all-gather.34.cloned.1.call-done = bf16[2048,256]{1,0:T(8,128)(2,1)} async-done(((bf16[64,256]{1,0:T(8,128)(2,1)}), bf16[2048,256]{1,0:T(8,128)(2,1)}) %all-gather.34.cloned.1.call-update) | async-done | bytes 1048592 | tf_op jit(solution)/shard_map/all_gather | solution.py:127
  714.9 31.3 all_gather.69
  746.3 13.1 fusion.77
  759.3 85.7 %all-gather.32.cloned.1.call-done = bf16[2048,2,2048]{2,0,1:T(8,128)(2,1)} async-done(((bf16[512,2,2048]{2,0,1:T(8,128)(2,1)}), bf16[2048,2,2048]{2,0,1:T(8,128)(2,1)}) %all-gather.32.cloned.1.call-update) | async-done | bytes 16777232 | tf_op jit(solution)/shard_map/all_gather | solution.py:201
  845.0 76.0 %all-gather.30.cloned.1.call-done = bf16[1024,2048]{1,0:T(8,128)(2,1)} async-done(((bf16[128,2048]{1,0:T(8,128)(2,1)}), bf16[1024,2048]{1,0:T(8,128)(2,1)}) %all-gather.30.cloned.1.call-update) | async-done | bytes 4194320 | tf_op jit(solution)/shard_map/all_gather | solution.py:207
  921.0 25.5 add_bitcast_fusion
  946.5 20.0 multiply_bitcast_fusion
  973.2 23.2 bitcast_convert_fusion
  1002.5 16.0 fusion.54
  1021.9 73.2 %reduce-scatter.15.cloned.1.call-done = bf16[128,2304]{1,0:T(8,128)(2,1)} async-done(((bf16[1024,2304]{1,0:T(8,128)(2,1)}), bf16[128,2304]{1,0:T(8,128)(2,1)}) %reduce-scatter.15.cloned.1.call-update) | async-done | bytes 589840 | tf_op jit(solution)/shard_map/reduce_scatter | solution.py:240
  1096.9 96.8 %reduce-scatter.13.cloned.1.call-done = bf16[128,2304]{1,0:T(8,128)(2,1)} async-done(((bf16[1024,2304]{1,0:T(8,128)(2,1)}), bf16[128,2304]{1,0:T(8,128)(2,1)}) %reduce-scatter.13.cloned.1.call-update) | async-done | bytes 589840 | tf_op jit(solution)/shard_map/reduce_scatter | solution.py:215
  1211.3 10.9 while.39
  1222.3 24.7 convolution_convert_fusion.1
  1246.9 20.9 copy.141
  1276.2 15.7 convolution_convert_fusion
  1291.9 31.8 pad_maximum_fusion.1
  1337.1 14.1 reduce-scatter.17.cloned.1.call-done
  1360.1 12.0 fusion.115
  1372.2 14.6 fusion.105
  1388.1 9.1 fusion.111
  1398.8 54.1 %all-reduce.6 = (f32[2048]{0:T(1024)S(1)}, f32[2048]{0:T(1024)S(1)}) all-reduce(f32[2048]{0:T(1024)S(1)} %get-tuple-element.269, f32[2048]{0:T(1024)S(1)} %copy-done.41), channel_id=5, replica_groups=mesh['seq'=2,'head'=2,'blk'=8] {'seq','head','blk'}, use_global_device_ids=true, to_apply=%region_17.18.clone | all-reduce | flops 4096 | bytes 32768
  1456.9 101.5 %reduce-scatter.31.cloned.1.call-done = bf16[512,6912]{1,0:T(8,128)(2,1)} async-done(((bf16[2048,6912]{1,0:T(8,128)(2,1)}), bf16[512,6912]{1,0:T(8,128)(2,1)}) %reduce-scatter.31.cloned.1.call-update) | async-done | bytes 7077904 | tf_op jit(solution)/shard_map/reduce_scatter | solution.py:265
  1565.1 11.7 reshape.322
  1585.5 118.1 %reduce-scatter.27.cloned.1.call-done = f32[64,256]{1,0:T(8,128)} async-done(((f32[2048,256]{1,0:T(8,128)}), f32[64,256]{1,0:T(8,128)}) %reduce-scatter.27.cloned.1.call-update) | async-done | bytes 65552 | tf_op jit(solution)/shard_map/reduce_scatter | solution.py:354
  1703.6 150.0 %reduce-scatter.29.cloned.1.call-done = f32[8,2048]{1,0:T(8,128)} async-done(((f32[256,2048]{1,0:T(8,128)}), f32[8,2048]{1,0:T(8,128)}) %reduce-scatter.29.cloned.1.call-update) | async-done | bytes 65552 | tf_op jit(solution)/shard_map/reduce_scatter | solution.py:355
  1853.5 149.8 %reduce-scatter.33.cloned.1.call-done = f32[64,256]{1,0:T(8,128)} async-done(((f32[2048,256]{1,0:T(8,128)}), f32[64,256]{1,0:T(8,128)}) %reduce-scatter.33.cloned.1.call-update) | async-done | bytes 65552 | tf_op jit(solution)/shard_map/reduce_scatter | solution.py:357
  2003.4 150.1 %reduce-scatter.35.cloned.1.call-done = f32[8,2048]{1,0:T(8,128)} async-done(((f32[256,2048]{1,0:T(8,128)}), f32[8,2048]{1,0:T(8,128)}) %reduce-scatter.35.cloned.1.call-update) | async-done | bytes 65552 | tf_op jit(solution)/shard_map/reduce_scatter | solution.py:358
  2153.5 150.0 %reduce-scatter.21.cloned.1.call-done = f32[64,256]{1,0:T(8,128)} async-done(((f32[2048,256]{1,0:T(8,128)}), f32[64,256]{1,0:T(8,128)}) %reduce-scatter.21.cloned.1.call-update) | async-done | bytes 65552 | tf_op jit(solution)/shard_map/reduce_scatter | solution.py:351
  2303.4 149.3 %reduce-scatter.23.cloned.1.call-done = f32[8,2560]{1,0:T(8,128)} async-done(((f32[256,2560]{1,0:T(8,128)}), f32[8,2560]{1,0:T(8,128)}) %reduce-scatter.23.cloned.1.call-update) | async-done | bytes 81936 | tf_op jit(solution)/shard_map/reduce_scatter | solution.py:352
  2452.7 367.9 %reduce-scatter.25.cloned.1.call-done = f32[64,2048]{1,0:T(8,128)} async-done(((f32[2048,2048]{1,0:T(8,128)}), f32[64,2048]{1,0:T(8,128)}) %reduce-scatter.25.cloned.1.call-update) | async-done | bytes 524304 | tf_op jit(solution)/shard_map/reduce_scatter | solution.py:353
  2820.6 446.5 %reduce-scatter.19.cloned.1.call-done = f32[64,2560]{1,0:T(8,128)} async-done(((f32[2048,2560]{1,0:T(8,128)}), f32[64,2560]{1,0:T(8,128)}) %reduce-scatter.19.cloned.1.call-update) | async-done | bytes 655376 | tf_op jit(solution)/shard_map/reduce_scatter | solution.py:350
  (302 shorter events, 166.7 us)
Async XLA Ops:
  7.2 60.3 %all-gather.18.cloned.1.call-start = ((), (), s32[]{:S(2)}) async-start(), calls=%async_computation.16 | async-start | bytes 1081344 | tf_op jit(solution)/shard_map/all_gather | solution.py:121
  7.9 148.3 %all-gather.16.cloned.1.call-start = ((), (), s32[]{:S(2)}) async-start(), calls=%async_computation.15 | async-start | bytes 10813440 | tf_op jit(solution)/shard_map/all_gather | solution.py:120
  8.7 203.4 %all-gather.20.cloned.1.call-start = ((), (), s32[]{:S(2)}) async-start(), calls=%async_computation.17 | async-start | bytes 1351680 | tf_op jit(solution)/shard_map/all_gather | solution.py:122
  9.4 265.8 %all-gather.22.cloned.1.call-start = ((), (), s32[]{:S(2)}) async-start(), calls=%async_computation.18 | async-start | bytes 2228224 | tf_op jit(solution)/shard_map/all_gather | solution.py:143
  53.3 108.6 %copy-start.29 = (f32[2048]{0:T(1024)}, f32[2048]{0:T(1024)S(1)}, u32[]{:S(2)}) copy-start(f32[2048]{0:T(1024)S(1)} %convert_element_type.97) | copy-start | bytes 24580
  53.4 160.4 %copy-start.44 = (f32[128]{0:T(128)}, f32[128]{0:T(128)S(1)}, u32[]{:S(2)}) copy-start(f32[128]{0:T(128)S(1)} %multiply_exponential_fusion) | copy-start | bytes 1540
  53.4 160.3 %copy-start.46 = (f32[128]{0:T(128)}, f32[128]{0:T(128)S(1)}, u32[]{:S(2)}) copy-start(f32[128]{0:T(128)S(1)} %add_convert_fusion.4) | copy-start | bytes 1540
  54.7 107.3 %copy-start.39 = (f32[128]{0:T(128)}, f32[128]{0:T(128)S(1)}, u32[]{:S(2)}) copy-start(f32[128]{0:T(128)S(1)} %add_rsqrt_fusion.1) | copy-start | bytes 1540
  69.3 142.8 %copy-start.34 = (bf16[128,256]{1,0:T(8,128)(2,1)}, bf16[128,256]{1,0:T(8,128)(2,1)S(1)}, u32[]{:S(2)}) copy-start(bf16[128,256]{1,0:T(8,128)(2,1)S(1)} %convolution_convert_fusion.8) | copy-start | bytes 196612
  215.4 115.2 %all-gather.26.cloned.1.call-start = ((), (), s32[]{:S(2)}) async-start(), calls=%async_computation.20 | async-start | bytes 1081344 | tf_op jit(solution)/shard_map/all_gather | solution.py:124
  216.0 193.8 %all-gather.24.cloned.1.call-start = ((), (), s32[]{:S(2)}) async-start(), calls=%async_computation.19 | async-start | bytes 8650752 | tf_op jit(solution)/shard_map/all_gather | solution.py:123
  216.6 248.6 %all-gather.28.cloned.1.call-start = ((), (), s32[]{:S(2)}) async-start(), calls=%async_computation.21 | async-start | bytes 1081344 | tf_op jit(solution)/shard_map/all_gather | solution.py:125
  217.3 303.6 %all-gather.42.cloned.1.call-start = ((), (), s32[]{:S(2)}) async-start(), calls=%async_computation.29 | async-start | bytes 1081344 | tf_op jit(solution)/shard_map/all_gather | solution.py:128
  218.0 380.5 %all-gather.44.cloned.1.call-start = ((), (), s32[]{:S(2)}) async-start(), calls=%async_computation.30 | async-start | bytes 4718592 | tf_op jit(solution)/shard_map/all_gather | solution.py:232
  218.8 437.8 %all-gather.38.cloned.1.call-start = ((), (), s32[]{:S(2)}) async-start(), calls=%async_computation.26 | async-start | bytes 10485760 | tf_op jit(solution)/shard_map/all_gather | solution.py:203
  219.4 494.0 %all-gather.34.cloned.1.call-start = ((), (), s32[]{:S(2)}) async-start(), calls=%async_computation.24 | async-start | bytes 1081344 | tf_op jit(solution)/shard_map/all_gather | solution.py:127
  220.1 526.1 %all-gather.36.cloned.1.call-start = ((), (), s32[]{:S(2)}) async-start(), calls=%async_computation.25 | async-start | bytes 2621440 | tf_op jit(solution)/shard_map/all_gather | solution.py:202
  221.1 624.0 %all-gather.32.cloned.1.call-start = ((), (), s32[]{:S(2)}) async-start(), calls=%async_computation.23 | async-start | bytes 20971520 | tf_op jit(solution)/shard_map/all_gather | solution.py:201
  228.9 12.2 all-to-all-start
  291.8 17.5 all-to-all-start.1
  295.4 625.6 %all-gather.30.cloned.1.call-start = ((), (), s32[]{:S(2)}) async-start(), calls=%async_computation.22 | async-start | bytes 4718592 | tf_op jit(solution)/shard_map/all_gather | solution.py:207
  295.7 901.5 %copy-start.37 = (f32[2048]{0:T(1024)}, f32[2048]{0:T(1024)S(1)}, u32[]{:S(2)}) copy-start(f32[2048]{0:T(1024)S(1)} %convert_element_type.104) | copy-start | bytes 24580
  310.8 103.6 %copy-start.4 = (bf16[128,2048]{1,0:T(8,128)(2,1)}, bf16[128,2048]{1,0:T(8,128)(2,1)S(1)}, u32[]{:S(2)}) copy-start(bf16[128,2048]{1,0:T(8,128)(2,1)S(1)} %convert_element_type.102) | copy-start | bytes 1572868
  332.1 133.0 %copy-start.25 = (bf16[128,256]{1,0:T(8,128)(2,1)}, bf16[128,256]{1,0:T(8,128)(2,1)S(1)}, u32[]{:S(2)}) copy-start(bf16[128,256]{1,0:T(8,128)(2,1)S(1)} %convolution_convert_fusion.7) | copy-start | bytes 196612
  332.1 133.0 %copy-start.2 = (bf16[128,2048]{1,0:T(8,128)(2,1)S(1)}, bf16[128,2048]{1,0:T(8,128)(2,1)}, u32[]{:S(2)}) copy-start(bf16[128,2048]{1,0:T(8,128)(2,1)} %param.22) | copy-start | bytes 1572868
  414.4 106.5 %copy-start.8 = (bf16[128,2048]{1,0:T(8,128)(2,1)S(1)}, bf16[128,2048]{1,0:T(8,128)(2,1)}, u32[]{:S(2)}) copy-start(bf16[128,2048]{1,0:T(8,128)(2,1)} %param.37) | copy-start | bytes 1572868
  467.4 729.8 %copy-start.6 = (f32[128,2048]{1,0:T(8,128)}, f32[128,2048]{1,0:T(8,128)S(1)}, u32[]{:S(2)}) copy-start(f32[128,2048]{1,0:T(8,128)S(1)} %get-tuple-element.328) | copy-start | bytes 3145732
  467.4 729.8 %copy-start.42 = (f32[128]{0:T(128)}, f32[128]{0:T(128)S(1)}, u32[]{:S(2)}) copy-start(f32[128]{0:T(128)S(1)} %add_rsqrt_fusion) | copy-start | bytes 1540
  468.6 478.0 %all-gather.40.cloned.1.call-start = ((), (), s32[]{:S(2)}) async-start(), calls=%async_computation.27 | async-start | bytes 1310720 | tf_op jit(solution)/shard_map/all_gather | solution.py:204
  469.2 625.9 %reduce-scatter.15.cloned.1.call-start = ((), (), s32[]{:S(2)}) async-start(), calls=%async_computation.31 | async-start | bytes 5308416 | tf_op jit(solution)/shard_map/reduce_scatter | solution.py:240
  555.6 391.0 %copy-start.31 = (bf16[1024,256]{1,0:T(8,128)(2,1)}, bf16[1024,256]{1,0:T(8,128)(2,1)S(1)}, u32[]{:S(2)}) copy-start(bf16[1024,256]{1,0:T(8,128)(2,1)S(1)} %all_gather.75) | copy-start | bytes 1572868
  555.6 157.8 %copy-start.17 = (bf16[128,2048]{1,0:T(8,128)(2,1)S(1)}, bf16[128,2048]{1,0:T(8,128)(2,1)}, u32[]{:S(2)}) copy-start(bf16[128,2048]{1,0:T(8,128)(2,1)} %multiply_convert_fusion.1) | copy-start | bytes 1572868
  1001.3 192.4 %reduce-scatter.13.cloned.1.call-start = ((), (), s32[]{:S(2)}) async-start(), calls=%async_computation.28 | async-start | bytes 5308416 | tf_op jit(solution)/shard_map/reduce_scatter | solution.py:215
  1018.6 189.1 %all-to-all-start.2 = ((f32[2,128,4]{1,2,0:T(4,128)}), f32[2,128,4]{1,2,0:T(4,128)S(1)}, u32[]{:S(2)}, u32[]{:S(2)}) async-start(f32[2,128,4]{1,2,0:T(4,128)} %bitcast.14), calls=%async_computation.4 | async-start | bytes 8192 | tf_op jit(solution)/shard_map/all_to_all | solution.py:191
  1021.8 329.4 %reduce-scatter.17.cloned.1.call-start = ((), (), s32[]{:S(2)}) async-start(), calls=%async_computation.32 | async-start | bytes 4456448 | tf_op jit(solution)/shard_map/reduce_scatter | solution.py:324
  1096.9 107.3 %copy-start.12 = (f32[128,2048]{1,0:T(8,128)}, f32[128,2048]{1,0:T(8,128)S(1)}, u32[]{:S(2)}) copy-start(f32[128,2048]{1,0:T(8,128)S(1)} %convolution_add_fusion.6) | copy-start | bytes 3145732
  1222.2 336.2 %reduce-scatter.31.cloned.1.call-start = ((), (), s32[]{:S(2)}) async-start(), calls=%async_computation.39 | async-start | bytes 35389440 | tf_op jit(solution)/shard_map/reduce_scatter | solution.py:265
  1323.8 379.8 %reduce-scatter.27.cloned.1.call-start = ((), (), s32[]{:S(2)}) async-start(), calls=%async_computation.37 | async-start | bytes 2162688 | tf_op jit(solution)/shard_map/reduce_scatter | solution.py:354
  1326.6 526.9 %reduce-scatter.29.cloned.1.call-start = ((), (), s32[]{:S(2)}) async-start(), calls=%async_computation.38 | async-start | bytes 2162688 | tf_op jit(solution)/shard_map/reduce_scatter | solution.py:355
  1328.5 674.9 %reduce-scatter.33.cloned.1.call-start = ((), (), s32[]{:S(2)}) async-start(), calls=%async_computation.40 | async-start | bytes 2162688 | tf_op jit(solution)/shard_map/reduce_scatter | solution.py:357
  1331.3 822.1 %reduce-scatter.35.cloned.1.call-start = ((), (), s32[]{:S(2)}) async-start(), calls=%async_computation.41 | async-start | bytes 2162688 | tf_op jit(solution)/shard_map/reduce_scatter | solution.py:358
  1334.1 969.4 %reduce-scatter.21.cloned.1.call-start = ((), (), s32[]{:S(2)}) async-start(), calls=%async_computation.34 | async-start | bytes 2162688 | tf_op jit(solution)/shard_map/reduce_scatter | solution.py:351
  1357.7 1095.0 %reduce-scatter.23.cloned.1.call-start = ((), (), s32[]{:S(2)}) async-start(), calls=%async_computation.35 | async-start | bytes 2703360 | tf_op jit(solution)/shard_map/reduce_scatter | solution.py:352
  1359.8 1460.7 %reduce-scatter.25.cloned.1.call-start = ((), (), s32[]{:S(2)}) async-start(), calls=%async_computation.36 | async-start | bytes 17301504 | tf_op jit(solution)/shard_map/reduce_scatter | solution.py:353
  1372.1 1895.0 %reduce-scatter.19.cloned.1.call-start = ((), (), s32[]{:S(2)}) async-start(), calls=%async_computation.33 | async-start | bytes 21626880 | tf_op jit(solution)/shard_map/reduce_scatter | solution.py:350
  1388.1 65.9 %copy-start.38 = (f32[2048]{0:T(1024)S(1)}, f32[2048]{0:T(1024)}, u32[]{:S(2)}) copy-start(f32[2048]{0:T(1024)} %copy-done.37) | copy-start | bytes 24580
  1388.1 65.9 %copy-start.43 = (f32[128]{0:T(128)S(1)}, f32[128]{0:T(128)}, u32[]{:S(2)}) copy-start(f32[128]{0:T(128)} %copy-done.42) | copy-start | bytes 1540
  1388.1 65.9 %copy-start.49 = (f32[128]{0:T(128)S(1)}, f32[128]{0:T(128)}, u32[]{:S(2)}) copy-start(f32[128]{0:T(128)} %copy-done.48) | copy-start | bytes 1540
  (36 other events, 499.3 us)
Sparse Core Ops, SparseCore 0:
  11.0 56.4 all-gather.17
  70.4 85.7 all-gather.15
  159.1 52.8 all-gather.19
  215.5 59.6 all-gather.21
  278.1 52.4 all-gather.25
  333.4 76.3 all-gather.23
  412.8 52.3 all-gather.27
  468.1 52.7 all-gather.41
  523.0 75.5 all-gather.43
  600.0 56.5 all-gather.37
  659.6 53.7 all-gather.33
  715.3 21.5 all-gather.35
  739.1 105.9 all-gather.31
  847.6 73.3 all-gather.29
  922.4 14.9 all-gather.39
  1001.5 93.5 reduce-scatter.14
  1098.6 95.1 reduce-scatter.12
  1222.3 128.8 reduce-scatter.16
  1353.8 204.5 reduce-scatter.30
  1561.2 142.3 reduce-scatter.26
  1706.4 147.0 reduce-scatter.28
  1856.5 146.8 reduce-scatter.32
  2006.2 147.2 reduce-scatter.34
  2156.3 147.1 reduce-scatter.20
  2306.3 146.3 reduce-scatter.22
  2455.4 365.0 reduce-scatter.24
  2823.3 443.7 reduce-scatter.18
where the time goes:
time: 3290 us; the launch traced here: 3270 us
  waiting for transfers between devices  2690 us (82%)
  matrix products  267 us (8%)
  blocking collectives  161 us (5%)
  local copies, waits for them, and re-layouts  77.1 us (2%)
  other arithmetic  56.4 us (2%)
    reduce_scatter x1, waiting for transfers between devices, body(): lax.psum_scatter(weight_qkv, ('seq', 'head', 'blk'), scatter_dimension=0,...  447 us
    reduce_scatter x1, waiting for transfers between devices, body(): lax.psum_scatter(weight_attn, ('seq', 'head', 'blk'), scatter_dimension=0...  368 us
    reduce_scatter x1, waiting for transfers between devices, body(): lax.psum_scatter(expand_down, ('seq', 'head', 'blk'), scatter_dimension=0...  150 us
    reduce_scatter x1, waiting for transfers between devices, body(): lax.psum_scatter(expand_attn, ('seq', 'head', 'blk'), scatter_dimension=0...  150 us
    reduce_scatter x1, waiting for transfers between devices, body(): lax.psum_scatter(adapt_qkv, ('seq', 'head', 'blk'), scatter_dimension=0,...  150 us
    reduce_scatter x1, waiting for transfers between devices, body(): lax.psum_scatter(adapt_ffn, ('seq', 'head', 'blk'), scatter_dimension=0,...  150 us
    reduce_scatter x1, waiting for transfers between devices, body(): lax.psum_scatter(expand_qkv, ('seq', 'head', 'blk'), scatter_dimension=0,...  149 us
    reduce_scatter x1, waiting for transfers between devices, body(): lax.psum_scatter(adapt_attn, ('seq', 'head', 'blk'), scatter_dimension=0,...  118 us
  transfers between devices with their start and end apart: 30, of which 27 were waited for; matrix products, arithmetic and copies ran while one was open for 10% of the time, Pallas kernels for 0%

commit v1 on v0

v1 whole, which is shorter than its diff:
```python
import functools
import math

import jax
import jax.numpy as jnp
from jax import lax
from jax.sharding import PartitionSpec as P

D = 2048
H = 8
DH = 256
R = 256


EPSILON = 1e-06
NEGATIVE = -1e30


def product(former, latter):
    return jnp.dot(former, latter, preferred_element_type=jnp.float32)


def product_back(former, latter):
    return lax.dot_general(
        former, latter, (((1,), (1,)), ((), ())), preferred_element_type=jnp.float32
    )


def product_rows(former, latter):
    return lax.dot_general(
        former, latter, (((0,), (0,)), ((), ())), preferred_element_type=jnp.float32
    )


def rope_tables(positions, full_width):
    half_width = full_width // 2
    rates = jnp.exp(
        jnp.arange(half_width, dtype=jnp.float32) * (-2.0 * math.log(10000.0) / full_width)
    )
    angles = positions.astype(jnp.float32)[:, None] * rates[None, :]
    return (jnp.cos(angles), jnp.sin(angles))


def rotate(values, cosine, sine_part):
    half_width = values.shape[-1] // 2
    former = values[..., :half_width]
    latter = values[..., half_width:]
    return jnp.concatenate(
        [former * cosine - latter * sine_part, latter * cosine + former * sine_part], axis=-1
    )


def unit_rows(values):
    inverse = lax.rsqrt(jnp.mean(values * values, axis=-1, keepdims=True) + EPSILON)
    return (values * inverse, inverse)


def norm_back(grad_in, scaled_rows, inverse, gain_row):
    weighted = grad_in * gain_row
    return inverse * (
        weighted - scaled_rows * jnp.mean(weighted * scaled_rows, axis=-1, keepdims=True)
    )


def root_mean(values):
    return jnp.sqrt(jnp.mean(values * values, axis=-1))


def shift(values, axes, mask):
    size = lax.axis_size(axes)
    return lax.ppermute(values, axes, [(i, i ^ mask) for i in range(size)])


def place(own, other, axis_name, position):
    first = lax.axis_index(axis_name) == 0
    return jnp.stack(
        [jnp.where(first, own, other), jnp.where(first, other, own)], axis=position
    )


class Gather:
    def __init__(self, shard, order, ranking):
        self.value, self.order, self.ranking = shard, list(order), ranking
        self.tail, self.done = shard.shape[1:], []

    def start(self):
        return shift(self.value, self.order[0], 1)

    def finish(self, other):
        name = self.order.pop(0)
        position = sum(self.ranking.index(d) < self.ranking.index(name) for d in self.done)
        self.value = place(self.value, other, name, position)
        self.done.append(name)

    def result(self):
        return self.value.reshape((-1,) + self.tail)


class Scatter:
    def __init__(self, terms, order, ranking):
        self.left = [name for name in ranking if name in order]
        self.order = list(order)
        rows = terms.shape[0] // 2 ** len(order)
        self.value = terms.reshape((2,) * len(order) + (rows,) + terms.shape[1:])

    def start(self):
        name = self.order[0]
        position, mine = self.left.index(name), lax.axis_index(name)
        sent = lax.dynamic_index_in_dim(self.value, 1 - mine, position, keepdims=False)
        return shift(sent, name, 1)

    def finish(self, other):
        name = self.order.pop(0)
        position, mine = self.left.index(name), lax.axis_index(name)
        kept = lax.dynamic_index_in_dim(self.value, mine, position, keepdims=False)
        self.value = kept.astype(jnp.float32) + other.astype(jnp.float32)
        if self.order:
            self.value = self.value.astype(jnp.bfloat16)
        self.left.remove(name)

    def result(self):
        return self.value


class ScatterNear(Scatter):
    def start(self):
        position = self.left.index(self.order[0])
        sent = lax.index_in_dim(self.value, 1, position, keepdims=False)
        return shift(sent, self.order[0], 1)

    def finish(self, other):
        name = self.order.pop(0)
        kept = lax.index_in_dim(self.value, 0, self.left.index(name), keepdims=False)
        self.value = kept.astype(jnp.float32) + other.astype(jnp.float32)
        if self.order:
            self.value = self.value.astype(jnp.bfloat16)
        self.left.remove(name)


def advance(*jobs, beside=()):
    arrived, beside = lax.optimization_barrier(([job.start() for job in jobs], beside))
    for job, other in zip(jobs, arrived):
        job.finish(other)
    return arrived, beside


def tie(values, *others):
    return lax.optimization_barrier((values, others))[0]


def body(
    ranking,
    stream,
    attn_gain,
    qkv_weight,
    qkv_adapt,
    qkv_expand,
    out_weight,
    out_adapt,
    out_expand,
    ffn_gain,
    gateup_weight,
    gateup_adapt,
    gateup_expand,
    down_weight,
    down_adapt,
    down_expand,
    cotangent,
):
    bf16 = jnp.bfloat16
    f32 = jnp.float32
    tokens = stream.shape[0]
    highs, low = ranking[2:-1], ranking[-1]
    row_axes, block_axes, unit_axes = ranking[1:], ranking[2:], ranking[:2]
    upper, mid, core = highs[:-1], highs[-1:], ("seq",)
    orders = (
        ("head",) + upper + (low,) + mid,
        ("head",) + mid + (low,) + upper,
        upper + ("head",) + mid + (low,),
        mid + ("head",) + upper + (low,),
    )
    steps = len(orders[0])
    backs = tuple(order[::-1] for order in orders)
    group = lax.axis_size(row_axes)
    planes = lax.axis_size(highs)
    plane = lax.axis_index(highs)
    side = lax.axis_index(low)
    own_pos = lax.axis_index(row_axes) * tokens + jnp.arange(tokens, dtype=jnp.int32)
    score_scale = DH ** (-0.5)
    half = H * DH // 2
    rank_rows = qkv_expand.shape[0]
    gain_columns = attn_gain.shape[0] // rank_rows

    from_row = jnp.concatenate(
        [
            qkv_expand,
            out_expand,
            down_expand,
            attn_gain.reshape(rank_rows, gain_columns),
            ffn_gain.reshape(rank_rows, gain_columns),
            jnp.zeros((rank_rows, 128 - 2 * gain_columns), bf16),
        ],
        axis=1,
    )
    jobs = [
        Gather(shard, order + core, ranking)
        for shard, order in zip(
            (
                jnp.concatenate([qkv_weight[:, 2 * half :], qkv_adapt], axis=1),
                from_row,
                qkv_weight[:, :half],
                qkv_weight[:, half : 2 * half],
            ),
            orders,
        )
    ]
    def gather_units(block):
        return lax.all_gather(block, unit_axes, axis=0, tiled=True)

    down_all = gather_units(jnp.concatenate([down_weight, down_adapt], axis=1))
    arrived, _ = advance(*jobs)
    pair_weight, pair_expand = tie((gateup_weight, gateup_expand), arrived)
    pairs = [
        jnp.concatenate([pair_weight[:, k], pair_expand[:, k]], axis=1) for k in range(2)
    ]
    arrived, pairs = advance(*jobs, beside=pairs)
    for _ in range(steps - 3):
        arrived, _ = advance(*jobs)
    gate_all = gather_units(tie(pairs[0], arrived))
    arrived, down_all = advance(*jobs, beside=down_all)
    advance(*jobs)
    kv_into, from_all, query_one, query_two = (job.result() for job in jobs)
    kv_full, qkv_into = kv_into[:, : 2 * DH], kv_into[:, 2 * DH :]
    qkv_columns = 2 * half + 2 * DH
    qkv_from = from_all[:, :qkv_columns]
    proj_from = from_all[:, qkv_columns : qkv_columns + D]
    down_from = from_all[:, qkv_columns + D : qkv_columns + 2 * D]
    gains = from_all[:, qkv_columns + 2 * D :]
    gain_one = gains[:, :gain_columns].reshape(D).astype(f32)
    gain_two = gains[:, gain_columns : 2 * gain_columns].reshape(D).astype(f32)

    residual = stream.astype(f32)
    unit_one, inverse_one = unit_rows(residual)
    normed_one = (unit_one * gain_one).astype(bf16)
    lowrank_one = product(normed_one, qkv_into).astype(bf16)
    joined_kv = product(normed_one, kv_full) + product(lowrank_one, qkv_from[:, 2 * half :])
    cosine, sine_part = rope_tables(own_pos, DH)
    keys = rotate(joined_kv[:, :DH], cosine, sine_part).astype(bf16)
    values = joined_kv[:, DH:].astype(bf16)
    joined_q = jnp.concatenate(
        [product(normed_one, query_one), product(normed_one, query_two)], axis=1
    ) + product(lowrank_one, qkv_from[:, : 2 * half])
    queries = (
        rotate(jnp.stack(jnp.split(joined_q, H, axis=1)), cosine, sine_part)
        .astype(bf16)
        .reshape(H * tokens, DH)
    )

    jobs = [
        Gather(shard, order, ranking)
        for shard, order in zip(
            (
                keys,
                values,
                jnp.concatenate([out_weight[:, :half], out_adapt], axis=1),
                jnp.concatenate([out_weight[:, half:], gateup_adapt], axis=1),
            ),
            (orders[1], orders[3], orders[0] + core, orders[2] + core),
        )
    ]
    arrived, (queries, gate_all) = advance(*jobs, beside=(queries, gate_all))
    up_all = gather_units(tie(pairs[1], gate_all))
    for _ in range(steps - 2):
        arrived, _ = advance(*jobs)
    arrived, up_all = advance(*jobs, beside=up_all)
    keys_all, values_all = jobs[0].result(), jobs[1].result()
    advance(*jobs[2:])
    out_one, out_two = jobs[2].result(), jobs[3].result()
    proj_one, proj_into = out_one[:, :half], out_one[:, half:]
    proj_two, ffn_into = out_two[:, :half], out_two[:, half:]

    def gather_near(rows):
        return [rows] + [shift(rows, highs, mask) for mask in range(1, planes)]

    def to_relative(rows):
        return jnp.concatenate(
            [
                lax.dynamic_slice_in_dim(
                    rows, ((plane ^ mask) * 2 + (side ^ far)) * tokens, tokens, 0
                )
                for far in range(2)
                for mask in range(planes)
            ],
            axis=0,
        )

    def to_absolute(rows):
        return jnp.concatenate(
            [
                lax.dynamic_slice_in_dim(
                    rows, ((side ^ far) * planes + (plane ^ mask)) * tokens, tokens, 0
                )
                for mask in range(planes)
                for far in range(2)
            ],
            axis=0,
        )

    key_pos = jnp.arange(group * tokens, dtype=jnp.int32)
    pieces = max(1, group * tokens // 2048)
    piece_rows = H * tokens // pieces
    visible = jnp.tile(key_pos[None, :] <= own_pos[:, None], (H // pieces, 1))

    def shares_of(query_rows):
        scores = jnp.where(
            visible, product_back(query_rows, keys_all) * score_scale, NEGATIVE
        )
        row_top = jnp.max(scores, axis=-1, keepdims=True)
        raised = jnp.where(visible, jnp.exp(scores - row_top), 0.0)
        return raised / jnp.sum(raised, axis=-1, keepdims=True)

    query_parts = jnp.split(queries, pieces, axis=0)
    kept, attended_parts = [], []
    for query_rows in query_parts:
        shares = shares_of(query_rows)
        attended_parts.append(product(shares.astype(bf16), values_all))
        if pieces == 1:
            kept.append(shares)

    def to_rows(parts):
        return jnp.concatenate(jnp.split(parts, H, axis=0), axis=1)

    def to_heads(rows):
        return jnp.concatenate(jnp.split(rows, H, axis=1), axis=0)

    attn_rows = to_rows(jnp.concatenate(attended_parts, axis=0).astype(bf16))
    lowrank_two = product(attn_rows, proj_into).astype(bf16)
    branch_attn = jnp.concatenate(
        [product(attn_rows, proj_one), product(attn_rows, proj_two)], axis=1
    ) + product(lowrank_two, proj_from)
    middle = residual + branch_attn
    unit_two, inverse_two = unit_rows(middle)
    normed_two = (unit_two * gain_two).astype(bf16)

    near = gather_near(normed_two)
    rows_group = jnp.concatenate(near + [shift(piece, low, 1) for piece in near], axis=0)
    back_all = lax.all_gather(
        tie(cotangent, near[1:], up_all), block_axes, axis=0, tiled=True
    )
    low_group = product(rows_group, ffn_into).astype(bf16)
    rows_joined = jnp.concatenate([rows_group, low_group], axis=1)
    gate = product_back(rows_joined, gate_all)
    up = product_back(rows_joined, up_all)
    hidden = (jax.nn.gelu(gate, approximate=True) * up).astype(bf16)
    out_terms = to_absolute(product(hidden, down_all).astype(bf16))
    mixed = lax.psum_scatter(
        tie(out_terms, back_all), block_axes, scatter_dimension=0, tiled=True
    )
    back_rows = tie(to_relative(back_all), out_terms)
    back_low = product_back(back_rows, down_from).astype(bf16)
    back_joined = jnp.concatenate([back_rows, back_low], axis=1)
    grad_hidden = product_back(back_joined, down_all)
    _, pullback = jax.vjp(lambda a, b: jax.nn.gelu(a, approximate=True) * b, gate, up)
    grad_gate, grad_up = (term.astype(bf16) for term in pullback(grad_hidden))

    row_terms = (product(grad_gate, gate_all) + product(grad_up, up_all)).astype(bf16)
    middle_column = row_terms.shape[1] // 2
    jobs = [
        ScatterNear(row_terms[:, :middle_column], (low,) + mid + upper, (low,) + highs),
        ScatterNear(row_terms[:, middle_column:], mid + upper + (low,), (low,) + highs),
    ]
    def scatter_units(terms):
        return lax.psum_scatter(terms, unit_axes, scatter_dimension=0, tiled=True)

    hidden_late, gate_late = tie((hidden, grad_gate), row_terms)
    work = (
        product_rows(hidden_late, back_joined).astype(bf16),
        product_rows(gate_late, rows_joined).astype(bf16),
    )
    arrived, (down_terms, gate_terms) = advance(*jobs, beside=work)
    up_terms = product_rows(tie(grad_up, arrived), rows_joined).astype(bf16)
    _, (up_terms, mixed) = advance(*jobs, beside=(up_terms, mixed))
    down_sum = scatter_units(tie(down_terms, mixed))
    mixed = mixed.astype(f32)
    for _ in range(len(highs) - 1):
        advance(*jobs)
    parts = jnp.concatenate([job.result() for job in jobs], axis=1)

    lowrank_four = mixed[:, D:].astype(bf16)
    branch_ffn = mixed[:, :D] + product(lowrank_four, down_from)
    final = middle + branch_ffn
    result = final.astype(bf16)
    root_means = jnp.stack([root_mean(final), root_mean(branch_attn), root_mean(branch_ffn)])
    expand_down = product_rows(lowrank_four, cotangent)

    grad_three = parts[:, D:].astype(bf16)
    adapt_ffn = product_rows(normed_two, grad_three)
    grad_normed_two = parts[:, :D] + product_back(grad_three, ffn_into)
    gain_two_grad = jnp.sum(grad_normed_two * unit_two, axis=0)
    grad_middle = cotangent.astype(f32) + norm_back(
        grad_normed_two, unit_two, inverse_two, gain_two
    )
    grad_branch = grad_middle.astype(bf16)
    grad_two = product_back(grad_branch, proj_from).astype(bf16)
    def scatter_weights(terms, order):
        return Scatter(terms.astype(bf16), core + order, ranking)

    out_jobs = [
        scatter_weights(terms, order)
        for terms, order in zip(
            (
                product_rows(
                    attn_rows, jnp.concatenate([grad_branch[:, :half], grad_two], axis=1)
                ),
                product_rows(attn_rows, grad_branch[:, half:]),
                adapt_ffn,
            ),
            (backs[0], backs[2], backs[3]),
        )
    ]
    grad_attn = to_heads(
        (
            product_back(grad_branch[:, :half], proj_one)
            + product_back(grad_branch[:, half:], proj_two)
            + product_back(grad_two, proj_into)
        ).astype(bf16)
    )
    _, grad_attn = advance(*out_jobs, beside=grad_attn)

    grad_queries, grad_keys, grad_values = [], 0.0, 0.0
    for i, query_rows in enumerate(query_parts):
        grad_rows = grad_attn[i * piece_rows : (i + 1) * piece_rows]
        shares = kept[i] if kept else shares_of(tie(query_rows, grad_rows))
        delta = jnp.sum(grad_rows.astype(f32) * attended_parts[i], axis=-1, keepdims=True)
        grad_shares = product_back(grad_rows, values_all)
        grad_scores = (shares * (grad_shares - delta)).astype(bf16)
        grad_queries.append(product(grad_scores, keys_all) * score_scale)
        grad_keys = grad_keys + product_rows(grad_scores, query_rows) * score_scale
        grad_values = grad_values + product_rows(shares.astype(bf16), grad_rows)
    grad_query = jnp.concatenate(grad_queries, axis=0)
    turned = rotate(grad_query.reshape(H, tokens, DH), cosine, -sine_part).astype(bf16)
    joined_q_grad = to_rows(turned.reshape(H * tokens, DH))
    query_jobs = [
        scatter_weights(product_rows(normed_one, rows), order)
        for rows, order in zip(
            (joined_q_grad[:, :half], joined_q_grad[:, half:]), (backs[0], backs[2])
        )
    ]
    _, (grad_keys, grad_values) = advance(
        *out_jobs, beside=(grad_keys.astype(bf16), grad_values.astype(bf16))
    )
    kv_jobs = [
        Scatter(grad_keys, ("head", low) + upper + mid, row_axes),
        Scatter(grad_values, mid + (low,) + upper + ("head",), row_axes),
    ]
    _, down_sum = advance(*kv_jobs, *out_jobs, beside=down_sum)
    gate_sum = scatter_units(tie(gate_terms, down_sum))
    for _ in range(steps - 2):
        advance(*kv_jobs, *out_jobs)
    advance(*kv_jobs, *query_jobs)
    keys_back, values_back = kv_jobs[0].result(), kv_jobs[1].result()
    joined_kv_grad = jnp.concatenate(
        [rotate(keys_back, cosine, -sine_part).astype(bf16), values_back.astype(bf16)], axis=1
    )
    grad_joined = jnp.concatenate([joined_q_grad, joined_kv_grad], axis=1)
    grad_one = product_back(grad_joined, qkv_from).astype(bf16)
    grad_normed_one = (
        product_back(joined_q_grad[:, :half], query_one)
        + product_back(joined_q_grad[:, half:], query_two)
        + product_back(joined_kv_grad, kv_full)
        + product_back(grad_one, qkv_into)
    )
    gain_one_grad = jnp.sum(grad_normed_one * unit_one, axis=0)
    stream_grad = grad_middle + norm_back(grad_normed_one, unit_one, inverse_one, gain_one)
    last = (
        product_rows(normed_one, jnp.concatenate([joined_kv_grad, grad_one], axis=1)).astype(bf16),
        jnp.concatenate(
            [
                product_rows(lowrank_one, grad_joined).astype(bf16),
                product_rows(lowrank_two, grad_branch).astype(bf16),
                expand_down.astype(bf16),
                gain_one_grad.reshape(R, -1).astype(bf16),
                gain_two_grad.reshape(R, -1).astype(bf16),
                jnp.zeros((R, 128 - 2 * gain_columns), bf16),
            ],
            axis=1,
        ),
    )
    _, (last, gate_sum) = advance(*query_jobs, beside=(last, gate_sum))
    up_sum = scatter_units(tie(up_terms, gate_sum))
    last_jobs = [scatter_weights(terms, order) for terms, order in zip(last, (backs[0], backs[2]))]
    for _ in range(steps - 1):
        arrived, _ = advance(*query_jobs, *last_jobs)
    sums = [value.astype(f32) for value in tie((down_sum, gate_sum, up_sum), arrived)]
    weights_grad = (
        sums[0][:, :D],
        sums[0][:, D:],
        jnp.stack([sums[1][:, :D], sums[2][:, :D]], axis=1),
        jnp.stack([sums[1][:, D:], sums[2][:, D:]], axis=1),
    )
    _, weights_grad = advance(*last_jobs, beside=weights_grad)
    downweight_grad, downadapt_grad, gateweight_grad, gateexpand_grad = weights_grad
    advance(*last_jobs)
    kv_grad, expand_grad = last_jobs[0].result(), last_jobs[1].result()
    gains_grad = expand_grad[:, qkv_columns + 2 * D :]
    n_gain = attn_gain.shape[0]
    return (
        result,
        stream_grad,
        gains_grad[:, :gain_columns].reshape(n_gain),
        jnp.concatenate([job.result() for job in query_jobs] + [kv_grad[:, : 2 * DH]], axis=1),
        kv_grad[:, 2 * DH : 2 * DH + R],
        expand_grad[:, :qkv_columns],
        jnp.concatenate([job.result()[:, :half] for job in out_jobs[:2]], axis=1),
        out_jobs[0].result()[:, half:],
        expand_grad[:, qkv_columns : qkv_columns + D],
        gains_grad[:, gain_columns : 2 * gain_columns].reshape(n_gain),
        gateweight_grad,
        out_jobs[2].result(),
        gateexpand_grad,
        downweight_grad,
        downadapt_grad,
        expand_grad[:, qkv_columns + D : qkv_columns + 2 * D],
        root_means,
    )


def solution(mesh):
    levels = mesh.shape["blk"].bit_length() - 1
    ranking = ("seq", "head") + tuple(f"blk{i}" for i in reversed(range(levels)))
    fine = jax.sharding.Mesh(mesh.devices.reshape((2,) * len(ranking)), ranking)
    rows = [P(ranking, *([None] * (rank - 1))) for rank in range(4)]
    in_specs = tuple(
        rows[rank] for rank in (2, 1, 2, 2, 2, 2, 2, 2, 1, 3, 2, 3, 2, 2, 2, 2)
    )
    out_specs = tuple(
        rows[rank] for rank in (2, 2, 1, 2, 2, 2, 2, 2, 2, 1, 3, 2, 3, 2, 2, 2)
    ) + (P(None, ranking),)
    return jax.shard_map(
        functools.partial(body, ranking),
        mesh=fine,
        in_specs=in_specs,
        out_specs=out_specs,
        check_vma=False,
    )
```

time: 3290 us -> 911 us (0.28)
  waiting for transfers between devices: 2690 us -> 362 us
  blocking collectives: 161 us -> 0 us
  starting transfers between devices: 11.8 us -> 108 us
  matrix products: 267 us -> 204 us
  other arithmetic: 56.4 us -> 108 us
    reduce_scatter x12 -> x4, waiting for transfers between devices: 1970 us -> 23.5 us  [the longest x3 23.5 us: scatter_units(): return lax.psum_scatter(terms, unit_axes, scatter_dimension=0, tiled=True)]
    all_gather x15 -> x4, waiting for transfers between devices: 688 us -> 0.01 us  [the longest x3 0.01 us: gather_units(): return lax.all_gather(block, unit_axes, axis=0, tiled=True)]
    ppermute x0 -> x94, waiting for transfers between devices: none -> 338 us  [shift(): return lax.ppermute(values, axes, [(i, i ^ mask) for i in range(size)])]
    dot_general x17 -> x0, matrix products: 115 us -> none  [the longest x1 25.5 us: body(): jnp.einsum('td,nkd->tkn', rows_group, group_gate, preferred_element_type=...]
    ppermute x0 -> x94, starting transfers between devices: none -> 107 us  [shift(): return lax.ppermute(values, axes, [(i, i ^ mask) for i in range(size)])]
    unnamed x2 -> x0, blocking collectives: 96.2 us -> none
    all_gather x2 -> x0, blocking collectives: 64.3 us -> none  [the longest x1 33 us: body(): lax.all_gather(grad_four, 'blk', axis=0, tiled=True)]
    another operation x3 -> x79, other arithmetic: 1.5 us -> 54 us  [the longest x75 52.5 us: place(): jnp.stack([jnp.where(first, own, other), jnp.where(first, other, own)], a...]
  transfers between devices with their start and end apart: 30 -> 102, of which waited for: 27 -> 47; matrix products, arithmetic and copies ran while one was open for 10% -> 41% of each run, Pallas kernels for 0% -> 0%
where the time goes in v1:
time: 911 us; the launch traced here: 904 us
  waiting for transfers between devices  362 us (40%)
  matrix products  204 us (22%)
  starting transfers between devices  108 us (12%)
  other arithmetic  108 us (12%)
  local copies, waits for them, and re-layouts  104 us (11%)
  between operations  17.9 us (2%)
    ppermute x94, waiting for transfers between devices, shift(): return lax.ppermute(values, axes, [(i, i ^ mask) for i in range(size)])  338 us
    ppermute x94, starting transfers between devices, shift(): return lax.ppermute(values, axes, [(i, i ^ mask) for i in range(size)])  107 us
    dot_general x16, matrix products, product_back(): lax.dot_general(former, latter, (((1,), (1,)), ((), ())), preferred_eleme...  76.8 us
    dot_general x17, matrix products, product(): return jnp.dot(former, latter, preferred_element_type=jnp.float32)  65.3 us
    dot_general x14, matrix products, product_rows(): lax.dot_general(former, latter, (((0,), (0,)), ((), ())), preferred_eleme...  61.6 us
    unnamed x366, local copies, waits for them, and re-layouts  54.2 us
    another operation x75, other arithmetic, place(): jnp.stack([jnp.where(first, own, other), jnp.where(first, other, own)], a...  52.5 us
    convert_element_type x38, other arithmetic, finish(): self.value = self.value.astype(jnp.bfloat16)  25.6 us
  transfers between devices with their start and end apart: 102, of which 47 were waited for; matrix products, arithmetic and copies ran while one was open for 41% of the time, Pallas kernels for 0%

profile of v1, /device:TPU:0, one launch (start us, length us, event | category | flops | bytes accessed | tf_op | source)
XLA Modules:
  0.0 903.6 jit_solution(11913706269411128750)
XLA Ops:
  7.3 3.4 pad_maximum_fusion.15
  10.8 4.1 collective-permute-start.2
  18.9 4.3 collective-permute-done
  23.3 4.9 copy.58
  35.7 6.0 collective-permute-done.4
  43.2 10.4 %collective-permute-done.6 = bf16[2,64,1024]{2,1,0:T(8,128)(2,1)S(1)} collective-permute-done((bf16[2,64,1024]{2,1,0:T(8,128)(2,1)S(1)}, bf16[2,64,1024]{2,1,0:T(8,128)(2,1)S(1)}, u32[]{:S(2)}, u32[]{:S(2)}) %collective-permute-start.6) | collective-permute-done | bytes 262176 | tf_op jit(solution)/shard_map/ppermute | solution.py:71
  61.8 16.4 %collective-permute-done.8 = bf16[2,2,64,768]{3,2,1,0:T(8,128)(2,1)} collective-permute-done((bf16[2,2,64,768]{3,2,1,0:T(8,128)(2,1)}, bf16[2,2,64,768]{3,2,1,0:T(8,128)(2,1)}, u32[]{:S(2)}, u32[]{:S(2)}) %collective-permute-start.8) | collective-permute-done | bytes 393248 | tf_op jit(solution)/shard_map/ppermute | solution.py:71
  93.5 35.1 %collective-permute-done.12 = bf16[2,2,2,64,768]{4,3,2,1,0:T(8,128)(2,1)} collective-permute-done((bf16[2,2,2,64,768]{4,3,2,1,0:T(8,128)(2,1)}, bf16[2,2,2,64,768]{4,3,2,1,0:T(8,128)(2,1)}, u32[]{:S(2)}, u32[]{:S(2)}) %collective-permute-start.12) | collective-permute-done | bytes 786464 | tf_op jit(solution)/shard_map/ppermute | solution.py:71
  165.5 3.4 select_bitcast_fusion.5
  182.1 8.7 collective-permute-done.25
  198.7 15.2 %collective-permute-done.29 = bf16[2,2,128,256]{3,2,1,0:T(8,128)(2,1)S(1)} collective-permute-done((bf16[2,2,128,256]{3,2,1,0:T(8,128)(2,1)S(1)}, bf16[2,2,128,256]{3,2,1,0:T(8,128)(2,1)S(1)}, u32[]{:S(2)}, u32[]{:S(2)}) %collective-permute-start.29) | collective-permute-done | bytes 262176 | tf_op jit(solution)/shard_map/ppermute | solution.py:71
  225.8 33.4 %collective-permute-done.33 = bf16[2,2,2,128,256]{4,3,2,0,1:T(8,128)(2,1)} collective-permute-done((bf16[2,2,2,128,256]{4,3,2,0,1:T(8,128)(2,1)}, bf16[2,2,2,128,256]{4,3,2,0,1:T(8,128)(2,1)}, u32[]{:S(2)}, u32[]{:S(2)}) %collective-permute-start.33) | collective-permute-done | bytes 524320 | tf_op jit(solution)/shard_map/ppermute | solution.py:71
  270.1 3.5 fusion.9
  273.7 3.6 fusion.8
  300.7 19.5 %collective-permute-done.38 = bf16[128,2048]{1,0:T(8,128)(2,1)S(1)} collective-permute-done((bf16[128,2048]{1,0:T(8,128)(2,1)S(1)}, bf16[128,2048]{1,0:T(8,128)(2,1)S(1)}, u32[]{:S(2)}, u32[]{:S(2)}) %collective-permute-start.38) | collective-permute-done | bytes 524320 | tf_op jit(solution)/shard_map/ppermute | solution.py:71
  320.1 15.7 %collective-permute-done.39 = bf16[128,2048]{1,0:T(8,128)(2,1)S(1)} collective-permute-done((bf16[128,2048]{1,0:T(8,128)(2,1)S(1)}, bf16[128,2048]{1,0:T(8,128)(2,1)S(1)}, u32[]{:S(2)}, u32[]{:S(2)}) %collective-permute-start.39) | collective-permute-done | bytes 524320 | tf_op jit(solution)/shard_map/ppermute | solution.py:71
  341.8 9.0 collective-permute-done.42
  351.6 16.0 %collective-permute-done.43 = bf16[128,2048]{1,0:T(8,128)(2,1)S(1)} collective-permute-done((bf16[128,2048]{1,0:T(8,128)(2,1)S(1)}, bf16[128,2048]{1,0:T(8,128)(2,1)S(1)}, u32[]{:S(2)}, u32[]{:S(2)}) %collective-permute-start.43) | collective-permute-done | bytes 524320 | tf_op jit(solution)/shard_map/ppermute | solution.py:71
  368.5 6.8 collective-permute-done.44
  376.1 3.9 convolution_convert_fusion.15
  380.0 14.9 %fusion.176 = f32[1024,2048]{1,0:T(8,128)} fusion(bf16[2048,2304]{1,0:T(8,128)(2,1)} %all-gather.7.cloned.1.call-done, bf16[1024,256]{1,0:T(8,128)(2,1)S(1)} %convolution_convert_fusion.15, bf16[1024,2048]{1,0:T(8,128)(2,1)S(1)} %copy-done.122), kind=kOutput, calls=%fused_computation.581 | convolution fusion | flops 9673113600 | bytes 22544384 | tf_op jit(solution)/shard_map/dot_general | solution.py:24
  395.0 19.2 %multiply_convert_fusion.2 = (bf16[1024,2048]{1,0:T(8,128)(2,1)}, f32[1024,2048]{1,0:T(8,128)}) fusion(f32[1024,2048]{1,0:T(8,128)} %fusion.176, bf16[2048,2304]{1,0:T(8,128)(2,1)} %all-gather.9.cloned.1.call-done, bf16[1024,256]{1,0:T(8,128)(2,1)S(1)} %convolution_convert_fusion.15, bf16[1024,2048]{1,0:T(8,128)(2,1)} %constant_dynamic-update-slice_fusion.8), kind=kOutput, calls=%fused_computation.18 | convolution fusion | flops 9694085120 | bytes 35127296 | tf_op jit(solution)/shard_map/dot_general | solution.py:24
  414.2 13.4 %convolution_convert_fusion.4 = bf16[1024,2304]{1,0:T(8,128)(2,1)S(1)} fusion(bf16[1024,2048]{1,0:T(8,128)(2,1)} %get-tuple-element.191, bf16[2048,2304]{1,0:T(8,128)(2,1)} %all-gather.5.cloned.1.call-done), kind=kOutput, calls=%fused_computation.24 | convolution fusion | flops 9666035712 | bytes 18350080 | tf_op jit(solution)/shard_map/dot_general | solution.py:20
  444.7 22.7 %fusion.6 = (bf16[1024,2048]{1,0:T(8,128)(2,1)}, bf16[1024,2048]{1,0:T(8,128)(2,1)}) fusion(f32[1024,2048]{1,0:T(8,128)} %fusion.176, f32[1024,2048]{1,0:T(8,128)} %get-tuple-element.467, bf16[2048,2304]{1,0:T(8,128)(2,1)} %all-gather.5.cloned.1.call-done, bf16[1024,256]{1,0:T(8,128)(2,1)S(1)} %copy.82, bf16[1024,2048]{1,0:T(8,128)(2,1)} %copy-done.125), kind=kOutput, calls=%fused_computation.14 | convolution fusion | flops 9723445248 | bytes 39321600 | tf_op jit(solution)/shard_map/dot_general | solution.py:24
  467.4 13.7 %fusion.205 = f32[1024,2304]{1,0:T(8,128)S(1)} fusion(bf16[1024,2048]{1,0:T(8,128)(2,1)} %get-tuple-element.195, bf16[2048,2304]{1,0:T(8,128)(2,1)} %all-gather.9.cloned.1.call-done), kind=kOutput, calls=%fused_computation.592 | convolution fusion | flops 9663676416 | bytes 23068672 | tf_op jit(solution)/shard_map/dot_general | solution.py:20
  481.0 12.2 %add_convert_fusion = bf16[1024,2304]{1,0:T(8,128)(2,1)S(1)} fusion(f32[1024,2304]{1,0:T(8,128)S(1)} %fusion.205, bf16[1024,2048]{1,0:T(8,128)(2,1)S(1)} %copy-done.152, bf16[2048,2304]{1,0:T(8,128)(2,1)} %all-gather.7.cloned.1.call-done), kind=kOutput, calls=%fused_computation.7 | convolution fusion | flops 9668395008 | bytes 27787264 | tf_op jit(solution)/shard_map/dot_general | solution.py:20
  494.8 17.6 %collective-permute-start.46 = (bf16[2,2,128,1152]{3,2,0,1:T(8,128)(2,1)}, bf16[2,2,128,1152]{3,2,0,1:T(8,128)(2,1)S(1)}, u32[]{:S(2)}, u32[]{:S(2)}) collective-permute-start(bf16[2,2,128,1152]{3,2,0,1:T(8,128)(2,1)} %bitcast.620), channel_id=1, source_target_pairs={{0,2},{2,0},{1,3},{3,1},{4,6},{6,4},{5,7},{7,5},{8,10},{10,8},{9,1... | collective-permute-start | bytes 3538952 | tf_op jit(solution)/shard_map/ppermute | solution.py:71
  514.3 13.1 %convolution_convert_fusion.1 = bf16[2048,2304]{1,0:T(8,128)(2,1)} fusion(bf16[1024,2048]{1,0:T(8,128)(2,1)S(1)} %copy-done.153, bf16[1024,256]{1,0:T(8,128)(2,1)S(1)} %copy-done.150, bf16[1024,2048]{1,0:T(8,128)(2,1)S(1)} %copy-done.123), kind=kOutput, calls=%fused_computation.5 | convolution fusion | flops 9677832192 | bytes 18350080 | tf_op jit(solution)/shard_map/dot_general | solution.py:30
  527.4 15.4 %convolution_convert_fusion.2 = bf16[2048,2304]{1,0:T(8,128)(2,1)} fusion(bf16[1024,2048]{1,0:T(8,128)(2,1)} %get-tuple-element.191, bf16[1024,256]{1,0:T(8,128)(2,1)} %copy-done.95, bf16[1024,2048]{1,0:T(8,128)(2,1)} %copy-done.125), kind=kOutput, calls=%fused_computation.6 | convolution fusion | flops 9677832192 | bytes 18350080 | tf_op jit(solution)/shard_map/dot_general | solution.py:30
  542.8 15.2 %collective-permute-done.46 = bf16[2,2,128,1152]{3,2,0,1:T(8,128)(2,1)S(1)} collective-permute-done((bf16[2,2,128,1152]{3,2,0,1:T(8,128)(2,1)}, bf16[2,2,128,1152]{3,2,0,1:T(8,128)(2,1)S(1)}, u32[]{:S(2)}, u32[]{:S(2)}) %collective-permute-start.46) | collective-permute-done | bytes 1179680 | tf_op jit(solution)/shard_map/ppermute | solution.py:71
  566.2 12.9 %convolution_convert_fusion = bf16[2048,2304]{1,0:T(8,128)(2,1)} fusion(bf16[1024,2048]{1,0:T(8,128)(2,1)S(1)} %copy-done.154, bf16[1024,256]{1,0:T(8,128)(2,1)S(1)} %copy-done.151, bf16[1024,2048]{1,0:T(8,128)(2,1)S(1)} %copy-done.124), kind=kOutput, calls=%fused_computation.4 | convolution fusion | flops 9677832192 | bytes 18350080 | tf_op jit(solution)/shard_map/dot_general | solution.py:30
  579.2 6.0 collective-permute-done.48
  589.2 5.2 collective-permute-done.50
  594.4 4.6 collective-permute-done.49
  630.8 19.8 %collective-permute-done.55 = bf16[2,2,2,64,1024]{4,3,1,0,2:T(8,128)(2,1)S(1)} collective-permute-done((bf16[2,2,2,64,1024]{4,3,1,0,2:T(8,128)(2,1)S(1)}, bf16[2,2,2,64,1024]{4,3,1,0,2:T(8,128)(2,1)S(1)}, u32[]{:S(2)}, u32[]{:S(2)}) %collective-permute-start.55) | collective-permute-done | bytes 1048608 | tf_op jit(solution)/shard_map/ppermute | solution.py:71
  662.4 16.2 %collective-permute-done.61 = bf16[2,2,64,256]{3,2,1,0:T(8,128)(2,1)} collective-permute-done((bf16[2,2,64,256]{3,2,1,0:T(8,128)(2,1)S(1)}, bf16[2,2,64,256]{3,2,1,0:T(8,128)(2,1)}, u32[]{:S(2)}, u32[]{:S(2)}) %collective-permute-start.61) | collective-permute-done | bytes 131104 | tf_op jit(solution)/shard_map/ppermute | solution.py:71
  685.1 4.7 convolution_multiply_fusion.1
  719.8 6.3 collective-permute-done.70
  728.9 5.1 collective-permute-done.67
  757.7 6.8 concatenate.131
  764.5 3.6 convolution_convert_fusion.9
  781.0 10.7 %collective-permute-done.79 = bf16[2,2,64,1024]{3,2,1,0:T(8,128)(2,1)S(1)} collective-permute-done((bf16[2,2,64,1024]{3,2,1,0:T(8,128)(2,1)S(1)}, bf16[2,2,64,1024]{3,2,1,0:T(8,128)(2,1)S(1)}, u32[]{:S(2)}, u32[]{:S(2)}) %collective-permute-start.79) | collective-permute-done | bytes 524320 | tf_op jit(solution)/shard_map/ppermute | solution.py:71
  800.8 10.3 %collective-permute-done.83 = bf16[2,64,1024]{2,1,0:T(8,128)(2,1)S(1)} collective-permute-done((bf16[2,64,1024]{2,1,0:T(8,128)(2,1)S(1)}, bf16[2,64,1024]{2,1,0:T(8,128)(2,1)S(1)}, u32[]{:S(2)}, u32[]{:S(2)}) %collective-permute-start.83) | collective-permute-done | bytes 262176 | tf_op jit(solution)/shard_map/ppermute | solution.py:71
  811.2 7.2 collective-permute-done.82
  827.4 3.4 collective-permute-done.87
  838.7 23.5 %reduce-scatter.11.cloned.1.call-done = bf16[512,2304]{1,0:T(8,128)(2,1)} async-done(((bf16[2048,2304]{1,0:T(8,128)(2,1)}), bf16[512,2304]{1,0:T(8,128)(2,1)}) %reduce-scatter.11.cloned.1.call-update) | async-done | bytes 2359312 | tf_op jit(solution)/shard_map/reduce_scatter | solution.py:373
  868.1 4.2 slice.341
  879.4 11.1 %copy.108 = f32[512,2,2048]{2,1,0:T(2,128)} copy(f32[512,2,2048]{2,0,1:T(8,128)S(1)} %pad_maximum_fusion) | data formatting | bytes 16777216
  (853 shorter events, 343.3 us)
Async XLA Ops:
  7.3 121.4 %all-gather.5.cloned.1.call-start = ((), (), s32[]{:S(2)}) async-start(), calls=%async_computation.4 | async-start | bytes 11796480 | tf_op jit(solution)/shard_map/all_gather | solution.py:218
  10.7 163.4 %all-gather.7.cloned.1.call-start = ((), (), s32[]{:S(2)}) async-start(), calls=%async_computation.5 | async-start | bytes 11796480 | tf_op jit(solution)/shard_map/all_gather | solution.py:218
  29.7 23.9 %collective-permute-start.6 = (bf16[2,64,1024]{2,1,0:T(8,128)(2,1)S(1)}, bf16[2,64,1024]{2,1,0:T(8,128)(2,1)S(1)}, u32[]{:S(2)}, u32[]{:S(2)}) collective-permute-start(bf16[2,64,1024]{2,1,0:T(8,128)(2,1)S(1)} %pad_maximum_fusion.43), channel_id=1, source_target_pairs={{0,8},{8,0},{1,9},{9,1},{2,10},{10,2},{3,11},{11,3},{4,12},{12,4},... | collective-permute-start | bytes 786440 | tf_op jit(solution)/shard_map/ppermute | solution.py:71
  54.5 24.1 %collective-permute-start.11 = (bf16[2,2,64,1024]{3,2,1,0:T(8,128)(2,1)}, bf16[2,2,64,1024]{3,2,1,0:T(8,128)(2,1)S(1)}, u32[]{:S(2)}, u32[]{:S(2)}) collective-permute-start(bf16[2,2,64,1024]{3,2,1,0:T(8,128)(2,1)} %pad_maximum_fusion.34), channel_id=1, source_target_pairs={{0,4},{4,0},{1,5},{5,1},{2,6},{6,2},{3,7},{7,3},{8,12},{12,8},{9,1... | collective-permute-start | bytes 1572872 | tf_op jit(solution)/shard_map/ppermute | solution.py:71
  54.8 24.6 %collective-permute-start.10 = (bf16[2,2,64,1024]{3,2,1,0:T(8,128)(2,1)S(1)}, bf16[2,2,64,1024]{3,2,1,0:T(8,128)(2,1)}, u32[]{:S(2)}, u32[]{:S(2)}) collective-permute-start(bf16[2,2,64,1024]{3,2,1,0:T(8,128)(2,1)S(1)} %pad_maximum_fusion.33), channel_id=1, source_target_pairs={{0,2},{2,0},{1,3},{3,1},{4,6},{6,4},{5,7},{7,5},{8,10},{10,8},{9,1... | collective-permute-start | bytes 1572872 | tf_op jit(solution)/shard_map/ppermute | solution.py:71
  81.6 47.1 %collective-permute-start.15 = (bf16[2,2,2,64,1024]{4,3,2,1,0:T(8,128)(2,1)}, bf16[2,2,2,64,1024]{4,3,2,1,0:T(8,128)(2,1)}, u32[]{:S(2)}, u32[]{:S(2)}) collective-permute-start(bf16[2,2,2,64,1024]{4,3,2,1,0:T(8,128)(2,1)} %pad_maximum_fusion.24), channel_id=1, source_target_pairs={{0,1},{1,0},{2,3},{3,2},{4,5},{5,4},{6,7},{7,6},{8,9},{9,8},{10,11... | collective-permute-start | bytes 3145736 | tf_op jit(solution)/shard_map/ppermute | solution.py:71
  85.5 43.2 %collective-permute-start.14 = (bf16[2,2,2,64,1024]{4,3,2,1,0:T(8,128)(2,1)}, bf16[2,2,2,64,1024]{4,3,2,1,0:T(8,128)(2,1)}, u32[]{:S(2)}, u32[]{:S(2)}) collective-permute-start(bf16[2,2,2,64,1024]{4,3,2,1,0:T(8,128)(2,1)} %pad_maximum_fusion.23), channel_id=1, source_target_pairs={{0,1},{1,0},{2,3},{3,2},{4,5},{5,4},{6,7},{7,6},{8,9},{9,8},{10,11... | collective-permute-start | bytes 3145736 | tf_op jit(solution)/shard_map/ppermute | solution.py:71
  88.3 40.3 %collective-permute-start.13 = (bf16[2,2,2,8,6784]{4,3,2,1,0:T(8,128)(2,1)}, bf16[2,2,2,8,6784]{4,3,2,1,0:T(8,128)(2,1)}, u32[]{:S(2)}, u32[]{:S(2)}) collective-permute-start(bf16[2,2,2,8,6784]{4,3,2,1,0:T(8,128)(2,1)} %pad_maximum_fusion.28), channel_id=1, source_target_pairs={{0,4},{4,0},{1,5},{5,1},{2,6},{6,2},{3,7},{7,3},{8,12},{12,8},{9,1... | collective-permute-start | bytes 2605064 | tf_op jit(solution)/shard_map/ppermute | solution.py:71
  91.5 37.1 %collective-permute-start.12 = (bf16[2,2,2,64,768]{4,3,2,1,0:T(8,128)(2,1)}, bf16[2,2,2,64,768]{4,3,2,1,0:T(8,128)(2,1)}, u32[]{:S(2)}, u32[]{:S(2)}) collective-permute-start(bf16[2,2,2,64,768]{4,3,2,1,0:T(8,128)(2,1)} %pad_maximum_fusion.29), channel_id=1, source_target_pairs={{0,2},{2,0},{1,3},{3,1},{4,6},{6,4},{5,7},{7,5},{8,10},{10,8},{9,1... | collective-permute-start | bytes 2359304 | tf_op jit(solution)/shard_map/ppermute | solution.py:71
  93.3 168.4 %all-gather.9.cloned.1.call-start = ((), (), s32[]{:S(2)}) async-start(), calls=%async_computation.6 | async-start | bytes 11796480 | tf_op jit(solution)/shard_map/all_gather | solution.py:218
  143.6 30.5 %collective-permute-start.22 = (bf16[64,1280]{1,0:T(8,128)(2,1)}, bf16[64,1280]{1,0:T(8,128)(2,1)}, u32[]{:S(2)}, u32[]{:S(2)}) collective-permute-start(bf16[64,1280]{1,0:T(8,128)(2,1)} %pad_maximum_fusion.51), channel_id=1, source_target_pairs={{0,8},{8,0},{1,9},{9,1},{2,10},{10,2},{3,11},{11,3},{4,12},{12,4},... | collective-permute-start | bytes 491528 | tf_op jit(solution)/shard_map/ppermute | solution.py:71
  146.8 27.3 %collective-permute-start.23 = (bf16[64,1280]{1,0:T(8,128)(2,1)}, bf16[64,1280]{1,0:T(8,128)(2,1)}, u32[]{:S(2)}, u32[]{:S(2)}) collective-permute-start(bf16[64,1280]{1,0:T(8,128)(2,1)} %pad_maximum_fusion.52), channel_id=1, source_target_pairs={{0,4},{4,0},{1,5},{5,1},{2,6},{6,2},{3,7},{7,3},{8,12},{12,8},{9,1... | collective-permute-start | bytes 491528 | tf_op jit(solution)/shard_map/ppermute | solution.py:71
  174.2 260.4 %all-gather.11.cloned.1.call-start = ((), (), s32[]{:S(2)}) async-start(), calls=%async_computation.7 | async-start | bytes 4718592 | tf_op jit(solution)/shard_map/all_gather | solution.py:347
  193.8 22.5 %collective-permute-start.31 = (bf16[2,2,64,1280]{3,2,1,0:T(8,128)(2,1)S(1)}, bf16[2,2,64,1280]{3,2,1,0:T(8,128)(2,1)S(1)}, u32[]{:S(2)}, u32[]{:S(2)}) collective-permute-start(bf16[2,2,64,1280]{3,2,1,0:T(8,128)(2,1)S(1)} %pad_maximum_fusion.31), channel_id=1, source_target_pairs={{0,2},{2,0},{1,3},{3,1},{4,6},{6,4},{5,7},{7,5},{8,10},{10,8},{9,1... | collective-permute-start | bytes 1966088 | tf_op jit(solution)/shard_map/ppermute | solution.py:71
  194.0 22.3 %collective-permute-start.30 = (bf16[2,2,64,1280]{3,2,1,0:T(8,128)(2,1)S(1)}, bf16[2,2,64,1280]{3,2,1,0:T(8,128)(2,1)S(1)}, u32[]{:S(2)}, u32[]{:S(2)}) collective-permute-start(bf16[2,2,64,1280]{3,2,1,0:T(8,128)(2,1)S(1)} %pad_maximum_fusion.30), channel_id=1, source_target_pairs={{0,1},{1,0},{2,3},{3,2},{4,5},{5,4},{6,7},{7,6},{8,9},{9,8},{10,11... | collective-permute-start | bytes 1966088 | tf_op jit(solution)/shard_map/ppermute | solution.py:71
  217.7 42.9 %collective-permute-start.35 = (bf16[2,2,2,64,1280]{4,3,2,1,0:T(8,128)(2,1)}, bf16[2,2,2,64,1280]{4,3,2,1,0:T(8,128)(2,1)}, u32[]{:S(2)}, u32[]{:S(2)}) collective-permute-start(bf16[2,2,2,64,1280]{4,3,2,1,0:T(8,128)(2,1)} %pad_maximum_fusion.21), channel_id=1, source_target_pairs={{0,1},{1,0},{2,3},{3,2},{4,5},{5,4},{6,7},{7,6},{8,9},{9,8},{10,11... | collective-permute-start | bytes 3932168 | tf_op jit(solution)/shard_map/ppermute | solution.py:71
  220.4 41.2 %collective-permute-start.34 = (bf16[2,2,2,64,1280]{4,3,2,1,0:T(8,128)(2,1)}, bf16[2,2,2,64,1280]{4,3,2,1,0:T(8,128)(2,1)}, u32[]{:S(2)}, u32[]{:S(2)}) collective-permute-start(bf16[2,2,2,64,1280]{4,3,2,1,0:T(8,128)(2,1)} %pad_maximum_fusion.20), channel_id=1, source_target_pairs={{0,2},{2,0},{1,3},{3,1},{4,6},{6,4},{5,7},{7,5},{8,10},{10,8},{9,1... | collective-permute-start | bytes 3932168 | tf_op jit(solution)/shard_map/ppermute | solution.py:71
  223.2 36.0 %collective-permute-start.33 = (bf16[2,2,2,128,256]{4,3,2,0,1:T(8,128)(2,1)}, bf16[2,2,2,128,256]{4,3,2,0,1:T(8,128)(2,1)}, u32[]{:S(2)}, u32[]{:S(2)}) collective-permute-start(bf16[2,2,2,128,256]{4,3,2,0,1:T(8,128)(2,1)} %pad_maximum_fusion.37), channel_id=1, source_target_pairs={{0,1},{1,0},{2,3},{3,2},{4,5},{5,4},{6,7},{7,6},{8,9},{9,8},{10,11... | collective-permute-start | bytes 1572872 | tf_op jit(solution)/shard_map/ppermute | solution.py:71
  224.7 35.9 %collective-permute-start.32 = (bf16[2,2,2,128,256]{4,3,0,1,2:T(8,128)(2,1)}, bf16[2,2,2,128,256]{4,3,0,1,2:T(8,128)(2,1)}, u32[]{:S(2)}, u32[]{:S(2)}) collective-permute-start(bf16[2,2,2,128,256]{4,3,0,1,2:T(8,128)(2,1)} %pad_maximum_fusion.36), channel_id=1, source_target_pairs={{0,4},{4,0},{1,5},{5,1},{2,6},{6,2},{3,7},{7,3},{8,12},{12,8},{9,1... | collective-permute-start | bytes 1572872 | tf_op jit(solution)/shard_map/ppermute | solution.py:71
  295.7 24.4 %collective-permute-start.38 = (bf16[128,2048]{1,0:T(8,128)(2,1)S(1)}, bf16[128,2048]{1,0:T(8,128)(2,1)S(1)}, u32[]{:S(2)}, u32[]{:S(2)}) collective-permute-start(bf16[128,2048]{1,0:T(8,128)(2,1)S(1)} %get-tuple-element.330), channel_id=1, source_target_pairs={{0,2},{2,0},{4,6},{6,4},{1,3},{3,1},{5,7},{7,5},{8,10},{10,8},{12,... | collective-permute-start | bytes 1572872 | tf_op jit(solution)/shard_map/ppermute | solution.py:71
  297.6 38.2 %collective-permute-start.39 = (bf16[128,2048]{1,0:T(8,128)(2,1)S(1)}, bf16[128,2048]{1,0:T(8,128)(2,1)S(1)}, u32[]{:S(2)}, u32[]{:S(2)}) collective-permute-start(bf16[128,2048]{1,0:T(8,128)(2,1)S(1)} %get-tuple-element.330), channel_id=1, source_target_pairs={{0,4},{2,6},{4,0},{6,2},{1,5},{3,7},{5,1},{7,3},{8,12},{10,14},{12... | collective-permute-start | bytes 1572872 | tf_op jit(solution)/shard_map/ppermute | solution.py:71
  298.2 37.6 %collective-permute-start.40 = (bf16[128,2048]{1,0:T(8,128)(2,1)S(1)}, bf16[128,2048]{1,0:T(8,128)(2,1)S(1)}, u32[]{:S(2)}, u32[]{:S(2)}) collective-permute-start(bf16[128,2048]{1,0:T(8,128)(2,1)S(1)} %get-tuple-element.330), channel_id=1, source_target_pairs={{0,6},{2,4},{4,2},{6,0},{1,7},{3,5},{5,3},{7,1},{8,14},{10,12},{12... | collective-permute-start | bytes 1572872 | tf_op jit(solution)/shard_map/ppermute | solution.py:71
  300.1 40.8 %collective-permute-start.41 = (bf16[128,2048]{1,0:T(8,128)(2,1)S(1)}, bf16[128,2048]{1,0:T(8,128)(2,1)S(1)}, u32[]{:S(2)}, u32[]{:S(2)}) collective-permute-start(bf16[128,2048]{1,0:T(8,128)(2,1)S(1)} %get-tuple-element.330), channel_id=1, source_target_pairs={{0,1},{1,0},{2,3},{3,2},{4,5},{5,4},{6,7},{7,6},{8,9},{9,8},{10,11... | collective-permute-start | bytes 1572872 | tf_op jit(solution)/shard_map/ppermute | solution.py:71
  335.8 249.4 %reduce-scatter.5.cloned.1.call-start = ((), (), s32[]{:S(2)}) async-start(), calls=%async_computation.8 | async-start | bytes 5308416 | tf_op jit(solution)/shard_map/reduce_scatter | solution.py:356
  336.5 31.2 %collective-permute-start.43 = (bf16[128,2048]{1,0:T(8,128)(2,1)S(1)}, bf16[128,2048]{1,0:T(8,128)(2,1)S(1)}, u32[]{:S(2)}, u32[]{:S(2)}) collective-permute-start(bf16[128,2048]{1,0:T(8,128)(2,1)S(1)} %collective-permute-done.39), channel_id=1, source_target_pairs={{0,1},{1,0},{2,3},{3,2},{4,5},{5,4},{6,7},{7,6},{8,9},{9,8},{10,11... | collective-permute-start | bytes 1572872 | tf_op jit(solution)/shard_map/ppermute | solution.py:71
  338.0 37.3 %collective-permute-start.44 = (bf16[128,2048]{1,0:T(8,128)(2,1)S(1)}, bf16[128,2048]{1,0:T(8,128)(2,1)S(1)}, u32[]{:S(2)}, u32[]{:S(2)}) collective-permute-start(bf16[128,2048]{1,0:T(8,128)(2,1)S(1)} %collective-permute-done.40), channel_id=1, source_target_pairs={{0,1},{1,0},{2,3},{3,2},{4,5},{5,4},{6,7},{7,6},{8,9},{9,8},{10,11... | collective-permute-start | bytes 1572872 | tf_op jit(solution)/shard_map/ppermute | solution.py:71
  434.6 246.0 %reduce-scatter.7.cloned.1.call-start = ((), (), s32[]{:S(2)}) async-start(), calls=%async_computation.9 | async-start | bytes 11796480 | tf_op jit(solution)/shard_map/reduce_scatter | solution.py:373
  494.8 63.3 %collective-permute-start.46 = (bf16[2,2,128,1152]{3,2,0,1:T(8,128)(2,1)}, bf16[2,2,128,1152]{3,2,0,1:T(8,128)(2,1)S(1)}, u32[]{:S(2)}, u32[]{:S(2)}) collective-permute-start(bf16[2,2,128,1152]{3,2,0,1:T(8,128)(2,1)} %bitcast.620), channel_id=1, source_target_pairs={{0,2},{2,0},{1,3},{3,1},{4,6},{6,4},{5,7},{7,5},{8,10},{10,8},{9,1... | collective-permute-start | bytes 3538952 | tf_op jit(solution)/shard_map/ppermute | solution.py:71
  513.7 44.4 %collective-permute-start.45 = (bf16[2,2,128,1152]{3,2,0,1:T(8,128)(2,1)}, bf16[2,2,128,1152]{3,2,0,1:T(8,128)(2,1)}, u32[]{:S(2)}, u32[]{:S(2)}) collective-permute-start(bf16[2,2,128,1152]{3,2,0,1:T(8,128)(2,1)} %copy.83), channel_id=1, source_target_pairs={{0,1},{1,0},{2,3},{3,2},{4,5},{5,4},{6,7},{7,6},{8,9},{9,8},{10,11... | collective-permute-start | bytes 3538952 | tf_op jit(solution)/shard_map/ppermute | solution.py:71
  561.7 23.5 %collective-permute-start.48 = (bf16[2,128,1152]{2,1,0:T(8,128)(2,1)}, bf16[2,128,1152]{2,1,0:T(8,128)(2,1)}, u32[]{:S(2)}, u32[]{:S(2)}) collective-permute-start(bf16[2,128,1152]{2,1,0:T(8,128)(2,1)} %slice_bitcast_fusion.6), channel_id=1, source_target_pairs={{0,4},{4,0},{1,5},{5,1},{2,6},{6,2},{3,7},{7,3},{8,12},{12,8},{9,1... | collective-permute-start | bytes 1769480 | tf_op jit(solution)/shard_map/ppermute | solution.py:71
  563.9 21.3 %collective-permute-start.47 = (bf16[2,128,1152]{2,1,0:T(8,128)(2,1)S(1)}, bf16[2,128,1152]{2,1,0:T(8,128)(2,1)S(1)}, u32[]{:S(2)}, u32[]{:S(2)}) collective-permute-start(bf16[2,128,1152]{2,1,0:T(8,128)(2,1)S(1)} %slice_bitcast_fusion.7), channel_id=1, source_target_pairs={{0,2},{2,0},{1,3},{3,1},{4,6},{6,4},{5,7},{7,5},{8,10},{10,8},{9,1... | collective-permute-start | bytes 1769480 | tf_op jit(solution)/shard_map/ppermute | solution.py:71
  586.0 184.3 %reduce-scatter.9.cloned.1.call-start = ((), (), s32[]{:S(2)}) async-start(), calls=%async_computation.10 | async-start | bytes 11796480 | tf_op jit(solution)/shard_map/reduce_scatter | solution.py:373
  620.9 30.8 %collective-permute-start.54 = (bf16[2,2,2,64,1280]{4,3,0,1,2:T(8,128)(2,1)S(1)}, bf16[2,2,2,64,1280]{4,3,0,1,2:T(8,128)(2,1)S(1)}, u32[]{:S(2)}, u32[]{:S(2)}) collective-permute-start(bf16[2,2,2,64,1280]{4,3,0,1,2:T(8,128)(2,1)S(1)} %dynamic-slice_bitcast_fusion), channel_id=1, source_target_pairs={{0,2},{2,0},{1,3},{3,1},{4,6},{6,4},{5,7},{7,5},{8,10},{10,8},{9,1... | collective-permute-start | bytes 3932168 | tf_op jit(solution)/shard_map/ppermute | solution.py:71
  625.3 25.2 %collective-permute-start.55 = (bf16[2,2,2,64,1024]{4,3,1,0,2:T(8,128)(2,1)S(1)}, bf16[2,2,2,64,1024]{4,3,1,0,2:T(8,128)(2,1)S(1)}, u32[]{:S(2)}, u32[]{:S(2)}) collective-permute-start(bf16[2,2,2,64,1024]{4,3,1,0,2:T(8,128)(2,1)S(1)} %dynamic-slice_bitcast_fusion.3), channel_id=1, source_target_pairs={{0,1},{1,0},{2,3},{3,2},{4,5},{5,4},{6,7},{7,6},{8,9},{9,8},{10,11... | collective-permute-start | bytes 3145736 | tf_op jit(solution)/shard_map/ppermute | solution.py:71
  653.0 25.5 %collective-permute-start.60 = (bf16[2,2,64,1024]{3,2,1,0:T(8,128)(2,1)}, bf16[2,2,64,1024]{3,2,1,0:T(8,128)(2,1)}, u32[]{:S(2)}, u32[]{:S(2)}) collective-permute-start(bf16[2,2,64,1024]{3,2,1,0:T(8,128)(2,1)} %dynamic-slice_bitcast_fusion.9), channel_id=1, source_target_pairs={{0,2},{2,0},{1,3},{3,1},{4,6},{6,4},{5,7},{7,5},{8,10},{10,8},{9,1... | collective-permute-start | bytes 1572872 | tf_op jit(solution)/shard_map/ppermute | solution.py:71
  654.7 25.9 %collective-permute-start.59 = (bf16[2,2,64,1280]{3,2,0,1:T(8,128)(2,1)}, bf16[2,2,64,1280]{3,2,0,1:T(8,128)(2,1)}, u32[]{:S(2)}, u32[]{:S(2)}) collective-permute-start(bf16[2,2,64,1280]{3,2,0,1:T(8,128)(2,1)} %dynamic-slice_bitcast_fusion.6), channel_id=1, source_target_pairs={{0,1},{1,0},{2,3},{3,2},{4,5},{5,4},{6,7},{7,6},{8,9},{9,8},{10,11... | collective-permute-start | bytes 1966088 | tf_op jit(solution)/shard_map/ppermute | solution.py:71
  656.7 23.9 %collective-permute-start.58 = (bf16[2,2,2,128,256]{4,3,0,1,2:T(8,128)(2,1)}, bf16[2,2,2,128,256]{4,3,0,1,2:T(8,128)(2,1)}, u32[]{:S(2)}, u32[]{:S(2)}) collective-permute-start(bf16[2,2,2,128,256]{4,3,0,1,2:T(8,128)(2,1)} %bitcast.621), channel_id=1, source_target_pairs={{0,2},{2,0},{1,3},{3,1},{4,6},{6,4},{5,7},{7,5},{8,10},{10,8},{9,1... | collective-permute-start | bytes 1572872 | tf_op jit(solution)/shard_map/ppermute | solution.py:71
  660.1 20.5 %collective-permute-start.57 = (bf16[2,2,2,128,256]{4,3,1,0,2:T(8,128)(2,1)}, bf16[2,2,2,128,256]{4,3,1,0,2:T(8,128)(2,1)}, u32[]{:S(2)}, u32[]{:S(2)}) collective-permute-start(bf16[2,2,2,128,256]{4,3,1,0,2:T(8,128)(2,1)} %bitcast.622), channel_id=1, source_target_pairs={{0,8},{8,0},{1,9},{9,1},{2,10},{10,2},{3,11},{11,3},{4,12},{12,4},... | collective-permute-start | bytes 1572872 | tf_op jit(solution)/shard_map/ppermute | solution.py:71
  680.6 181.6 %reduce-scatter.11.cloned.1.call-start = ((), (), s32[]{:S(2)}) async-start(), calls=%async_computation.11 | async-start | bytes 11796480 | tf_op jit(solution)/shard_map/reduce_scatter | solution.py:373
  709.5 28.6 %collective-permute-start.75 = (bf16[2,2,2,2,64,1024]{5,4,1,0,2,3:T(8,128)(2,1)S(1)}, bf16[2,2,2,2,64,1024]{5,4,1,0,2,3:T(8,128)(2,1)S(1)}, u32[]{:S(2)}, u32[]{:S(2)}) collective-permute-start(bf16[2,2,2,2,64,1024]{5,4,1,0,2,3:T(8,128)(2,1)S(1)} %bitcast.671), channel_id=1, source_target_pairs={{0,16},{16,0},{1,17},{17,1},{2,18},{18,2},{3,19},{19,3},{4,20},{20... | collective-permute-start | bytes 6291464 | tf_op jit(solution)/shard_map/ppermute | solution.py:71
  709.6 28.6 %collective-permute-start.74 = (bf16[2,2,2,2,64,1024]{5,4,0,1,3,2:T(8,128)(2,1)S(1)}, bf16[2,2,2,2,64,1024]{5,4,0,1,3,2:T(8,128)(2,1)S(1)}, u32[]{:S(2)}, u32[]{:S(2)}) collective-permute-start(bf16[2,2,2,2,64,1024]{5,4,0,1,3,2:T(8,128)(2,1)S(1)} %bitcast.670), channel_id=1, source_target_pairs={{0,16},{16,0},{1,17},{17,1},{2,18},{18,2},{3,19},{19,3},{4,20},{20... | collective-permute-start | bytes 6291464 | tf_op jit(solution)/shard_map/ppermute | solution.py:71
  743.1 25.0 %collective-permute-start.77 = (bf16[2,2,2,64,1024]{4,3,1,0,2:T(8,128)(2,1)}, bf16[2,2,2,64,1024]{4,3,1,0,2:T(8,128)(2,1)}, u32[]{:S(2)}, u32[]{:S(2)}) collective-permute-start(bf16[2,2,2,64,1024]{4,3,1,0,2:T(8,128)(2,1)} %dynamic-slice_bitcast_fusion.1), channel_id=1, source_target_pairs={{0,1},{1,0},{2,3},{3,2},{4,5},{5,4},{6,7},{7,6},{8,9},{9,8},{10,11... | collective-permute-start | bytes 3145736 | tf_op jit(solution)/shard_map/ppermute | solution.py:71
  746.7 23.6 %collective-permute-start.76 = (bf16[2,2,2,64,1024]{4,3,0,1,2:T(8,128)(2,1)}, bf16[2,2,2,64,1024]{4,3,0,1,2:T(8,128)(2,1)}, u32[]{:S(2)}, u32[]{:S(2)}) collective-permute-start(bf16[2,2,2,64,1024]{4,3,0,1,2:T(8,128)(2,1)} %dynamic-slice_bitcast_fusion.2), channel_id=1, source_target_pairs={{0,2},{2,0},{1,3},{3,1},{4,6},{6,4},{5,7},{7,5},{8,10},{10,8},{9,1... | collective-permute-start | bytes 3145736 | tf_op jit(solution)/shard_map/ppermute | solution.py:71
  773.5 20.3 %collective-permute-start.81 = (bf16[2,2,2,2,8,6784]{5,4,1,0,2,3:T(8,128)(2,1)S(1)}, bf16[2,2,2,2,8,6784]{5,4,1,0,2,3:T(8,128)(2,1)S(1)}, u32[]{:S(2)}, u32[]{:S(2)}) collective-permute-start(bf16[2,2,2,2,8,6784]{5,4,1,0,2,3:T(8,128)(2,1)S(1)} %bitcast.673), channel_id=1, source_target_pairs={{0,16},{16,0},{1,17},{17,1},{2,18},{18,2},{3,19},{19,3},{4,20},{20... | collective-permute-start | bytes 5210120 | tf_op jit(solution)/shard_map/ppermute | solution.py:71
  794.3 25.2 %collective-permute-start.85 = (bf16[2,2,2,8,6784]{4,3,1,0,2:T(8,128)(2,1)S(1)}, bf16[2,2,2,8,6784]{4,3,1,0,2:T(8,128)(2,1)S(1)}, u32[]{:S(2)}, u32[]{:S(2)}) collective-permute-start(bf16[2,2,2,8,6784]{4,3,1,0,2:T(8,128)(2,1)S(1)} %dynamic-slice_bitcast_fusion.4), channel_id=1, source_target_pairs={{0,1},{1,0},{2,3},{3,2},{4,5},{5,4},{6,7},{7,6},{8,9},{9,8},{10,11... | collective-permute-start | bytes 2605064 | tf_op jit(solution)/shard_map/ppermute | solution.py:71
  795.2 24.3 %collective-permute-start.84 = (bf16[2,2,2,64,768]{4,3,0,1,2:T(8,128)(2,1)S(1)}, bf16[2,2,2,64,768]{4,3,0,1,2:T(8,128)(2,1)S(1)}, u32[]{:S(2)}, u32[]{:S(2)}) collective-permute-start(bf16[2,2,2,64,768]{4,3,0,1,2:T(8,128)(2,1)S(1)} %dynamic-slice_bitcast_fusion.5), channel_id=1, source_target_pairs={{0,2},{2,0},{1,3},{3,1},{4,6},{6,4},{5,7},{7,5},{8,10},{10,8},{9,1... | collective-permute-start | bytes 2359304 | tf_op jit(solution)/shard_map/ppermute | solution.py:71
  833.7 40.5 %collective-permute-start.91 = (bf16[2,8,6784]{2,1,0:T(8,128)(2,1)}, bf16[2,8,6784]{2,1,0:T(8,128)(2,1)}, u32[]{:S(2)}, u32[]{:S(2)}) collective-permute-start(bf16[2,8,6784]{2,1,0:T(8,128)(2,1)} %dynamic-slice_bitcast_fusion.19), channel_id=1, source_target_pairs={{0,8},{8,0},{1,9},{9,1},{2,10},{10,2},{3,11},{11,3},{4,12},{12,4},... | collective-permute-start | bytes 651272 | tf_op jit(solution)/shard_map/ppermute | solution.py:71
  836.1 38.1 %collective-permute-start.90 = (bf16[2,64,768]{2,1,0:T(8,128)(2,1)}, bf16[2,64,768]{2,1,0:T(8,128)(2,1)}, u32[]{:S(2)}, u32[]{:S(2)}) collective-permute-start(bf16[2,64,768]{2,1,0:T(8,128)(2,1)} %dynamic-slice_bitcast_fusion.20), channel_id=1, source_target_pairs={{0,4},{4,0},{1,5},{5,1},{2,6},{6,2},{3,7},{7,3},{8,12},{12,8},{9,1... | collective-permute-start | bytes 589832 | tf_op jit(solution)/shard_map/ppermute | solution.py:71
  (215 other events, 1931.5 us)
Sparse Core Ops, SparseCore 0:
  10.9 78.1 all-gather.4
  93.4 67.3 all-gather.6
  174.3 65.2 all-gather.8
  335.9 87.1 all-gather.10
  434.7 121.0 reduce-scatter.4
  585.3 76.8 reduce-scatter.6
  680.7 82.1 reduce-scatter.8
  770.5 91.7 reduce-scatter.10

commit v2 on v1

--- a/solution.py
+++ b/solution.py
@@ -4,6 +4,7 @@
 import jax
 import jax.numpy as jnp
 from jax import lax
+from jax.experimental import pallas as pl
 from jax.sharding import PartitionSpec as P
 
 D = 2048
@@ -138,7 +139,10 @@
 
 
 def advance(*jobs, beside=()):
-    arrived, beside = lax.optimization_barrier(([job.start() for job in jobs], beside))
+    arrived = [job.start() for job in jobs]
+    if callable(beside):
+        beside = beside(arrived[-1])
+    arrived, beside = lax.optimization_barrier((arrived, beside))
     for job, other in zip(jobs, arrived):
         job.finish(other)
     return arrived, beside
@@ -146,6 +150,34 @@
 
 def tie(values, *others):
     return lax.optimization_barrier((values, others))[0]
+
+
+def pair_units(gate_sum, up_sum):
+    units = gate_sum.shape[0]
+    block = min(64, units)
+
+    def kernel(gate_ref, up_ref, weight_ref, expand_ref):
+        for k, ref in enumerate((gate_ref, up_ref)):
+            terms = ref[...].astype(jnp.float32)
+            weight_ref[:, k, :] = terms[:, :D]
+            expand_ref[:, k, :] = terms[:, D:]
+
+    return pl.pallas_call(
+        kernel,
+        grid=(units // block,),
+        in_specs=[pl.BlockSpec((block, D + R), lambda i: (i, 0))] * 2,
+        out_specs=[
+            pl.BlockSpec((block, 2, D), lambda i: (i, 0, 0)),
+            pl.BlockSpec((block, 2, R), lambda i: (i, 0, 0)),
+        ],
+        out_shape=[
+            jax.ShapeDtypeStruct((units, 2, D), jnp.float32),
+            jax.ShapeDtypeStruct((units, 2, R), jnp.float32),
+        ],
+        cost_estimate=pl.CostEstimate(
+            flops=0, transcendentals=0, bytes_accessed=12 * units * (D + R)
+        ),
+    )(gate_sum, up_sum)
 
 
 def body(
@@ -377,10 +409,10 @@
         product_rows(hidden_late, back_joined).astype(bf16),
         product_rows(gate_late, rows_joined).astype(bf16),
     )
-    arrived, (down_terms, gate_terms) = advance(*jobs, beside=work)
+    arrived, (down_terms, gate_terms, mixed) = advance(*jobs, beside=(*work, mixed))
+    down_sum = scatter_units(tie(down_terms, mixed))
     up_terms = product_rows(tie(grad_up, arrived), rows_joined).astype(bf16)
-    _, (up_terms, mixed) = advance(*jobs, beside=(up_terms, mixed))
-    down_sum = scatter_units(tie(down_terms, mixed))
+    _, up_terms = advance(*jobs, beside=up_terms)
     mixed = mixed.astype(f32)
     for _ in range(len(highs) - 1):
         advance(*jobs)
@@ -427,34 +459,46 @@
     )
     _, grad_attn = advance(*out_jobs, beside=grad_attn)
 
-    grad_queries, grad_keys, grad_values = [], 0.0, 0.0
+    scores_back, grad_keys, grad_values = [], 0.0, 0.0
     for i, query_rows in enumerate(query_parts):
         grad_rows = grad_attn[i * piece_rows : (i + 1) * piece_rows]
         shares = kept[i] if kept else shares_of(tie(query_rows, grad_rows))
         delta = jnp.sum(grad_rows.astype(f32) * attended_parts[i], axis=-1, keepdims=True)
         grad_shares = product_back(grad_rows, values_all)
         grad_scores = (shares * (grad_shares - delta)).astype(bf16)
-        grad_queries.append(product(grad_scores, keys_all) * score_scale)
+        scores_back.append(grad_scores)
         grad_keys = grad_keys + product_rows(grad_scores, query_rows) * score_scale
         grad_values = grad_values + product_rows(shares.astype(bf16), grad_rows)
-    grad_query = jnp.concatenate(grad_queries, axis=0)
-    turned = rotate(grad_query.reshape(H, tokens, DH), cosine, -sine_part).astype(bf16)
-    joined_q_grad = to_rows(turned.reshape(H * tokens, DH))
-    query_jobs = [
-        scatter_weights(product_rows(normed_one, rows), order)
-        for rows, order in zip(
-            (joined_q_grad[:, :half], joined_q_grad[:, half:]), (backs[0], backs[2])
-        )
-    ]
-    _, (grad_keys, grad_values) = advance(
-        *out_jobs, beside=(grad_keys.astype(bf16), grad_values.astype(bf16))
-    )
+    _, (grad_keys, grad_values, down_sum) = advance(
+        *out_jobs, beside=(grad_keys.astype(bf16), grad_values.astype(bf16), down_sum)
+    )
+    gate_sum = scatter_units(tie(gate_terms, down_sum))
     kv_jobs = [
         Scatter(grad_keys, ("head", low) + upper + mid, row_axes),
         Scatter(grad_values, mid + (low,) + upper + ("head",), row_axes),
     ]
-    _, down_sum = advance(*kv_jobs, *out_jobs, beside=down_sum)
-    gate_sum = scatter_units(tie(gate_terms, down_sum))
+
+    def query_back(seen):
+        parts, lowrank, rows = tie((scores_back, lowrank_two, grad_branch), seen)
+        grad_query = jnp.concatenate([product(part, keys_all) for part in parts], axis=0)
+        turned = rotate(
+            grad_query.reshape(H, tokens, DH) * score_scale, cosine, -sine_part
+        ).astype(bf16)
+        joined = to_rows(turned.reshape(H * tokens, DH))
+        return (
+            joined,
+            product_rows(normed_one, joined[:, :half]).astype(bf16),
+            product_rows(normed_one, joined[:, half:]).astype(bf16),
+            product_rows(lowrank, rows).astype(bf16),
+        )
+
+    _, (joined_q_grad, *query_terms, out_expand_terms) = advance(
+        *kv_jobs, *out_jobs, beside=query_back
+    )
+    query_jobs = [
+        scatter_weights(terms, order)
+        for terms, order in zip(query_terms, (backs[0], backs[2]))
+    ]
     for _ in range(steps - 2):
         advance(*kv_jobs, *out_jobs)
     advance(*kv_jobs, *query_jobs)
@@ -477,7 +521,7 @@
         jnp.concatenate(
             [
                 product_rows(lowrank_one, grad_joined).astype(bf16),
-                product_rows(lowrank_two, grad_branch).astype(bf16),
+                out_expand_terms,
                 expand_down.astype(bf16),
                 gain_one_grad.reshape(R, -1).astype(bf16),
                 gain_two_grad.reshape(R, -1).astype(bf16),
@@ -491,15 +535,10 @@
     last_jobs = [scatter_weights(terms, order) for terms, order in zip(last, (backs[0], backs[2]))]
     for _ in range(steps - 1):
         arrived, _ = advance(*query_jobs, *last_jobs)
-    sums = [value.astype(f32) for value in tie((down_sum, gate_sum, up_sum), arrived)]
-    weights_grad = (
-        sums[0][:, :D],
-        sums[0][:, D:],
-        jnp.stack([sums[1][:, :D], sums[2][:, :D]], axis=1),
-        jnp.stack([sums[1][:, D:], sums[2][:, D:]], axis=1),
-    )
-    _, weights_grad = advance(*last_jobs, beside=weights_grad)
-    downweight_grad, downadapt_grad, gateweight_grad, gateexpand_grad = weights_grad
+    arrived, _ = advance(*last_jobs)
+    down_sum, gate_sum, up_sum = tie((down_sum, gate_sum, up_sum), arrived)
+    downweight_grad, downadapt_grad = down_sum[:, :D].astype(f32), down_sum[:, D:].astype(f32)
+    gateweight_grad, gateexpand_grad = pair_units(gate_sum, up_sum)
     advance(*last_jobs)
     kv_grad, expand_grad = last_jobs[0].result(), last_jobs[1].result()
     gains_grad = expand_grad[:, qkv_columns + 2 * D :]

time: 911 us -> 886 us (0.973)
  local copies, waits for them, and re-layouts: 104 us -> 73.2 us
    ppermute x94, waiting for transfers between devices: 338 us -> 364 us  [shift(): return lax.ppermute(values, axes, [(i, i ^ mask) for i in range(size)])]
    reduce_scatter x3, waiting for transfers between devices: 23.5 us -> 6.14 us  [scatter_units(): return lax.psum_scatter(terms, unit_axes, scatter_dimension=0, tiled=True)]
    unnamed x366 -> x354, local copies, waits for them, and re-layouts: 54.2 us -> 37.8 us
  transfers between devices with their start and end apart: 102 -> 102, of which waited for: 47 -> 51; matrix products, arithmetic and copies ran while one was open for 41% -> 39% of each run, Pallas kernels for 0% -> 0%
where the time goes in v2:
time: 886 us; the launch traced here: 880 us
  waiting for transfers between devices  371 us (42%)
  matrix products  201 us (23%)
  other arithmetic  106 us (12%)
  starting transfers between devices  102 us (12%)
  local copies, waits for them, and re-layouts  73.2 us (8%)
  between operations  17.7 us (2%)
    ppermute x94, waiting for transfers between devices, shift(): return lax.ppermute(values, axes, [(i, i ^ mask) for i in range(size)])  364 us
    ppermute x94, starting transfers between devices, shift(): return lax.ppermute(values, axes, [(i, i ^ mask) for i in range(size)])  101 us
    dot_general x16, matrix products, product_back(): lax.dot_general(former, latter, (((1,), (1,)), ((), ())), preferred_eleme...  77 us
    dot_general x14, matrix products, product_rows(): lax.dot_general(former, latter, (((0,), (0,)), ((), ())), preferred_eleme...  62.6 us
    dot_general x17, matrix products, product(): return jnp.dot(former, latter, preferred_element_type=jnp.float32)  61.6 us
    another operation x75, other arithmetic, place(): jnp.stack([jnp.where(first, own, other), jnp.where(first, other, own)], a...  51.7 us
    unnamed x354, local copies, waits for them, and re-layouts  37.8 us
    convert_element_type x38, other arithmetic, finish(): self.value = self.value.astype(jnp.bfloat16)  23.1 us
  transfers between devices with their start and end apart: 102, of which 51 were waited for; matrix products, arithmetic and copies ran while one was open for 39% of the time, Pallas kernels for 0%

profile of v2, /device:TPU:0, one launch (start us, length us, event | category | flops | bytes accessed | tf_op | source)
XLA Modules:
  0.0 879.6 jit_solution(12714020465255700257)
XLA Ops:
  7.3 3.4 pad_maximum_fusion.14
  10.8 4.1 collective-permute-start.2
  18.9 4.3 collective-permute-done
  23.3 4.9 copy.56
  35.7 6.0 collective-permute-done.4
  43.1 10.4 %collective-permute-done.6 = bf16[2,64,1024]{2,1,0:T(8,128)(2,1)S(1)} collective-permute-done((bf16[2,64,1024]{2,1,0:T(8,128)(2,1)S(1)}, bf16[2,64,1024]{2,1,0:T(8,128)(2,1)S(1)}, u32[]{:S(2)}, u32[]{:S(2)}) %collective-permute-start.6) | collective-permute-done | bytes 262176 | tf_op jit(solution)/shard_map/ppermute | solution.py:72
  61.8 16.4 %collective-permute-done.8 = bf16[2,2,64,768]{3,2,1,0:T(8,128)(2,1)} collective-permute-done((bf16[2,2,64,768]{3,2,1,0:T(8,128)(2,1)}, bf16[2,2,64,768]{3,2,1,0:T(8,128)(2,1)}, u32[]{:S(2)}, u32[]{:S(2)}) %collective-permute-start.8) | collective-permute-done | bytes 393248 | tf_op jit(solution)/shard_map/ppermute | solution.py:72
  93.6 35.0 %collective-permute-done.12 = bf16[2,2,2,64,768]{4,3,2,1,0:T(8,128)(2,1)} collective-permute-done((bf16[2,2,2,64,768]{4,3,2,1,0:T(8,128)(2,1)}, bf16[2,2,2,64,768]{4,3,2,1,0:T(8,128)(2,1)}, u32[]{:S(2)}, u32[]{:S(2)}) %collective-permute-start.12) | collective-permute-done | bytes 786464 | tf_op jit(solution)/shard_map/ppermute | solution.py:72
  181.6 9.8 %collective-permute-done.25 = bf16[2,128,256]{2,1,0:T(8,128)(2,1)S(1)} collective-permute-done((bf16[2,128,256]{2,1,0:T(8,128)(2,1)S(1)}, bf16[2,128,256]{2,1,0:T(8,128)(2,1)S(1)}, u32[]{:S(2)}, u32[]{:S(2)}) %collective-permute-start.25) | collective-permute-done | bytes 131104 | tf_op jit(solution)/shard_map/ppermute | solution.py:72
  199.1 15.2 %collective-permute-done.29 = bf16[2,2,128,256]{3,2,1,0:T(8,128)(2,1)S(1)} collective-permute-done((bf16[2,2,128,256]{3,2,1,0:T(8,128)(2,1)S(1)}, bf16[2,2,128,256]{3,2,1,0:T(8,128)(2,1)S(1)}, u32[]{:S(2)}, u32[]{:S(2)}) %collective-permute-start.29) | collective-permute-done | bytes 262176 | tf_op jit(solution)/shard_map/ppermute | solution.py:72
  226.1 33.4 %collective-permute-done.33 = bf16[2,2,2,128,256]{4,3,2,0,1:T(8,128)(2,1)} collective-permute-done((bf16[2,2,2,128,256]{4,3,2,0,1:T(8,128)(2,1)}, bf16[2,2,2,128,256]{4,3,2,0,1:T(8,128)(2,1)}, u32[]{:S(2)}, u32[]{:S(2)}) %collective-permute-start.33) | collective-permute-done | bytes 524320 | tf_op jit(solution)/shard_map/ppermute | solution.py:72
  273.7 3.6 fusion.8
  300.7 19.5 %collective-permute-done.38 = bf16[128,2048]{1,0:T(8,128)(2,1)S(1)} collective-permute-done((bf16[128,2048]{1,0:T(8,128)(2,1)S(1)}, bf16[128,2048]{1,0:T(8,128)(2,1)S(1)}, u32[]{:S(2)}, u32[]{:S(2)}) %collective-permute-start.38) | collective-permute-done | bytes 524320 | tf_op jit(solution)/shard_map/ppermute | solution.py:72
  320.2 15.7 %collective-permute-done.39 = bf16[128,2048]{1,0:T(8,128)(2,1)S(1)} collective-permute-done((bf16[128,2048]{1,0:T(8,128)(2,1)S(1)}, bf16[128,2048]{1,0:T(8,128)(2,1)S(1)}, u32[]{:S(2)}, u32[]{:S(2)}) %collective-permute-start.39) | collective-permute-done | bytes 524320 | tf_op jit(solution)/shard_map/ppermute | solution.py:72
  341.9 9.0 %collective-permute-done.42 = bf16[128,2048]{1,0:T(8,128)(2,1)S(1)} collective-permute-done((bf16[128,2048]{1,0:T(8,128)(2,1)S(1)}, bf16[128,2048]{1,0:T(8,128)(2,1)S(1)}, u32[]{:S(2)}, u32[]{:S(2)}) %collective-permute-start.42) | collective-permute-done | bytes 524320 | tf_op jit(solution)/shard_map/ppermute | solution.py:72
  351.7 16.0 %collective-permute-done.43 = bf16[128,2048]{1,0:T(8,128)(2,1)S(1)} collective-permute-done((bf16[128,2048]{1,0:T(8,128)(2,1)S(1)}, bf16[128,2048]{1,0:T(8,128)(2,1)S(1)}, u32[]{:S(2)}, u32[]{:S(2)}) %collective-permute-start.43) | collective-permute-done | bytes 524320 | tf_op jit(solution)/shard_map/ppermute | solution.py:72
  368.6 6.8 collective-permute-done.44
  376.2 3.9 convolution_convert_fusion.15
  380.1 15.0 %fusion.192 = f32[1024,2048]{1,0:T(8,128)} fusion(bf16[2048,2304]{1,0:T(8,128)(2,1)} %all-gather.7.cloned.1.call-done, bf16[1024,256]{1,0:T(8,128)(2,1)S(1)} %convolution_convert_fusion.15, bf16[1024,2048]{1,0:T(8,128)(2,1)S(1)} %copy-done.119), kind=kOutput, calls=%fused_computation.589 | convolution fusion | flops 9673113600 | bytes 22544384 | tf_op jit(solution)/shard_map/dot_general | solution.py:25
  395.1 19.3 %multiply_convert_fusion.2 = (bf16[1024,2048]{1,0:T(8,128)(2,1)}, f32[1024,2048]{1,0:T(8,128)}) fusion(f32[1024,2048]{1,0:T(8,128)} %fusion.192, bf16[2048,2304]{1,0:T(8,128)(2,1)} %all-gather.9.cloned.1.call-done, bf16[1024,256]{1,0:T(8,128)(2,1)S(1)} %convolution_convert_fusion.15, bf16[1024,2048]{1,0:T(8,128)(2,1)} %constant_dynamic-update-slice_fusion.8), kind=kOutput, calls=%fused_computation.17 | convolution fusion | flops 9694085120 | bytes 35127296 | tf_op jit(solution)/shard_map/dot_general | solution.py:25
  414.4 13.4 %convolution_convert_fusion.4 = bf16[1024,2304]{1,0:T(8,128)(2,1)S(1)} fusion(bf16[1024,2048]{1,0:T(8,128)(2,1)} %get-tuple-element.196, bf16[2048,2304]{1,0:T(8,128)(2,1)} %all-gather.5.cloned.1.call-done), kind=kOutput, calls=%fused_computation.23 | convolution fusion | flops 9666035712 | bytes 18350080 | tf_op jit(solution)/shard_map/dot_general | solution.py:21
  444.9 22.7 %fusion.6 = (bf16[1024,2048]{1,0:T(8,128)(2,1)}, bf16[1024,2048]{1,0:T(8,128)(2,1)}) fusion(f32[1024,2048]{1,0:T(8,128)} %fusion.192, f32[1024,2048]{1,0:T(8,128)} %get-tuple-element.439, bf16[2048,2304]{1,0:T(8,128)(2,1)} %all-gather.5.cloned.1.call-done, bf16[1024,256]{1,0:T(8,128)(2,1)S(1)} %copy.80, bf16[1024,2048]{1,0:T(8,128)(2,1)} %copy-done.122), kind=kOutput, calls=%fused_computation.14 | convolution fusion | flops 9723445248 | bytes 39321600 | tf_op jit(solution)/shard_map/dot_general | solution.py:25
  467.5 13.7 %fusion.218 = f32[1024,2304]{1,0:T(8,128)S(1)} fusion(bf16[1024,2048]{1,0:T(8,128)(2,1)} %get-tuple-element.202, bf16[2048,2304]{1,0:T(8,128)(2,1)} %all-gather.9.cloned.1.call-done), kind=kOutput, calls=%fused_computation.600 | convolution fusion | flops 9663676416 | bytes 23068672 | tf_op jit(solution)/shard_map/dot_general | solution.py:21
  481.2 12.2 %add_convert_fusion = bf16[1024,2304]{1,0:T(8,128)(2,1)S(1)} fusion(f32[1024,2304]{1,0:T(8,128)S(1)} %fusion.218, bf16[1024,2048]{1,0:T(8,128)(2,1)S(1)} %copy-done.147, bf16[2048,2304]{1,0:T(8,128)(2,1)} %all-gather.7.cloned.1.call-done), kind=kOutput, calls=%fused_computation.7 | convolution fusion | flops 9668395008 | bytes 27787264 | tf_op jit(solution)/shard_map/dot_general | solution.py:21
  495.0 17.6 %collective-permute-start.46 = (bf16[2,2,128,1152]{3,2,0,1:T(8,128)(2,1)}, bf16[2,2,128,1152]{3,2,0,1:T(8,128)(2,1)S(1)}, u32[]{:S(2)}, u32[]{:S(2)}) collective-permute-start(bf16[2,2,128,1152]{3,2,0,1:T(8,128)(2,1)} %bitcast.611), channel_id=1, source_target_pairs={{0,2},{2,0},{1,3},{3,1},{4,6},{6,4},{5,7},{7,5},{8,10},{10,8},{9,1... | collective-permute-start | bytes 3538952 | tf_op jit(solution)/shard_map/ppermute | solution.py:72
  514.4 13.0 %convolution_convert_fusion.1 = bf16[2048,2304]{1,0:T(8,128)(2,1)} fusion(bf16[1024,2048]{1,0:T(8,128)(2,1)S(1)} %copy-done.148, bf16[1024,256]{1,0:T(8,128)(2,1)S(1)} %copy-done.145, bf16[1024,2048]{1,0:T(8,128)(2,1)S(1)} %copy-done.120), kind=kOutput, calls=%fused_computation.5 | convolution fusion | flops 9677832192 | bytes 18350080 | tf_op jit(solution)/shard_map/dot_general | solution.py:31
  527.5 15.4 %convolution_convert_fusion.2 = bf16[2048,2304]{1,0:T(8,128)(2,1)} fusion(bf16[1024,2048]{1,0:T(8,128)(2,1)} %get-tuple-element.196, bf16[1024,256]{1,0:T(8,128)(2,1)} %copy-done.92, bf16[1024,2048]{1,0:T(8,128)(2,1)} %copy-done.122), kind=kOutput, calls=%fused_computation.6 | convolution fusion | flops 9677832192 | bytes 18350080 | tf_op jit(solution)/shard_map/dot_general | solution.py:31
  542.9 9.5 %collective-permute-done.46 = bf16[2,2,128,1152]{3,2,0,1:T(8,128)(2,1)S(1)} collective-permute-done((bf16[2,2,128,1152]{3,2,0,1:T(8,128)(2,1)}, bf16[2,2,128,1152]{3,2,0,1:T(8,128)(2,1)S(1)}, u32[]{:S(2)}, u32[]{:S(2)}) %collective-permute-start.46) | collective-permute-done | bytes 1179680 | tf_op jit(solution)/shard_map/ppermute | solution.py:72
  560.2 13.2 %convolution_convert_fusion = bf16[2048,2304]{1,0:T(8,128)(2,1)} fusion(bf16[1024,2048]{1,0:T(8,128)(2,1)S(1)} %copy-done.149, bf16[1024,256]{1,0:T(8,128)(2,1)S(1)} %copy-done.146, bf16[1024,2048]{1,0:T(8,128)(2,1)S(1)} %copy-done.121), kind=kOutput, calls=%fused_computation.4 | convolution fusion | flops 9677832192 | bytes 18350080 | tf_op jit(solution)/shard_map/dot_general | solution.py:31
  573.4 11.5 %collective-permute-done.48 = bf16[2,128,1152]{2,1,0:T(8,128)(2,1)} collective-permute-done((bf16[2,128,1152]{2,1,0:T(8,128)(2,1)}, bf16[2,128,1152]{2,1,0:T(8,128)(2,1)}, u32[]{:S(2)}, u32[]{:S(2)}) %collective-permute-start.48) | collective-permute-done | bytes 589856 | tf_op jit(solution)/shard_map/ppermute | solution.py:72
  590.4 3.7 collective-permute-done.50
  594.1 8.8 %collective-permute-done.49 = bf16[128,1152]{1,0:T(8,128)(2,1)S(1)} collective-permute-done((bf16[128,1152]{1,0:T(8,128)(2,1)S(1)}, bf16[128,1152]{1,0:T(8,128)(2,1)S(1)}, u32[]{:S(2)}, u32[]{:S(2)}) %collective-permute-start.49) | collective-permute-done | bytes 294944 | tf_op jit(solution)/shard_map/ppermute | solution.py:72
  636.3 19.3 %collective-permute-done.55 = bf16[2,2,2,64,1024]{4,3,1,0,2:T(8,128)(2,1)S(1)} collective-permute-done((bf16[2,2,2,64,1024]{4,3,1,0,2:T(8,128)(2,1)S(1)}, bf16[2,2,2,64,1024]{4,3,1,0,2:T(8,128)(2,1)S(1)}, u32[]{:S(2)}, u32[]{:S(2)}) %collective-permute-start.55) | collective-permute-done | bytes 1048608 | tf_op jit(solution)/shard_map/ppermute | solution.py:72
  681.4 10.6 %collective-permute-done.58 = bf16[2,2,2,128,256]{4,3,0,1,2:T(8,128)(2,1)S(1)} collective-permute-done((bf16[2,2,2,128,256]{4,3,0,1,2:T(8,128)(2,1)S(1)}, bf16[2,2,2,128,256]{4,3,0,1,2:T(8,128)(2,1)S(1)}, u32[]{:S(2)}, u32[]{:S(2)}) %collective-permute-start.58) | collective-permute-done | bytes 524320 | tf_op jit(solution)/shard_map/ppermute | solution.py:72
  700.1 9.2 %collective-permute-done.65 = bf16[2,64,1024]{2,1,0:T(8,128)(2,1)S(1)} collective-permute-done((bf16[2,64,1024]{2,1,0:T(8,128)(2,1)S(1)}, bf16[2,64,1024]{2,1,0:T(8,128)(2,1)S(1)}, u32[]{:S(2)}, u32[]{:S(2)}) %collective-permute-start.65) | collective-permute-done | bytes 262176 | tf_op jit(solution)/shard_map/ppermute | solution.py:72
  717.1 7.9 collective-permute-done.70
  726.6 4.1 collective-permute-done.68
  735.2 3.7 collective-permute-done.73
  754.1 6.6 concatenate.134
  760.7 3.6 convolution_convert_fusion.9
  778.1 9.8 %collective-permute-done.79 = bf16[2,2,64,1024]{3,2,1,0:T(8,128)(2,1)S(1)} collective-permute-done((bf16[2,2,64,1024]{3,2,1,0:T(8,128)(2,1)S(1)}, bf16[2,2,64,1024]{3,2,1,0:T(8,128)(2,1)S(1)}, u32[]{:S(2)}, u32[]{:S(2)}) %collective-permute-start.79) | collective-permute-done | bytes 524320 | tf_op jit(solution)/shard_map/ppermute | solution.py:72
  796.5 12.3 %collective-permute-done.83 = bf16[2,64,1024]{2,1,0:T(8,128)(2,1)S(1)} collective-permute-done((bf16[2,64,1024]{2,1,0:T(8,128)(2,1)S(1)}, bf16[2,64,1024]{2,1,0:T(8,128)(2,1)S(1)}, u32[]{:S(2)}, u32[]{:S(2)}) %collective-permute-start.83) | collective-permute-done | bytes 262176 | tf_op jit(solution)/shard_map/ppermute | solution.py:72
  808.8 7.3 collective-permute-done.82
  822.5 6.2 collective-permute-done.87
  832.8 8.4 collective-permute-done.90
  844.4 6.3 collective-permute-done.92
  854.8 6.1 reduce-scatter.11.cloned.1.call-done.up_ref
  864.3 8.2 shard_map.287
  (833 shorter events, 326.0 us)
Async XLA Ops:
  7.3 121.4 %all-gather.5.cloned.1.call-start = ((), (), s32[]{:S(2)}) async-start(), calls=%async_computation.4 | async-start | bytes 11796480 | tf_op jit(solution)/shard_map/all_gather | solution.py:250
  10.7 163.5 %all-gather.7.cloned.1.call-start = ((), (), s32[]{:S(2)}) async-start(), calls=%async_computation.5 | async-start | bytes 11796480 | tf_op jit(solution)/shard_map/all_gather | solution.py:250
  29.7 23.9 %collective-permute-start.6 = (bf16[2,64,1024]{2,1,0:T(8,128)(2,1)S(1)}, bf16[2,64,1024]{2,1,0:T(8,128)(2,1)S(1)}, u32[]{:S(2)}, u32[]{:S(2)}) collective-permute-start(bf16[2,64,1024]{2,1,0:T(8,128)(2,1)S(1)} %pad_maximum_fusion.42), channel_id=1, source_target_pairs={{0,8},{8,0},{1,9},{9,1},{2,10},{10,2},{3,11},{11,3},{4,12},{12,4},... | collective-permute-start | bytes 786440 | tf_op jit(solution)/shard_map/ppermute | solution.py:72
  54.5 24.1 %collective-permute-start.11 = (bf16[2,2,64,1024]{3,2,1,0:T(8,128)(2,1)}, bf16[2,2,64,1024]{3,2,1,0:T(8,128)(2,1)S(1)}, u32[]{:S(2)}, u32[]{:S(2)}) collective-permute-start(bf16[2,2,64,1024]{3,2,1,0:T(8,128)(2,1)} %pad_maximum_fusion.33), channel_id=1, source_target_pairs={{0,4},{4,0},{1,5},{5,1},{2,6},{6,2},{3,7},{7,3},{8,12},{12,8},{9,1... | collective-permute-start | bytes 1572872 | tf_op jit(solution)/shard_map/ppermute | solution.py:72
  54.7 24.6 %collective-permute-start.10 = (bf16[2,2,64,1024]{3,2,1,0:T(8,128)(2,1)S(1)}, bf16[2,2,64,1024]{3,2,1,0:T(8,128)(2,1)}, u32[]{:S(2)}, u32[]{:S(2)}) collective-permute-start(bf16[2,2,64,1024]{3,2,1,0:T(8,128)(2,1)S(1)} %pad_maximum_fusion.32), channel_id=1, source_target_pairs={{0,2},{2,0},{1,3},{3,1},{4,6},{6,4},{5,7},{7,5},{8,10},{10,8},{9,1... | collective-permute-start | bytes 1572872 | tf_op jit(solution)/shard_map/ppermute | solution.py:72
  58.9 19.3 %collective-permute-start.9 = (bf16[2,2,8,6784]{3,2,1,0:T(8,128)(2,1)}, bf16[2,2,8,6784]{3,2,1,0:T(8,128)(2,1)}, u32[]{:S(2)}, u32[]{:S(2)}) collective-permute-start(bf16[2,2,8,6784]{3,2,1,0:T(8,128)(2,1)} %pad_maximum_fusion.38), channel_id=1, source_target_pairs={{0,1},{1,0},{2,3},{3,2},{4,5},{5,4},{6,7},{7,6},{8,9},{9,8},{10,11... | collective-permute-start | bytes 1302536 | tf_op jit(solution)/shard_map/ppermute | solution.py:72
  81.5 47.1 %collective-permute-start.15 = (bf16[2,2,2,64,1024]{4,3,2,1,0:T(8,128)(2,1)}, bf16[2,2,2,64,1024]{4,3,2,1,0:T(8,128)(2,1)}, u32[]{:S(2)}, u32[]{:S(2)}) collective-permute-start(bf16[2,2,2,64,1024]{4,3,2,1,0:T(8,128)(2,1)} %pad_maximum_fusion.23), channel_id=1, source_target_pairs={{0,1},{1,0},{2,3},{3,2},{4,5},{5,4},{6,7},{7,6},{8,9},{9,8},{10,11... | collective-permute-start | bytes 3145736 | tf_op jit(solution)/shard_map/ppermute | solution.py:72
  85.5 43.2 %collective-permute-start.14 = (bf16[2,2,2,64,1024]{4,3,2,1,0:T(8,128)(2,1)}, bf16[2,2,2,64,1024]{4,3,2,1,0:T(8,128)(2,1)}, u32[]{:S(2)}, u32[]{:S(2)}) collective-permute-start(bf16[2,2,2,64,1024]{4,3,2,1,0:T(8,128)(2,1)} %pad_maximum_fusion.22), channel_id=1, source_target_pairs={{0,1},{1,0},{2,3},{3,2},{4,5},{5,4},{6,7},{7,6},{8,9},{9,8},{10,11... | collective-permute-start | bytes 3145736 | tf_op jit(solution)/shard_map/ppermute | solution.py:72
  88.3 40.3 %collective-permute-start.13 = (bf16[2,2,2,8,6784]{4,3,2,1,0:T(8,128)(2,1)}, bf16[2,2,2,8,6784]{4,3,2,1,0:T(8,128)(2,1)}, u32[]{:S(2)}, u32[]{:S(2)}) collective-permute-start(bf16[2,2,2,8,6784]{4,3,2,1,0:T(8,128)(2,1)} %pad_maximum_fusion.26), channel_id=1, source_target_pairs={{0,4},{4,0},{1,5},{5,1},{2,6},{6,2},{3,7},{7,3},{8,12},{12,8},{9,1... | collective-permute-start | bytes 2605064 | tf_op jit(solution)/shard_map/ppermute | solution.py:72
  91.5 37.1 %collective-permute-start.12 = (bf16[2,2,2,64,768]{4,3,2,1,0:T(8,128)(2,1)}, bf16[2,2,2,64,768]{4,3,2,1,0:T(8,128)(2,1)}, u32[]{:S(2)}, u32[]{:S(2)}) collective-permute-start(bf16[2,2,2,64,768]{4,3,2,1,0:T(8,128)(2,1)} %pad_maximum_fusion.27), channel_id=1, source_target_pairs={{0,2},{2,0},{1,3},{3,1},{4,6},{6,4},{5,7},{7,5},{8,10},{10,8},{9,1... | collective-permute-start | bytes 2359304 | tf_op jit(solution)/shard_map/ppermute | solution.py:72
  93.3 168.7 %all-gather.9.cloned.1.call-start = ((), (), s32[]{:S(2)}) async-start(), calls=%async_computation.6 | async-start | bytes 11796480 | tf_op jit(solution)/shard_map/all_gather | solution.py:250
  143.6 30.6 %collective-permute-start.22 = (bf16[64,1280]{1,0:T(8,128)(2,1)}, bf16[64,1280]{1,0:T(8,128)(2,1)}, u32[]{:S(2)}, u32[]{:S(2)}) collective-permute-start(bf16[64,1280]{1,0:T(8,128)(2,1)} %pad_maximum_fusion.48), channel_id=1, source_target_pairs={{0,8},{8,0},{1,9},{9,1},{2,10},{10,2},{3,11},{11,3},{4,12},{12,4},... | collective-permute-start | bytes 491528 | tf_op jit(solution)/shard_map/ppermute | solution.py:72
  146.9 27.3 %collective-permute-start.23 = (bf16[64,1280]{1,0:T(8,128)(2,1)}, bf16[64,1280]{1,0:T(8,128)(2,1)}, u32[]{:S(2)}, u32[]{:S(2)}) collective-permute-start(bf16[64,1280]{1,0:T(8,128)(2,1)} %pad_maximum_fusion.49), channel_id=1, source_target_pairs={{0,4},{4,0},{1,5},{5,1},{2,6},{6,2},{3,7},{7,3},{8,12},{12,8},{9,1... | collective-permute-start | bytes 491528 | tf_op jit(solution)/shard_map/ppermute | solution.py:72
  174.2 260.5 %all-gather.11.cloned.1.call-start = ((), (), s32[]{:S(2)}) async-start(), calls=%async_computation.7 | async-start | bytes 4718592 | tf_op jit(solution)/shard_map/all_gather | solution.py:379
  194.1 22.5 %collective-permute-start.31 = (bf16[2,2,64,1280]{3,2,1,0:T(8,128)(2,1)S(1)}, bf16[2,2,64,1280]{3,2,1,0:T(8,128)(2,1)S(1)}, u32[]{:S(2)}, u32[]{:S(2)}) collective-permute-start(bf16[2,2,64,1280]{3,2,1,0:T(8,128)(2,1)S(1)} %pad_maximum_fusion.29), channel_id=1, source_target_pairs={{0,2},{2,0},{1,3},{3,1},{4,6},{6,4},{5,7},{7,5},{8,10},{10,8},{9,1... | collective-permute-start | bytes 1966088 | tf_op jit(solution)/shard_map/ppermute | solution.py:72
  194.3 22.3 %collective-permute-start.30 = (bf16[2,2,64,1280]{3,2,1,0:T(8,128)(2,1)S(1)}, bf16[2,2,64,1280]{3,2,1,0:T(8,128)(2,1)S(1)}, u32[]{:S(2)}, u32[]{:S(2)}) collective-permute-start(bf16[2,2,64,1280]{3,2,1,0:T(8,128)(2,1)S(1)} %pad_maximum_fusion.28), channel_id=1, source_target_pairs={{0,1},{1,0},{2,3},{3,2},{4,5},{5,4},{6,7},{7,6},{8,9},{9,8},{10,11... | collective-permute-start | bytes 1966088 | tf_op jit(solution)/shard_map/ppermute | solution.py:72
  218.0 42.9 %collective-permute-start.35 = (bf16[2,2,2,64,1280]{4,3,2,1,0:T(8,128)(2,1)}, bf16[2,2,2,64,1280]{4,3,2,1,0:T(8,128)(2,1)}, u32[]{:S(2)}, u32[]{:S(2)}) collective-permute-start(bf16[2,2,2,64,1280]{4,3,2,1,0:T(8,128)(2,1)} %pad_maximum_fusion.20), channel_id=1, source_target_pairs={{0,1},{1,0},{2,3},{3,2},{4,5},{5,4},{6,7},{7,6},{8,9},{9,8},{10,11... | collective-permute-start | bytes 3932168 | tf_op jit(solution)/shard_map/ppermute | solution.py:72
  220.7 41.2 %collective-permute-start.34 = (bf16[2,2,2,64,1280]{4,3,2,1,0:T(8,128)(2,1)}, bf16[2,2,2,64,1280]{4,3,2,1,0:T(8,128)(2,1)}, u32[]{:S(2)}, u32[]{:S(2)}) collective-permute-start(bf16[2,2,2,64,1280]{4,3,2,1,0:T(8,128)(2,1)} %pad_maximum_fusion.19), channel_id=1, source_target_pairs={{0,2},{2,0},{1,3},{3,1},{4,6},{6,4},{5,7},{7,5},{8,10},{10,8},{9,1... | collective-permute-start | bytes 3932168 | tf_op jit(solution)/shard_map/ppermute | solution.py:72
  223.5 36.0 %collective-permute-start.33 = (bf16[2,2,2,128,256]{4,3,2,0,1:T(8,128)(2,1)}, bf16[2,2,2,128,256]{4,3,2,0,1:T(8,128)(2,1)}, u32[]{:S(2)}, u32[]{:S(2)}) collective-permute-start(bf16[2,2,2,128,256]{4,3,2,0,1:T(8,128)(2,1)} %pad_maximum_fusion.36), channel_id=1, source_target_pairs={{0,1},{1,0},{2,3},{3,2},{4,5},{5,4},{6,7},{7,6},{8,9},{9,8},{10,11... | collective-permute-start | bytes 1572872 | tf_op jit(solution)/shard_map/ppermute | solution.py:72
  225.0 35.9 %collective-permute-start.32 = (bf16[2,2,2,128,256]{4,3,0,1,2:T(8,128)(2,1)}, bf16[2,2,2,128,256]{4,3,0,1,2:T(8,128)(2,1)}, u32[]{:S(2)}, u32[]{:S(2)}) collective-permute-start(bf16[2,2,2,128,256]{4,3,0,1,2:T(8,128)(2,1)} %pad_maximum_fusion.35), channel_id=1, source_target_pairs={{0,4},{4,0},{1,5},{5,1},{2,6},{6,2},{3,7},{7,3},{8,12},{12,8},{9,1... | collective-permute-start | bytes 1572872 | tf_op jit(solution)/shard_map/ppermute | solution.py:72
  295.8 24.4 %collective-permute-start.38 = (bf16[128,2048]{1,0:T(8,128)(2,1)S(1)}, bf16[128,2048]{1,0:T(8,128)(2,1)S(1)}, u32[]{:S(2)}, u32[]{:S(2)}) collective-permute-start(bf16[128,2048]{1,0:T(8,128)(2,1)S(1)} %get-tuple-element.300), channel_id=1, source_target_pairs={{0,2},{2,0},{4,6},{6,4},{1,3},{3,1},{5,7},{7,5},{8,10},{10,8},{12,... | collective-permute-start | bytes 1572872 | tf_op jit(solution)/shard_map/ppermute | solution.py:72
  297.7 38.2 %collective-permute-start.39 = (bf16[128,2048]{1,0:T(8,128)(2,1)S(1)}, bf16[128,2048]{1,0:T(8,128)(2,1)S(1)}, u32[]{:S(2)}, u32[]{:S(2)}) collective-permute-start(bf16[128,2048]{1,0:T(8,128)(2,1)S(1)} %get-tuple-element.300), channel_id=1, source_target_pairs={{0,4},{2,6},{4,0},{6,2},{1,5},{3,7},{5,1},{7,3},{8,12},{10,14},{12... | collective-permute-start | bytes 1572872 | tf_op jit(solution)/shard_map/ppermute | solution.py:72
  298.3 37.6 %collective-permute-start.40 = (bf16[128,2048]{1,0:T(8,128)(2,1)S(1)}, bf16[128,2048]{1,0:T(8,128)(2,1)S(1)}, u32[]{:S(2)}, u32[]{:S(2)}) collective-permute-start(bf16[128,2048]{1,0:T(8,128)(2,1)S(1)} %get-tuple-element.300), channel_id=1, source_target_pairs={{0,6},{2,4},{4,2},{6,0},{1,7},{3,5},{5,3},{7,1},{8,14},{10,12},{12... | collective-permute-start | bytes 1572872 | tf_op jit(solution)/shard_map/ppermute | solution.py:72
  300.2 40.8 %collective-permute-start.41 = (bf16[128,2048]{1,0:T(8,128)(2,1)S(1)}, bf16[128,2048]{1,0:T(8,128)(2,1)S(1)}, u32[]{:S(2)}, u32[]{:S(2)}) collective-permute-start(bf16[128,2048]{1,0:T(8,128)(2,1)S(1)} %get-tuple-element.300), channel_id=1, source_target_pairs={{0,1},{1,0},{2,3},{3,2},{4,5},{5,4},{6,7},{7,6},{8,9},{9,8},{10,11... | collective-permute-start | bytes 1572872 | tf_op jit(solution)/shard_map/ppermute | solution.py:72
  335.9 217.0 %reduce-scatter.5.cloned.1.call-start = ((), (), s32[]{:S(2)}) async-start(), calls=%async_computation.8 | async-start | bytes 5308416 | tf_op jit(solution)/shard_map/reduce_scatter | solution.py:388
  336.5 31.2 %collective-permute-start.43 = (bf16[128,2048]{1,0:T(8,128)(2,1)S(1)}, bf16[128,2048]{1,0:T(8,128)(2,1)S(1)}, u32[]{:S(2)}, u32[]{:S(2)}) collective-permute-start(bf16[128,2048]{1,0:T(8,128)(2,1)S(1)} %collective-permute-done.39), channel_id=1, source_target_pairs={{0,1},{1,0},{2,3},{3,2},{4,5},{5,4},{6,7},{7,6},{8,9},{9,8},{10,11... | collective-permute-start | bytes 1572872 | tf_op jit(solution)/shard_map/ppermute | solution.py:72
  338.0 37.3 %collective-permute-start.44 = (bf16[128,2048]{1,0:T(8,128)(2,1)S(1)}, bf16[128,2048]{1,0:T(8,128)(2,1)S(1)}, u32[]{:S(2)}, u32[]{:S(2)}) collective-permute-start(bf16[128,2048]{1,0:T(8,128)(2,1)S(1)} %collective-permute-done.40), channel_id=1, source_target_pairs={{0,1},{1,0},{2,3},{3,2},{4,5},{5,4},{6,7},{7,6},{8,9},{9,8},{10,11... | collective-permute-start | bytes 1572872 | tf_op jit(solution)/shard_map/ppermute | solution.py:72
  434.7 221.9 %reduce-scatter.7.cloned.1.call-start = ((), (), s32[]{:S(2)}) async-start(), calls=%async_computation.9 | async-start | bytes 11796480 | tf_op jit(solution)/shard_map/reduce_scatter | solution.py:405
  495.0 57.5 %collective-permute-start.46 = (bf16[2,2,128,1152]{3,2,0,1:T(8,128)(2,1)}, bf16[2,2,128,1152]{3,2,0,1:T(8,128)(2,1)S(1)}, u32[]{:S(2)}, u32[]{:S(2)}) collective-permute-start(bf16[2,2,128,1152]{3,2,0,1:T(8,128)(2,1)} %bitcast.611), channel_id=1, source_target_pairs={{0,2},{2,0},{1,3},{3,1},{4,6},{6,4},{5,7},{7,5},{8,10},{10,8},{9,1... | collective-permute-start | bytes 3538952 | tf_op jit(solution)/shard_map/ppermute | solution.py:72
  513.9 38.5 %collective-permute-start.45 = (bf16[2,2,128,1152]{3,2,0,1:T(8,128)(2,1)}, bf16[2,2,128,1152]{3,2,0,1:T(8,128)(2,1)}, u32[]{:S(2)}, u32[]{:S(2)}) collective-permute-start(bf16[2,2,128,1152]{3,2,0,1:T(8,128)(2,1)} %copy.81), channel_id=1, source_target_pairs={{0,1},{1,0},{2,3},{3,2},{4,5},{5,4},{6,7},{7,6},{8,9},{9,8},{10,11... | collective-permute-start | bytes 3538952 | tf_op jit(solution)/shard_map/ppermute | solution.py:72
  553.4 213.8 %reduce-scatter.9.cloned.1.call-start = ((), (), s32[]{:S(2)}) async-start(), calls=%async_computation.10 | async-start | bytes 11796480 | tf_op jit(solution)/shard_map/reduce_scatter | solution.py:405
  556.0 29.0 %collective-permute-start.48 = (bf16[2,128,1152]{2,1,0:T(8,128)(2,1)}, bf16[2,128,1152]{2,1,0:T(8,128)(2,1)}, u32[]{:S(2)}, u32[]{:S(2)}) collective-permute-start(bf16[2,128,1152]{2,1,0:T(8,128)(2,1)} %slice_bitcast_fusion.3), channel_id=1, source_target_pairs={{0,4},{4,0},{1,5},{5,1},{2,6},{6,2},{3,7},{7,3},{8,12},{12,8},{9,1... | collective-permute-start | bytes 1769480 | tf_op jit(solution)/shard_map/ppermute | solution.py:72
  559.8 25.9 %collective-permute-start.47 = (bf16[2,128,1152]{2,1,0:T(8,128)(2,1)S(1)}, bf16[2,128,1152]{2,1,0:T(8,128)(2,1)}, u32[]{:S(2)}, u32[]{:S(2)}) collective-permute-start(bf16[2,128,1152]{2,1,0:T(8,128)(2,1)S(1)} %slice_bitcast_fusion.4), channel_id=1, source_target_pairs={{0,2},{2,0},{1,3},{3,1},{4,6},{6,4},{5,7},{7,5},{8,10},{10,8},{9,1... | collective-permute-start | bytes 1769480 | tf_op jit(solution)/shard_map/ppermute | solution.py:72
  625.0 31.6 %collective-permute-start.54 = (bf16[2,2,2,64,1280]{4,3,0,1,2:T(8,128)(2,1)S(1)}, bf16[2,2,2,64,1280]{4,3,0,1,2:T(8,128)(2,1)}, u32[]{:S(2)}, u32[]{:S(2)}) collective-permute-start(bf16[2,2,2,64,1280]{4,3,0,1,2:T(8,128)(2,1)S(1)} %dynamic-slice_bitcast_fusion), channel_id=1, source_target_pairs={{0,2},{2,0},{1,3},{3,1},{4,6},{6,4},{5,7},{7,5},{8,10},{10,8},{9,1... | collective-permute-start | bytes 3932168 | tf_op jit(solution)/shard_map/ppermute | solution.py:72
  630.5 25.1 %collective-permute-start.55 = (bf16[2,2,2,64,1024]{4,3,1,0,2:T(8,128)(2,1)S(1)}, bf16[2,2,2,64,1024]{4,3,1,0,2:T(8,128)(2,1)S(1)}, u32[]{:S(2)}, u32[]{:S(2)}) collective-permute-start(bf16[2,2,2,64,1024]{4,3,1,0,2:T(8,128)(2,1)S(1)} %dynamic-slice_bitcast_fusion.3), channel_id=1, source_target_pairs={{0,1},{1,0},{2,3},{3,2},{4,5},{5,4},{6,7},{7,6},{8,9},{9,8},{10,11... | collective-permute-start | bytes 3145736 | tf_op jit(solution)/shard_map/ppermute | solution.py:72
  656.7 204.3 %reduce-scatter.11.cloned.1.call-start = ((), (), s32[]{:S(2)}) async-start(), calls=%async_computation.11 | async-start | bytes 11796480 | tf_op jit(solution)/shard_map/reduce_scatter | solution.py:405
  670.6 21.4 %collective-permute-start.59 = (bf16[2,2,64,1280]{3,2,0,1:T(8,128)(2,1)S(1)}, bf16[2,2,64,1280]{3,2,0,1:T(8,128)(2,1)S(1)}, u32[]{:S(2)}, u32[]{:S(2)}) collective-permute-start(bf16[2,2,64,1280]{3,2,0,1:T(8,128)(2,1)S(1)} %dynamic-slice_bitcast_fusion.6), channel_id=1, source_target_pairs={{0,1},{1,0},{2,3},{3,2},{4,5},{5,4},{6,7},{7,6},{8,9},{9,8},{10,11... | collective-permute-start | bytes 1966088 | tf_op jit(solution)/shard_map/ppermute | solution.py:72
  671.3 20.7 %collective-permute-start.58 = (bf16[2,2,2,128,256]{4,3,0,1,2:T(8,128)(2,1)S(1)}, bf16[2,2,2,128,256]{4,3,0,1,2:T(8,128)(2,1)S(1)}, u32[]{:S(2)}, u32[]{:S(2)}) collective-permute-start(bf16[2,2,2,128,256]{4,3,0,1,2:T(8,128)(2,1)S(1)} %bitcast.670), channel_id=1, source_target_pairs={{0,2},{2,0},{1,3},{3,1},{4,6},{6,4},{5,7},{7,5},{8,10},{10,8},{9,1... | collective-permute-start | bytes 1572872 | tf_op jit(solution)/shard_map/ppermute | solution.py:72
  671.6 20.4 %collective-permute-start.57 = (bf16[2,2,2,128,256]{4,3,1,0,2:T(8,128)(2,1)S(1)}, bf16[2,2,2,128,256]{4,3,1,0,2:T(8,128)(2,1)S(1)}, u32[]{:S(2)}, u32[]{:S(2)}) collective-permute-start(bf16[2,2,2,128,256]{4,3,1,0,2:T(8,128)(2,1)S(1)} %bitcast.671), channel_id=1, source_target_pairs={{0,8},{8,0},{1,9},{9,1},{2,10},{10,2},{3,11},{11,3},{4,12},{12,4},... | collective-permute-start | bytes 1572872 | tf_op jit(solution)/shard_map/ppermute | solution.py:72
  700.0 38.9 %collective-permute-start.74 = (bf16[2,2,2,2,64,1024]{5,4,0,1,3,2:T(8,128)(2,1)S(1)}, bf16[2,2,2,2,64,1024]{5,4,0,1,3,2:T(8,128)(2,1)S(1)}, u32[]{:S(2)}, u32[]{:S(2)}) collective-permute-start(bf16[2,2,2,2,64,1024]{5,4,0,1,3,2:T(8,128)(2,1)S(1)} %bitcast.663), channel_id=1, source_target_pairs={{0,16},{16,0},{1,17},{17,1},{2,18},{18,2},{3,19},{19,3},{4,20},{20... | collective-permute-start | bytes 6291464 | tf_op jit(solution)/shard_map/ppermute | solution.py:72
  709.3 29.6 %collective-permute-start.75 = (bf16[2,2,2,2,64,1024]{5,4,1,0,2,3:T(8,128)(2,1)S(1)}, bf16[2,2,2,2,64,1024]{5,4,1,0,2,3:T(8,128)(2,1)S(1)}, u32[]{:S(2)}, u32[]{:S(2)}) collective-permute-start(bf16[2,2,2,2,64,1024]{5,4,1,0,2,3:T(8,128)(2,1)S(1)} %bitcast.662), channel_id=1, source_target_pairs={{0,16},{16,0},{1,17},{17,1},{2,18},{18,2},{3,19},{19,3},{4,20},{20... | collective-permute-start | bytes 6291464 | tf_op jit(solution)/shard_map/ppermute | solution.py:72
  741.3 23.8 %collective-permute-start.77 = (bf16[2,2,2,64,1024]{4,3,1,0,2:T(8,128)(2,1)}, bf16[2,2,2,64,1024]{4,3,1,0,2:T(8,128)(2,1)}, u32[]{:S(2)}, u32[]{:S(2)}) collective-permute-start(bf16[2,2,2,64,1024]{4,3,1,0,2:T(8,128)(2,1)} %dynamic-slice_bitcast_fusion.1), channel_id=1, source_target_pairs={{0,1},{1,0},{2,3},{3,2},{4,5},{5,4},{6,7},{7,6},{8,9},{9,8},{10,11... | collective-permute-start | bytes 3145736 | tf_op jit(solution)/shard_map/ppermute | solution.py:72
  743.5 23.8 %collective-permute-start.76 = (bf16[2,2,2,64,1024]{4,3,0,1,2:T(8,128)(2,1)}, bf16[2,2,2,64,1024]{4,3,0,1,2:T(8,128)(2,1)}, u32[]{:S(2)}, u32[]{:S(2)}) collective-permute-start(bf16[2,2,2,64,1024]{4,3,0,1,2:T(8,128)(2,1)} %dynamic-slice_bitcast_fusion.2), channel_id=1, source_target_pairs={{0,2},{2,0},{1,3},{3,1},{4,6},{6,4},{5,7},{7,5},{8,10},{10,8},{9,1... | collective-permute-start | bytes 3145736 | tf_op jit(solution)/shard_map/ppermute | solution.py:72
  769.8 19.8 %collective-permute-start.81 = (bf16[2,2,2,2,8,6784]{5,4,1,0,2,3:T(8,128)(2,1)S(1)}, bf16[2,2,2,2,8,6784]{5,4,1,0,2,3:T(8,128)(2,1)S(1)}, u32[]{:S(2)}, u32[]{:S(2)}) collective-permute-start(bf16[2,2,2,2,8,6784]{5,4,1,0,2,3:T(8,128)(2,1)S(1)} %bitcast.665), channel_id=1, source_target_pairs={{0,16},{16,0},{1,17},{17,1},{2,18},{18,2},{3,19},{19,3},{4,20},{20... | collective-permute-start | bytes 5210120 | tf_op jit(solution)/shard_map/ppermute | solution.py:72
  770.7 18.9 %collective-permute-start.80 = (bf16[2,2,2,2,64,768]{5,4,0,1,3,2:T(8,128)(2,1)S(1)}, bf16[2,2,2,2,64,768]{5,4,0,1,3,2:T(8,128)(2,1)S(1)}, u32[]{:S(2)}, u32[]{:S(2)}) collective-permute-start(bf16[2,2,2,2,64,768]{5,4,0,1,3,2:T(8,128)(2,1)S(1)} %bitcast.666), channel_id=1, source_target_pairs={{0,16},{16,0},{1,17},{17,1},{2,18},{18,2},{3,19},{19,3},{4,20},{20... | collective-permute-start | bytes 4718600 | tf_op jit(solution)/shard_map/ppermute | solution.py:72
  790.1 26.8 %collective-permute-start.85 = (bf16[2,2,2,8,6784]{4,3,1,0,2:T(8,128)(2,1)S(1)}, bf16[2,2,2,8,6784]{4,3,1,0,2:T(8,128)(2,1)S(1)}, u32[]{:S(2)}, u32[]{:S(2)}) collective-permute-start(bf16[2,2,2,8,6784]{4,3,1,0,2:T(8,128)(2,1)S(1)} %dynamic-slice_bitcast_fusion.4), channel_id=1, source_target_pairs={{0,1},{1,0},{2,3},{3,2},{4,5},{5,4},{6,7},{7,6},{8,9},{9,8},{10,11... | collective-permute-start | bytes 2605064 | tf_op jit(solution)/shard_map/ppermute | solution.py:72
  792.5 24.5 %collective-permute-start.84 = (bf16[2,2,2,64,768]{4,3,0,1,2:T(8,128)(2,1)S(1)}, bf16[2,2,2,64,768]{4,3,0,1,2:T(8,128)(2,1)S(1)}, u32[]{:S(2)}, u32[]{:S(2)}) collective-permute-start(bf16[2,2,2,64,768]{4,3,0,1,2:T(8,128)(2,1)S(1)} %dynamic-slice_bitcast_fusion.5), channel_id=1, source_target_pairs={{0,2},{2,0},{1,3},{3,1},{4,6},{6,4},{5,7},{7,5},{8,10},{10,8},{9,1... | collective-permute-start | bytes 2359304 | tf_op jit(solution)/shard_map/ppermute | solution.py:72
  795.0 21.0 %collective-permute-start.82 = (bf16[2,64,1024]{2,1,0:T(8,128)(2,1)S(1)}, bf16[2,64,1024]{2,1,0:T(8,128)(2,1)S(1)}, u32[]{:S(2)}, u32[]{:S(2)}) collective-permute-start(bf16[2,64,1024]{2,1,0:T(8,128)(2,1)S(1)} %dynamic-slice_bitcast_fusion.14), channel_id=1, source_target_pairs={{0,4},{4,0},{1,5},{5,1},{2,6},{6,2},{3,7},{7,3},{8,12},{12,8},{9,1... | collective-permute-start | bytes 786440 | tf_op jit(solution)/shard_map/ppermute | solution.py:72
  (210 other events, 2039.2 us)
Sparse Core Ops, SparseCore 0:
  10.8 78.1 all-gather.4
  93.4 67.3 all-gather.6
  174.3 65.4 all-gather.8
  336.0 87.1 all-gather.10
  434.8 118.0 reduce-scatter.4
  555.4 76.9 reduce-scatter.6
  656.8 90.8 reduce-scatter.8
  767.4 93.5 reduce-scatter.10

commit v3 on v2

--- a/solution.py
+++ b/solution.py
@@ -249,8 +249,10 @@
     def gather_units(block):
         return lax.all_gather(block, unit_axes, axis=0, tiled=True)
 
-    down_all = gather_units(jnp.concatenate([down_weight, down_adapt], axis=1))
     arrived, _ = advance(*jobs)
+    down_all = gather_units(
+        jnp.concatenate(tie((down_weight, down_adapt), arrived[0]), axis=1)
+    )
     pair_weight, pair_expand = tie((gateup_weight, gateup_expand), arrived)
     pairs = [
         jnp.concatenate([pair_weight[:, k], pair_expand[:, k]], axis=1) for k in range(2)
@@ -260,7 +262,8 @@
         arrived, _ = advance(*jobs)
     gate_all = gather_units(tie(pairs[0], arrived))
     arrived, down_all = advance(*jobs, beside=down_all)
-    advance(*jobs)
+    advance(*jobs[:2])
+    advance(*jobs[2:])
     kv_into, from_all, query_one, query_two = (job.result() for job in jobs)
     kv_full, qkv_into = kv_into[:, : 2 * DH], kv_into[:, 2 * DH :]
     qkv_columns = 2 * half + 2 * DH

time: 886 us -> 881 us (level)
  waiting for transfers between devices: 371 us -> 357 us
  starting transfers between devices: 102 us -> 115 us
    ppermute x94, waiting for transfers between devices: 364 us -> 345 us  [shift(): return lax.ppermute(values, axes, [(i, i ^ mask) for i in range(size)])]
    ppermute x94, starting transfers between devices: 101 us -> 113 us  [shift(): return lax.ppermute(values, axes, [(i, i ^ mask) for i in range(size)])]
    unnamed x354 -> x330, local copies, waits for them, and re-layouts: 37.8 us -> 35.6 us
  transfers between devices with their start and end apart: 102 -> 102, of which waited for: 51 -> 55; matrix products, arithmetic and copies ran while one was open for 39% -> 39% of each run, Pallas kernels for 0% -> 0%
where the time goes in v3:
time: 881 us; the launch traced here: 874 us
  waiting for transfers between devices  357 us (41%)
  matrix products  201 us (23%)
  starting transfers between devices  115 us (13%)
  other arithmetic  101 us (11%)
  local copies, waits for them, and re-layouts  75.3 us (9%)
  between operations  17.6 us (2%)
    ppermute x94, waiting for transfers between devices, shift(): return lax.ppermute(values, axes, [(i, i ^ mask) for i in range(size)])  345 us
    ppermute x94, starting transfers between devices, shift(): return lax.ppermute(values, axes, [(i, i ^ mask) for i in range(size)])  113 us
    dot_general x16, matrix products, product_back(): lax.dot_general(former, latter, (((1,), (1,)), ((), ())), preferred_eleme...  76.7 us
    dot_general x14, matrix products, product_rows(): lax.dot_general(former, latter, (((0,), (0,)), ((), ())), preferred_eleme...  62.7 us
    dot_general x17, matrix products, product(): return jnp.dot(former, latter, preferred_element_type=jnp.float32)  61.6 us
    another operation x75, other arithmetic, place(): jnp.stack([jnp.where(first, own, other), jnp.where(first, other, own)], a...  47.3 us
    unnamed x330, local copies, waits for them, and re-layouts  35.6 us
    convert_element_type x38, other arithmetic, finish(): self.value = self.value.astype(jnp.bfloat16)  22.6 us
  transfers between devices with their start and end apart: 102, of which 55 were waited for; matrix products, arithmetic and copies ran while one was open for 39% of the time, Pallas kernels for 0%

profile of v3, /device:TPU:0, one launch (start us, length us, event | category | flops | bytes accessed | tf_op | source)
XLA Modules:
  0.0 874.4 jit_solution(3935064504187948702)
XLA Ops:
  8.2 4.1 collective-permute-start.2
  19.9 4.1 collective-permute-done
  27.5 4.1 copy.56
  38.2 5.3 collective-permute-done.4
  45.2 8.4 collective-permute-done.6
  59.1 11.8 %collective-permute-done.8 = bf16[2,2,64,768]{3,2,1,0:T(8,128)(2,1)} collective-permute-done((bf16[2,2,64,768]{3,2,1,0:T(8,128)(2,1)}, bf16[2,2,64,768]{3,2,1,0:T(8,128)(2,1)}, u32[]{:S(2)}, u32[]{:S(2)}) %collective-permute-start.8) | collective-permute-done | bytes 393248 | tf_op jit(solution)/shard_map/ppermute | solution.py:72
  87.6 27.9 %collective-permute-done.12 = bf16[2,2,2,64,768]{4,3,2,1,0:T(8,128)(2,1)} collective-permute-done((bf16[2,2,2,64,768]{4,3,2,1,0:T(8,128)(2,1)S(1)}, bf16[2,2,2,64,768]{4,3,2,1,0:T(8,128)(2,1)}, u32[]{:S(2)}, u32[]{:S(2)}) %collective-permute-start.12) | collective-permute-done | bytes 786464 | tf_op jit(solution)/shard_map/ppermute | solution.py:72
  115.5 4.5 collective-permute-done.14
  162.2 3.6 all-gather.7.cloned.1.call-done
  174.8 6.1 collective-permute-done.25
  181.5 4.9 collective-permute-done.26
  193.2 13.9 %collective-permute-done.29 = bf16[2,2,128,256]{3,2,1,0:T(8,128)(2,1)S(1)} collective-permute-done((bf16[2,2,128,256]{3,2,1,0:T(8,128)(2,1)S(1)}, bf16[2,2,128,256]{3,2,1,0:T(8,128)(2,1)S(1)}, u32[]{:S(2)}, u32[]{:S(2)}) %collective-permute-start.29) | collective-permute-done | bytes 262176 | tf_op jit(solution)/shard_map/ppermute | solution.py:72
  220.2 31.8 %collective-permute-done.33 = bf16[2,2,2,128,256]{4,3,2,0,1:T(8,128)(2,1)} collective-permute-done((bf16[2,2,2,128,256]{4,3,2,0,1:T(8,128)(2,1)}, bf16[2,2,2,128,256]{4,3,2,0,1:T(8,128)(2,1)}, u32[]{:S(2)}, u32[]{:S(2)}) %collective-permute-start.33) | collective-permute-done | bytes 524320 | tf_op jit(solution)/shard_map/ppermute | solution.py:72
  294.7 19.1 %collective-permute-done.38 = bf16[128,2048]{1,0:T(8,128)(2,1)S(1)} collective-permute-done((bf16[128,2048]{1,0:T(8,128)(2,1)S(1)}, bf16[128,2048]{1,0:T(8,128)(2,1)S(1)}, u32[]{:S(2)}, u32[]{:S(2)}) %collective-permute-start.38) | collective-permute-done | bytes 524320 | tf_op jit(solution)/shard_map/ppermute | solution.py:72
  313.8 16.1 %collective-permute-done.39 = bf16[128,2048]{1,0:T(8,128)(2,1)S(1)} collective-permute-done((bf16[128,2048]{1,0:T(8,128)(2,1)S(1)}, bf16[128,2048]{1,0:T(8,128)(2,1)S(1)}, u32[]{:S(2)}, u32[]{:S(2)}) %collective-permute-start.39) | collective-permute-done | bytes 524320 | tf_op jit(solution)/shard_map/ppermute | solution.py:72
  336.0 9.0 %collective-permute-done.42 = bf16[128,2048]{1,0:T(8,128)(2,1)S(1)} collective-permute-done((bf16[128,2048]{1,0:T(8,128)(2,1)S(1)}, bf16[128,2048]{1,0:T(8,128)(2,1)S(1)}, u32[]{:S(2)}, u32[]{:S(2)}) %collective-permute-start.42) | collective-permute-done | bytes 524320 | tf_op jit(solution)/shard_map/ppermute | solution.py:72
  345.8 16.0 %collective-permute-done.43 = bf16[128,2048]{1,0:T(8,128)(2,1)S(1)} collective-permute-done((bf16[128,2048]{1,0:T(8,128)(2,1)S(1)}, bf16[128,2048]{1,0:T(8,128)(2,1)S(1)}, u32[]{:S(2)}, u32[]{:S(2)}) %collective-permute-start.43) | collective-permute-done | bytes 524320 | tf_op jit(solution)/shard_map/ppermute | solution.py:72
  362.6 7.3 collective-permute-done.44
  370.7 3.9 convolution_convert_fusion.15
  374.6 14.8 %fusion.192 = f32[1024,2048]{1,0:T(8,128)} fusion(bf16[2048,2304]{1,0:T(8,128)(2,1)} %all-gather.7.cloned.1.call-done, bf16[1024,256]{1,0:T(8,128)(2,1)S(1)} %convolution_convert_fusion.15, bf16[1024,2048]{1,0:T(8,128)(2,1)S(1)} %copy-done.112), kind=kOutput, calls=%fused_computation.589 | convolution fusion | flops 9673113600 | bytes 22544384 | tf_op jit(solution)/shard_map/dot_general | solution.py:25
  389.4 19.2 %multiply_convert_fusion.2 = (bf16[1024,2048]{1,0:T(8,128)(2,1)}, f32[1024,2048]{1,0:T(8,128)}) fusion(f32[1024,2048]{1,0:T(8,128)} %fusion.192, bf16[2048,2304]{1,0:T(8,128)(2,1)} %all-gather.9.cloned.1.call-done, bf16[1024,256]{1,0:T(8,128)(2,1)S(1)} %convolution_convert_fusion.15, bf16[1024,2048]{1,0:T(8,128)(2,1)} %constant_dynamic-update-slice_fusion.8), kind=kOutput, calls=%fused_computation.17 | convolution fusion | flops 9694085120 | bytes 35127296 | tf_op jit(solution)/shard_map/dot_general | solution.py:25
  408.6 13.5 %convolution_convert_fusion.4 = bf16[1024,2304]{1,0:T(8,128)(2,1)S(1)} fusion(bf16[1024,2048]{1,0:T(8,128)(2,1)} %get-tuple-element.200, bf16[2048,2304]{1,0:T(8,128)(2,1)} %all-gather.5.cloned.1.call-done), kind=kOutput, calls=%fused_computation.23 | convolution fusion | flops 9666035712 | bytes 18350080 | tf_op jit(solution)/shard_map/dot_general | solution.py:21
  439.2 22.7 %fusion.6 = (bf16[1024,2048]{1,0:T(8,128)(2,1)}, bf16[1024,2048]{1,0:T(8,128)(2,1)}) fusion(f32[1024,2048]{1,0:T(8,128)} %fusion.192, f32[1024,2048]{1,0:T(8,128)} %get-tuple-element.443, bf16[2048,2304]{1,0:T(8,128)(2,1)} %all-gather.5.cloned.1.call-done, bf16[1024,256]{1,0:T(8,128)(2,1)S(1)} %copy.80, bf16[1024,2048]{1,0:T(8,128)(2,1)} %copy-done.115), kind=kOutput, calls=%fused_computation.14 | convolution fusion | flops 9723445248 | bytes 39321600 | tf_op jit(solution)/shard_map/dot_general | solution.py:25
  461.9 13.7 %fusion.218 = f32[1024,2304]{1,0:T(8,128)S(1)} fusion(bf16[1024,2048]{1,0:T(8,128)(2,1)} %get-tuple-element.206, bf16[2048,2304]{1,0:T(8,128)(2,1)} %all-gather.9.cloned.1.call-done), kind=kOutput, calls=%fused_computation.600 | convolution fusion | flops 9663676416 | bytes 23068672 | tf_op jit(solution)/shard_map/dot_general | solution.py:21
  475.6 12.2 %add_convert_fusion = bf16[1024,2304]{1,0:T(8,128)(2,1)S(1)} fusion(f32[1024,2304]{1,0:T(8,128)S(1)} %fusion.218, bf16[1024,2048]{1,0:T(8,128)(2,1)S(1)} %copy-done.135, bf16[2048,2304]{1,0:T(8,128)(2,1)} %all-gather.7.cloned.1.call-done), kind=kOutput, calls=%fused_computation.7 | convolution fusion | flops 9668395008 | bytes 27787264 | tf_op jit(solution)/shard_map/dot_general | solution.py:21
  489.3 17.6 %collective-permute-start.46 = (bf16[2,2,128,1152]{3,2,0,1:T(8,128)(2,1)}, bf16[2,2,128,1152]{3,2,0,1:T(8,128)(2,1)S(1)}, u32[]{:S(2)}, u32[]{:S(2)}) collective-permute-start(bf16[2,2,128,1152]{3,2,0,1:T(8,128)(2,1)} %bitcast.611), channel_id=1, source_target_pairs={{0,2},{2,0},{1,3},{3,1},{4,6},{6,4},{5,7},{7,5},{8,10},{10,8},{9,1... | collective-permute-start | bytes 3538952 | tf_op jit(solution)/shard_map/ppermute | solution.py:72
  508.7 13.1 %convolution_convert_fusion.1 = bf16[2048,2304]{1,0:T(8,128)(2,1)} fusion(bf16[1024,2048]{1,0:T(8,128)(2,1)S(1)} %copy-done.136, bf16[1024,256]{1,0:T(8,128)(2,1)S(1)} %copy-done.133, bf16[1024,2048]{1,0:T(8,128)(2,1)S(1)} %copy-done.113), kind=kOutput, calls=%fused_computation.5 | convolution fusion | flops 9677832192 | bytes 18350080 | tf_op jit(solution)/shard_map/dot_general | solution.py:31
  521.9 15.4 %convolution_convert_fusion.2 = bf16[2048,2304]{1,0:T(8,128)(2,1)} fusion(bf16[1024,2048]{1,0:T(8,128)(2,1)} %get-tuple-element.200, bf16[1024,256]{1,0:T(8,128)(2,1)} %copy-done.87, bf16[1024,2048]{1,0:T(8,128)(2,1)} %copy-done.115), kind=kOutput, calls=%fused_computation.6 | convolution fusion | flops 9677832192 | bytes 18350080 | tf_op jit(solution)/shard_map/dot_general | solution.py:31
  537.3 9.5 %collective-permute-done.46 = bf16[2,2,128,1152]{3,2,0,1:T(8,128)(2,1)S(1)} collective-permute-done((bf16[2,2,128,1152]{3,2,0,1:T(8,128)(2,1)}, bf16[2,2,128,1152]{3,2,0,1:T(8,128)(2,1)S(1)}, u32[]{:S(2)}, u32[]{:S(2)}) %collective-permute-start.46) | collective-permute-done | bytes 1179680 | tf_op jit(solution)/shard_map/ppermute | solution.py:72
  554.6 13.3 %convolution_convert_fusion = bf16[2048,2304]{1,0:T(8,128)(2,1)} fusion(bf16[1024,2048]{1,0:T(8,128)(2,1)S(1)} %copy-done.137, bf16[1024,256]{1,0:T(8,128)(2,1)S(1)} %copy-done.134, bf16[1024,2048]{1,0:T(8,128)(2,1)S(1)} %copy-done.114), kind=kOutput, calls=%fused_computation.4 | convolution fusion | flops 9677832192 | bytes 18350080 | tf_op jit(solution)/shard_map/dot_general | solution.py:31
  567.9 11.4 %collective-permute-done.48 = bf16[2,128,1152]{2,1,0:T(8,128)(2,1)} collective-permute-done((bf16[2,128,1152]{2,1,0:T(8,128)(2,1)}, bf16[2,128,1152]{2,1,0:T(8,128)(2,1)}, u32[]{:S(2)}, u32[]{:S(2)}) %collective-permute-start.48) | collective-permute-done | bytes 589856 | tf_op jit(solution)/shard_map/ppermute | solution.py:72
  584.8 3.7 collective-permute-done.50
  588.5 8.9 %collective-permute-done.49 = bf16[128,1152]{1,0:T(8,128)(2,1)S(1)} collective-permute-done((bf16[128,1152]{1,0:T(8,128)(2,1)S(1)}, bf16[128,1152]{1,0:T(8,128)(2,1)S(1)}, u32[]{:S(2)}, u32[]{:S(2)}) %collective-permute-start.49) | collective-permute-done | bytes 294944 | tf_op jit(solution)/shard_map/ppermute | solution.py:72
  630.7 19.2 %collective-permute-done.55 = bf16[2,2,2,64,1024]{4,3,1,0,2:T(8,128)(2,1)S(1)} collective-permute-done((bf16[2,2,2,64,1024]{4,3,1,0,2:T(8,128)(2,1)S(1)}, bf16[2,2,2,64,1024]{4,3,1,0,2:T(8,128)(2,1)S(1)}, u32[]{:S(2)}, u32[]{:S(2)}) %collective-permute-start.55) | collective-permute-done | bytes 1048608 | tf_op jit(solution)/shard_map/ppermute | solution.py:72
  675.8 10.3 %collective-permute-done.58 = bf16[2,2,2,128,256]{4,3,0,1,2:T(8,128)(2,1)S(1)} collective-permute-done((bf16[2,2,2,128,256]{4,3,0,1,2:T(8,128)(2,1)S(1)}, bf16[2,2,2,128,256]{4,3,0,1,2:T(8,128)(2,1)S(1)}, u32[]{:S(2)}, u32[]{:S(2)}) %collective-permute-start.58) | collective-permute-done | bytes 524320 | tf_op jit(solution)/shard_map/ppermute | solution.py:72
  693.9 9.5 %collective-permute-done.65 = bf16[2,64,1024]{2,1,0:T(8,128)(2,1)S(1)} collective-permute-done((bf16[2,64,1024]{2,1,0:T(8,128)(2,1)S(1)}, bf16[2,64,1024]{2,1,0:T(8,128)(2,1)S(1)}, u32[]{:S(2)}, u32[]{:S(2)}) %collective-permute-start.65) | collective-permute-done | bytes 262176 | tf_op jit(solution)/shard_map/ppermute | solution.py:72
  710.3 7.8 collective-permute-done.70
  721.7 3.9 collective-permute-done.67
  748.4 6.6 concatenate.134
  755.0 3.6 convolution_convert_fusion.9
  771.1 11.2 %collective-permute-done.79 = bf16[2,2,64,1024]{3,2,1,0:T(8,128)(2,1)S(1)} collective-permute-done((bf16[2,2,64,1024]{3,2,1,0:T(8,128)(2,1)S(1)}, bf16[2,2,64,1024]{3,2,1,0:T(8,128)(2,1)S(1)}, u32[]{:S(2)}, u32[]{:S(2)}) %collective-permute-start.79) | collective-permute-done | bytes 524320 | tf_op jit(solution)/shard_map/ppermute | solution.py:72
  791.5 10.0 %collective-permute-done.83 = bf16[2,64,1024]{2,1,0:T(8,128)(2,1)S(1)} collective-permute-done((bf16[2,64,1024]{2,1,0:T(8,128)(2,1)S(1)}, bf16[2,64,1024]{2,1,0:T(8,128)(2,1)S(1)}, u32[]{:S(2)}, u32[]{:S(2)}) %collective-permute-start.83) | collective-permute-done | bytes 262176 | tf_op jit(solution)/shard_map/ppermute | solution.py:72
  801.6 7.4 collective-permute-done.82
  817.3 5.0 collective-permute-done.87
  827.7 6.5 collective-permute-done.90
  839.3 5.0 collective-permute-done.92
  848.5 7.3 reduce-scatter.11.cloned.1.call-done.up_ref
  859.2 8.2 shard_map.287
  (809 shorter events, 344.4 us)
Async XLA Ops:
  7.2 112.9 %all-gather.5.cloned.1.call-start = ((), (), s32[]{:S(2)}) async-start(), calls=%async_computation.4 | async-start | bytes 11796480 | tf_op jit(solution)/shard_map/all_gather | solution.py:250
  27.4 138.4 %all-gather.7.cloned.1.call-start = ((), (), s32[]{:S(2)}) async-start(), calls=%async_computation.5 | async-start | bytes 11796480 | tf_op jit(solution)/shard_map/all_gather | solution.py:250
  32.5 21.1 %collective-permute-start.6 = (bf16[2,64,1024]{2,1,0:T(8,128)(2,1)S(1)}, bf16[2,64,1024]{2,1,0:T(8,128)(2,1)S(1)}, u32[]{:S(2)}, u32[]{:S(2)}) collective-permute-start(bf16[2,64,1024]{2,1,0:T(8,128)(2,1)S(1)} %pad_maximum_fusion.42), channel_id=1, source_target_pairs={{0,8},{8,0},{1,9},{9,1},{2,10},{10,2},{3,11},{11,3},{4,12},{12,4},... | collective-permute-start | bytes 786440 | tf_op jit(solution)/shard_map/ppermute | solution.py:72
  54.5 18.8 %collective-permute-start.11 = (bf16[2,2,64,1024]{3,2,1,0:T(8,128)(2,1)}, bf16[2,2,64,1024]{3,2,1,0:T(8,128)(2,1)S(1)}, u32[]{:S(2)}, u32[]{:S(2)}) collective-permute-start(bf16[2,2,64,1024]{3,2,1,0:T(8,128)(2,1)} %pad_maximum_fusion.33), channel_id=1, source_target_pairs={{0,4},{4,0},{1,5},{5,1},{2,6},{6,2},{3,7},{7,3},{8,12},{12,8},{9,1... | collective-permute-start | bytes 1572872 | tf_op jit(solution)/shard_map/ppermute | solution.py:72
  55.4 19.2 %collective-permute-start.10 = (bf16[2,2,64,1024]{3,2,1,0:T(8,128)(2,1)}, bf16[2,2,64,1024]{3,2,1,0:T(8,128)(2,1)S(1)}, u32[]{:S(2)}, u32[]{:S(2)}) collective-permute-start(bf16[2,2,64,1024]{3,2,1,0:T(8,128)(2,1)} %pad_maximum_fusion.32), channel_id=1, source_target_pairs={{0,2},{2,0},{1,3},{3,1},{4,6},{6,4},{5,7},{7,5},{8,10},{10,8},{9,1... | collective-permute-start | bytes 1572872 | tf_op jit(solution)/shard_map/ppermute | solution.py:72
  75.9 39.6 %collective-permute-start.15 = (bf16[2,2,2,64,1024]{4,3,2,1,0:T(8,128)(2,1)}, bf16[2,2,2,64,1024]{4,3,2,1,0:T(8,128)(2,1)}, u32[]{:S(2)}, u32[]{:S(2)}) collective-permute-start(bf16[2,2,2,64,1024]{4,3,2,1,0:T(8,128)(2,1)} %pad_maximum_fusion.23), channel_id=1, source_target_pairs={{0,1},{1,0},{2,3},{3,2},{4,5},{5,4},{6,7},{7,6},{8,9},{9,8},{10,11... | collective-permute-start | bytes 3145736 | tf_op jit(solution)/shard_map/ppermute | solution.py:72
  78.4 41.6 %collective-permute-start.14 = (bf16[2,2,2,64,1024]{4,3,2,1,0:T(8,128)(2,1)}, bf16[2,2,2,64,1024]{4,3,2,1,0:T(8,128)(2,1)}, u32[]{:S(2)}, u32[]{:S(2)}) collective-permute-start(bf16[2,2,2,64,1024]{4,3,2,1,0:T(8,128)(2,1)} %pad_maximum_fusion.22), channel_id=1, source_target_pairs={{0,1},{1,0},{2,3},{3,2},{4,5},{5,4},{6,7},{7,6},{8,9},{9,8},{10,11... | collective-permute-start | bytes 3145736 | tf_op jit(solution)/shard_map/ppermute | solution.py:72
  80.4 35.1 %collective-permute-start.13 = (bf16[2,2,2,8,6784]{4,3,2,1,0:T(8,128)(2,1)}, bf16[2,2,2,8,6784]{4,3,2,1,0:T(8,128)(2,1)S(1)}, u32[]{:S(2)}, u32[]{:S(2)}) collective-permute-start(bf16[2,2,2,8,6784]{4,3,2,1,0:T(8,128)(2,1)} %pad_maximum_fusion.26), channel_id=1, source_target_pairs={{0,4},{4,0},{1,5},{5,1},{2,6},{6,2},{3,7},{7,3},{8,12},{12,8},{9,1... | collective-permute-start | bytes 2605064 | tf_op jit(solution)/shard_map/ppermute | solution.py:72
  81.6 33.9 %collective-permute-start.12 = (bf16[2,2,2,64,768]{4,3,2,1,0:T(8,128)(2,1)S(1)}, bf16[2,2,2,64,768]{4,3,2,1,0:T(8,128)(2,1)}, u32[]{:S(2)}, u32[]{:S(2)}) collective-permute-start(bf16[2,2,2,64,768]{4,3,2,1,0:T(8,128)(2,1)S(1)} %pad_maximum_fusion.27), channel_id=1, source_target_pairs={{0,2},{2,0},{1,3},{3,1},{4,6},{6,4},{5,7},{7,5},{8,10},{10,8},{9,1... | collective-permute-start | bytes 2359304 | tf_op jit(solution)/shard_map/ppermute | solution.py:72
  82.3 172.8 %all-gather.9.cloned.1.call-start = ((), (), s32[]{:S(2)}) async-start(), calls=%async_computation.6 | async-start | bytes 11796480 | tf_op jit(solution)/shard_map/all_gather | solution.py:250
  85.0 77.2 %collective-permute-start.20 = (bf16[64,1280]{1,0:T(8,128)(2,1)}, bf16[64,1280]{1,0:T(8,128)(2,1)}, u32[]{:S(2)}, u32[]{:S(2)}) collective-permute-start(bf16[64,1280]{1,0:T(8,128)(2,1)} %pad_maximum_fusion.48), channel_id=1, source_target_pairs={{0,8},{8,0},{1,9},{9,1},{2,10},{10,2},{3,11},{11,3},{4,12},{12,4},... | collective-permute-start | bytes 491528 | tf_op jit(solution)/shard_map/ppermute | solution.py:72
  127.0 35.2 %collective-permute-start.21 = (bf16[64,1280]{1,0:T(8,128)(2,1)}, bf16[64,1280]{1,0:T(8,128)(2,1)}, u32[]{:S(2)}, u32[]{:S(2)}) collective-permute-start(bf16[64,1280]{1,0:T(8,128)(2,1)} %pad_maximum_fusion.49), channel_id=1, source_target_pairs={{0,4},{4,0},{1,5},{5,1},{2,6},{6,2},{3,7},{7,3},{8,12},{12,8},{9,1... | collective-permute-start | bytes 491528 | tf_op jit(solution)/shard_map/ppermute | solution.py:72
  131.1 19.9 %collective-permute-start.23 = (bf16[2,2,2,2,64,1024]{5,4,3,2,1,0:T(8,128)(2,1)}, bf16[2,2,2,2,64,1024]{5,4,3,2,1,0:T(8,128)(2,1)}, u32[]{:S(2)}, u32[]{:S(2)}) collective-permute-start(bf16[2,2,2,2,64,1024]{5,4,3,2,1,0:T(8,128)(2,1)} %pad_maximum_fusion.16), channel_id=1, source_target_pairs={{0,16},{16,0},{1,17},{17,1},{2,18},{18,2},{3,19},{19,3},{4,20},{20... | collective-permute-start | bytes 6291464 | tf_op jit(solution)/shard_map/ppermute | solution.py:72
  165.9 263.2 %all-gather.11.cloned.1.call-start = ((), (), s32[]{:S(2)}) async-start(), calls=%async_computation.7 | async-start | bytes 4718592 | tf_op jit(solution)/shard_map/all_gather | solution.py:382
  186.6 23.0 %collective-permute-start.31 = (bf16[2,2,64,1280]{3,2,1,0:T(8,128)(2,1)S(1)}, bf16[2,2,64,1280]{3,2,1,0:T(8,128)(2,1)S(1)}, u32[]{:S(2)}, u32[]{:S(2)}) collective-permute-start(bf16[2,2,64,1280]{3,2,1,0:T(8,128)(2,1)S(1)} %pad_maximum_fusion.29), channel_id=1, source_target_pairs={{0,2},{2,0},{1,3},{3,1},{4,6},{6,4},{5,7},{7,5},{8,10},{10,8},{9,1... | collective-permute-start | bytes 1966088 | tf_op jit(solution)/shard_map/ppermute | solution.py:72
  187.5 22.1 %collective-permute-start.30 = (bf16[2,2,64,1280]{3,2,1,0:T(8,128)(2,1)S(1)}, bf16[2,2,64,1280]{3,2,1,0:T(8,128)(2,1)S(1)}, u32[]{:S(2)}, u32[]{:S(2)}) collective-permute-start(bf16[2,2,64,1280]{3,2,1,0:T(8,128)(2,1)S(1)} %pad_maximum_fusion.28), channel_id=1, source_target_pairs={{0,1},{1,0},{2,3},{3,2},{4,5},{5,4},{6,7},{7,6},{8,9},{9,8},{10,11... | collective-permute-start | bytes 1966088 | tf_op jit(solution)/shard_map/ppermute | solution.py:72
  210.9 43.4 %collective-permute-start.35 = (bf16[2,2,2,64,1280]{4,3,2,1,0:T(8,128)(2,1)}, bf16[2,2,2,64,1280]{4,3,2,1,0:T(8,128)(2,1)}, u32[]{:S(2)}, u32[]{:S(2)}) collective-permute-start(bf16[2,2,2,64,1280]{4,3,2,1,0:T(8,128)(2,1)} %pad_maximum_fusion.20), channel_id=1, source_target_pairs={{0,1},{1,0},{2,3},{3,2},{4,5},{5,4},{6,7},{7,6},{8,9},{9,8},{10,11... | collective-permute-start | bytes 3932168 | tf_op jit(solution)/shard_map/ppermute | solution.py:72
  213.6 41.4 %collective-permute-start.34 = (bf16[2,2,2,64,1280]{4,3,2,1,0:T(8,128)(2,1)}, bf16[2,2,2,64,1280]{4,3,2,1,0:T(8,128)(2,1)}, u32[]{:S(2)}, u32[]{:S(2)}) collective-permute-start(bf16[2,2,2,64,1280]{4,3,2,1,0:T(8,128)(2,1)} %pad_maximum_fusion.19), channel_id=1, source_target_pairs={{0,2},{2,0},{1,3},{3,1},{4,6},{6,4},{5,7},{7,5},{8,10},{10,8},{9,1... | collective-permute-start | bytes 3932168 | tf_op jit(solution)/shard_map/ppermute | solution.py:72
  216.4 35.7 %collective-permute-start.33 = (bf16[2,2,2,128,256]{4,3,2,0,1:T(8,128)(2,1)}, bf16[2,2,2,128,256]{4,3,2,0,1:T(8,128)(2,1)}, u32[]{:S(2)}, u32[]{:S(2)}) collective-permute-start(bf16[2,2,2,128,256]{4,3,2,0,1:T(8,128)(2,1)} %pad_maximum_fusion.36), channel_id=1, source_target_pairs={{0,1},{1,0},{2,3},{3,2},{4,5},{5,4},{6,7},{7,6},{8,9},{9,8},{10,11... | collective-permute-start | bytes 1572872 | tf_op jit(solution)/shard_map/ppermute | solution.py:72
  217.9 36.4 %collective-permute-start.32 = (bf16[2,2,2,128,256]{4,3,0,1,2:T(8,128)(2,1)}, bf16[2,2,2,128,256]{4,3,0,1,2:T(8,128)(2,1)}, u32[]{:S(2)}, u32[]{:S(2)}) collective-permute-start(bf16[2,2,2,128,256]{4,3,0,1,2:T(8,128)(2,1)} %pad_maximum_fusion.35), channel_id=1, source_target_pairs={{0,4},{4,0},{1,5},{5,1},{2,6},{6,2},{3,7},{7,3},{8,12},{12,8},{9,1... | collective-permute-start | bytes 1572872 | tf_op jit(solution)/shard_map/ppermute | solution.py:72
  288.9 25.0 %collective-permute-start.38 = (bf16[128,2048]{1,0:T(8,128)(2,1)S(1)}, bf16[128,2048]{1,0:T(8,128)(2,1)S(1)}, u32[]{:S(2)}, u32[]{:S(2)}) collective-permute-start(bf16[128,2048]{1,0:T(8,128)(2,1)S(1)} %get-tuple-element.304), channel_id=1, source_target_pairs={{0,2},{2,0},{4,6},{6,4},{1,3},{3,1},{5,7},{7,5},{8,10},{10,8},{12,... | collective-permute-start | bytes 1572872 | tf_op jit(solution)/shard_map/ppermute | solution.py:72
  291.7 38.2 %collective-permute-start.39 = (bf16[128,2048]{1,0:T(8,128)(2,1)S(1)}, bf16[128,2048]{1,0:T(8,128)(2,1)S(1)}, u32[]{:S(2)}, u32[]{:S(2)}) collective-permute-start(bf16[128,2048]{1,0:T(8,128)(2,1)S(1)} %get-tuple-element.304), channel_id=1, source_target_pairs={{0,4},{2,6},{4,0},{6,2},{1,5},{3,7},{5,1},{7,3},{8,12},{10,14},{12... | collective-permute-start | bytes 1572872 | tf_op jit(solution)/shard_map/ppermute | solution.py:72
  292.3 37.6 %collective-permute-start.40 = (bf16[128,2048]{1,0:T(8,128)(2,1)S(1)}, bf16[128,2048]{1,0:T(8,128)(2,1)S(1)}, u32[]{:S(2)}, u32[]{:S(2)}) collective-permute-start(bf16[128,2048]{1,0:T(8,128)(2,1)S(1)} %get-tuple-element.304), channel_id=1, source_target_pairs={{0,6},{2,4},{4,2},{6,0},{1,7},{3,5},{5,3},{7,1},{8,14},{10,12},{12... | collective-permute-start | bytes 1572872 | tf_op jit(solution)/shard_map/ppermute | solution.py:72
  294.2 41.0 %collective-permute-start.41 = (bf16[128,2048]{1,0:T(8,128)(2,1)S(1)}, bf16[128,2048]{1,0:T(8,128)(2,1)S(1)}, u32[]{:S(2)}, u32[]{:S(2)}) collective-permute-start(bf16[128,2048]{1,0:T(8,128)(2,1)S(1)} %get-tuple-element.304), channel_id=1, source_target_pairs={{0,1},{1,0},{2,3},{3,2},{4,5},{5,4},{6,7},{7,6},{8,9},{9,8},{10,11... | collective-permute-start | bytes 1572872 | tf_op jit(solution)/shard_map/ppermute | solution.py:72
  330.0 217.5 %reduce-scatter.5.cloned.1.call-start = ((), (), s32[]{:S(2)}) async-start(), calls=%async_computation.8 | async-start | bytes 5308416 | tf_op jit(solution)/shard_map/reduce_scatter | solution.py:391
  330.6 31.2 %collective-permute-start.43 = (bf16[128,2048]{1,0:T(8,128)(2,1)S(1)}, bf16[128,2048]{1,0:T(8,128)(2,1)S(1)}, u32[]{:S(2)}, u32[]{:S(2)}) collective-permute-start(bf16[128,2048]{1,0:T(8,128)(2,1)S(1)} %collective-permute-done.39), channel_id=1, source_target_pairs={{0,1},{1,0},{2,3},{3,2},{4,5},{5,4},{6,7},{7,6},{8,9},{9,8},{10,11... | collective-permute-start | bytes 1572872 | tf_op jit(solution)/shard_map/ppermute | solution.py:72
  332.1 37.8 %collective-permute-start.44 = (bf16[128,2048]{1,0:T(8,128)(2,1)S(1)}, bf16[128,2048]{1,0:T(8,128)(2,1)S(1)}, u32[]{:S(2)}, u32[]{:S(2)}) collective-permute-start(bf16[128,2048]{1,0:T(8,128)(2,1)S(1)} %collective-permute-done.40), channel_id=1, source_target_pairs={{0,1},{1,0},{2,3},{3,2},{4,5},{5,4},{6,7},{7,6},{8,9},{9,8},{10,11... | collective-permute-start | bytes 1572872 | tf_op jit(solution)/shard_map/ppermute | solution.py:72
  429.1 221.9 %reduce-scatter.7.cloned.1.call-start = ((), (), s32[]{:S(2)}) async-start(), calls=%async_computation.9 | async-start | bytes 11796480 | tf_op jit(solution)/shard_map/reduce_scatter | solution.py:408
  489.3 57.5 %collective-permute-start.46 = (bf16[2,2,128,1152]{3,2,0,1:T(8,128)(2,1)}, bf16[2,2,128,1152]{3,2,0,1:T(8,128)(2,1)S(1)}, u32[]{:S(2)}, u32[]{:S(2)}) collective-permute-start(bf16[2,2,128,1152]{3,2,0,1:T(8,128)(2,1)} %bitcast.611), channel_id=1, source_target_pairs={{0,2},{2,0},{1,3},{3,1},{4,6},{6,4},{5,7},{7,5},{8,10},{10,8},{9,1... | collective-permute-start | bytes 3538952 | tf_op jit(solution)/shard_map/ppermute | solution.py:72
  508.2 38.6 %collective-permute-start.45 = (bf16[2,2,128,1152]{3,2,0,1:T(8,128)(2,1)}, bf16[2,2,128,1152]{3,2,0,1:T(8,128)(2,1)}, u32[]{:S(2)}, u32[]{:S(2)}) collective-permute-start(bf16[2,2,128,1152]{3,2,0,1:T(8,128)(2,1)} %copy.81), channel_id=1, source_target_pairs={{0,1},{1,0},{2,3},{3,2},{4,5},{5,4},{6,7},{7,6},{8,9},{9,8},{10,11... | collective-permute-start | bytes 3538952 | tf_op jit(solution)/shard_map/ppermute | solution.py:72
  547.8 213.9 %reduce-scatter.9.cloned.1.call-start = ((), (), s32[]{:S(2)}) async-start(), calls=%async_computation.10 | async-start | bytes 11796480 | tf_op jit(solution)/shard_map/reduce_scatter | solution.py:408
  550.4 28.9 %collective-permute-start.48 = (bf16[2,128,1152]{2,1,0:T(8,128)(2,1)}, bf16[2,128,1152]{2,1,0:T(8,128)(2,1)}, u32[]{:S(2)}, u32[]{:S(2)}) collective-permute-start(bf16[2,128,1152]{2,1,0:T(8,128)(2,1)} %slice_bitcast_fusion.3), channel_id=1, source_target_pairs={{0,4},{4,0},{1,5},{5,1},{2,6},{6,2},{3,7},{7,3},{8,12},{12,8},{9,1... | collective-permute-start | bytes 1769480 | tf_op jit(solution)/shard_map/ppermute | solution.py:72
  554.1 26.0 %collective-permute-start.47 = (bf16[2,128,1152]{2,1,0:T(8,128)(2,1)S(1)}, bf16[2,128,1152]{2,1,0:T(8,128)(2,1)}, u32[]{:S(2)}, u32[]{:S(2)}) collective-permute-start(bf16[2,128,1152]{2,1,0:T(8,128)(2,1)S(1)} %slice_bitcast_fusion.4), channel_id=1, source_target_pairs={{0,2},{2,0},{1,3},{3,1},{4,6},{6,4},{5,7},{7,5},{8,10},{10,8},{9,1... | collective-permute-start | bytes 1769480 | tf_op jit(solution)/shard_map/ppermute | solution.py:72
  619.4 31.5 %collective-permute-start.54 = (bf16[2,2,2,64,1280]{4,3,0,1,2:T(8,128)(2,1)S(1)}, bf16[2,2,2,64,1280]{4,3,0,1,2:T(8,128)(2,1)}, u32[]{:S(2)}, u32[]{:S(2)}) collective-permute-start(bf16[2,2,2,64,1280]{4,3,0,1,2:T(8,128)(2,1)S(1)} %dynamic-slice_bitcast_fusion), channel_id=1, source_target_pairs={{0,2},{2,0},{1,3},{3,1},{4,6},{6,4},{5,7},{7,5},{8,10},{10,8},{9,1... | collective-permute-start | bytes 3932168 | tf_op jit(solution)/shard_map/ppermute | solution.py:72
  624.9 25.0 %collective-permute-start.55 = (bf16[2,2,2,64,1024]{4,3,1,0,2:T(8,128)(2,1)S(1)}, bf16[2,2,2,64,1024]{4,3,1,0,2:T(8,128)(2,1)S(1)}, u32[]{:S(2)}, u32[]{:S(2)}) collective-permute-start(bf16[2,2,2,64,1024]{4,3,1,0,2:T(8,128)(2,1)S(1)} %dynamic-slice_bitcast_fusion.3), channel_id=1, source_target_pairs={{0,1},{1,0},{2,3},{3,2},{4,5},{5,4},{6,7},{7,6},{8,9},{9,8},{10,11... | collective-permute-start | bytes 3145736 | tf_op jit(solution)/shard_map/ppermute | solution.py:72
  650.9 204.9 %reduce-scatter.11.cloned.1.call-start = ((), (), s32[]{:S(2)}) async-start(), calls=%async_computation.11 | async-start | bytes 11796480 | tf_op jit(solution)/shard_map/reduce_scatter | solution.py:408
  665.0 21.1 %collective-permute-start.59 = (bf16[2,2,64,1280]{3,2,0,1:T(8,128)(2,1)S(1)}, bf16[2,2,64,1280]{3,2,0,1:T(8,128)(2,1)S(1)}, u32[]{:S(2)}, u32[]{:S(2)}) collective-permute-start(bf16[2,2,64,1280]{3,2,0,1:T(8,128)(2,1)S(1)} %dynamic-slice_bitcast_fusion.6), channel_id=1, source_target_pairs={{0,1},{1,0},{2,3},{3,2},{4,5},{5,4},{6,7},{7,6},{8,9},{9,8},{10,11... | collective-permute-start | bytes 1966088 | tf_op jit(solution)/shard_map/ppermute | solution.py:72
  665.2 20.9 %collective-permute-start.58 = (bf16[2,2,2,128,256]{4,3,0,1,2:T(8,128)(2,1)S(1)}, bf16[2,2,2,128,256]{4,3,0,1,2:T(8,128)(2,1)S(1)}, u32[]{:S(2)}, u32[]{:S(2)}) collective-permute-start(bf16[2,2,2,128,256]{4,3,0,1,2:T(8,128)(2,1)S(1)} %bitcast.670), channel_id=1, source_target_pairs={{0,2},{2,0},{1,3},{3,1},{4,6},{6,4},{5,7},{7,5},{8,10},{10,8},{9,1... | collective-permute-start | bytes 1572872 | tf_op jit(solution)/shard_map/ppermute | solution.py:72
  665.8 20.3 %collective-permute-start.57 = (bf16[2,2,2,128,256]{4,3,1,0,2:T(8,128)(2,1)S(1)}, bf16[2,2,2,128,256]{4,3,1,0,2:T(8,128)(2,1)S(1)}, u32[]{:S(2)}, u32[]{:S(2)}) collective-permute-start(bf16[2,2,2,128,256]{4,3,1,0,2:T(8,128)(2,1)S(1)} %bitcast.671), channel_id=1, source_target_pairs={{0,8},{8,0},{1,9},{9,1},{2,10},{10,2},{3,11},{11,3},{4,12},{12,4},... | collective-permute-start | bytes 1572872 | tf_op jit(solution)/shard_map/ppermute | solution.py:72
  693.8 38.6 %collective-permute-start.74 = (bf16[2,2,2,2,64,1024]{5,4,0,1,3,2:T(8,128)(2,1)S(1)}, bf16[2,2,2,2,64,1024]{5,4,0,1,3,2:T(8,128)(2,1)S(1)}, u32[]{:S(2)}, u32[]{:S(2)}) collective-permute-start(bf16[2,2,2,2,64,1024]{5,4,0,1,3,2:T(8,128)(2,1)S(1)} %bitcast.663), channel_id=1, source_target_pairs={{0,16},{16,0},{1,17},{17,1},{2,18},{18,2},{3,19},{19,3},{4,20},{20... | collective-permute-start | bytes 6291464 | tf_op jit(solution)/shard_map/ppermute | solution.py:72
  703.3 29.0 %collective-permute-start.75 = (bf16[2,2,2,2,64,1024]{5,4,1,0,2,3:T(8,128)(2,1)S(1)}, bf16[2,2,2,2,64,1024]{5,4,1,0,2,3:T(8,128)(2,1)S(1)}, u32[]{:S(2)}, u32[]{:S(2)}) collective-permute-start(bf16[2,2,2,2,64,1024]{5,4,1,0,2,3:T(8,128)(2,1)S(1)} %bitcast.662), channel_id=1, source_target_pairs={{0,16},{16,0},{1,17},{17,1},{2,18},{18,2},{3,19},{19,3},{4,20},{20... | collective-permute-start | bytes 6291464 | tf_op jit(solution)/shard_map/ppermute | solution.py:72
  734.7 23.9 %collective-permute-start.77 = (bf16[2,2,2,64,1024]{4,3,1,0,2:T(8,128)(2,1)}, bf16[2,2,2,64,1024]{4,3,1,0,2:T(8,128)(2,1)}, u32[]{:S(2)}, u32[]{:S(2)}) collective-permute-start(bf16[2,2,2,64,1024]{4,3,1,0,2:T(8,128)(2,1)} %dynamic-slice_bitcast_fusion.1), channel_id=1, source_target_pairs={{0,1},{1,0},{2,3},{3,2},{4,5},{5,4},{6,7},{7,6},{8,9},{9,8},{10,11... | collective-permute-start | bytes 3145736 | tf_op jit(solution)/shard_map/ppermute | solution.py:72
  737.8 23.9 %collective-permute-start.76 = (bf16[2,2,2,64,1024]{4,3,0,1,2:T(8,128)(2,1)}, bf16[2,2,2,64,1024]{4,3,0,1,2:T(8,128)(2,1)}, u32[]{:S(2)}, u32[]{:S(2)}) collective-permute-start(bf16[2,2,2,64,1024]{4,3,0,1,2:T(8,128)(2,1)} %dynamic-slice_bitcast_fusion.2), channel_id=1, source_target_pairs={{0,2},{2,0},{1,3},{3,1},{4,6},{6,4},{5,7},{7,5},{8,10},{10,8},{9,1... | collective-permute-start | bytes 3145736 | tf_op jit(solution)/shard_map/ppermute | solution.py:72
  764.3 19.8 %collective-permute-start.81 = (bf16[2,2,2,2,8,6784]{5,4,1,0,2,3:T(8,128)(2,1)S(1)}, bf16[2,2,2,2,8,6784]{5,4,1,0,2,3:T(8,128)(2,1)S(1)}, u32[]{:S(2)}, u32[]{:S(2)}) collective-permute-start(bf16[2,2,2,2,8,6784]{5,4,1,0,2,3:T(8,128)(2,1)S(1)} %bitcast.665), channel_id=1, source_target_pairs={{0,16},{16,0},{1,17},{17,1},{2,18},{18,2},{3,19},{19,3},{4,20},{20... | collective-permute-start | bytes 5210120 | tf_op jit(solution)/shard_map/ppermute | solution.py:72
  765.2 18.9 %collective-permute-start.80 = (bf16[2,2,2,2,64,768]{5,4,0,1,3,2:T(8,128)(2,1)S(1)}, bf16[2,2,2,2,64,768]{5,4,0,1,3,2:T(8,128)(2,1)S(1)}, u32[]{:S(2)}, u32[]{:S(2)}) collective-permute-start(bf16[2,2,2,2,64,768]{5,4,0,1,3,2:T(8,128)(2,1)S(1)} %bitcast.666), channel_id=1, source_target_pairs={{0,16},{16,0},{1,17},{17,1},{2,18},{18,2},{3,19},{19,3},{4,20},{20... | collective-permute-start | bytes 4718600 | tf_op jit(solution)/shard_map/ppermute | solution.py:72
  784.6 25.4 %collective-permute-start.85 = (bf16[2,2,2,8,6784]{4,3,1,0,2:T(8,128)(2,1)S(1)}, bf16[2,2,2,8,6784]{4,3,1,0,2:T(8,128)(2,1)S(1)}, u32[]{:S(2)}, u32[]{:S(2)}) collective-permute-start(bf16[2,2,2,8,6784]{4,3,1,0,2:T(8,128)(2,1)S(1)} %dynamic-slice_bitcast_fusion.4), channel_id=1, source_target_pairs={{0,1},{1,0},{2,3},{3,2},{4,5},{5,4},{6,7},{7,6},{8,9},{9,8},{10,11... | collective-permute-start | bytes 2605064 | tf_op jit(solution)/shard_map/ppermute | solution.py:72
  785.5 24.5 %collective-permute-start.84 = (bf16[2,2,2,64,768]{4,3,0,1,2:T(8,128)(2,1)S(1)}, bf16[2,2,2,64,768]{4,3,0,1,2:T(8,128)(2,1)S(1)}, u32[]{:S(2)}, u32[]{:S(2)}) collective-permute-start(bf16[2,2,2,64,768]{4,3,0,1,2:T(8,128)(2,1)S(1)} %dynamic-slice_bitcast_fusion.5), channel_id=1, source_target_pairs={{0,2},{2,0},{1,3},{3,1},{4,6},{6,4},{5,7},{7,5},{8,10},{10,8},{9,1... | collective-permute-start | bytes 2359304 | tf_op jit(solution)/shard_map/ppermute | solution.py:72
  789.3 19.6 %collective-permute-start.82 = (bf16[2,64,1024]{2,1,0:T(8,128)(2,1)S(1)}, bf16[2,64,1024]{2,1,0:T(8,128)(2,1)S(1)}, u32[]{:S(2)}, u32[]{:S(2)}) collective-permute-start(bf16[2,64,1024]{2,1,0:T(8,128)(2,1)S(1)} %dynamic-slice_bitcast_fusion.14), channel_id=1, source_target_pairs={{0,4},{4,0},{1,5},{5,1},{2,6},{6,2},{3,7},{7,3},{8,12},{12,8},{9,1... | collective-permute-start | bytes 786440 | tf_op jit(solution)/shard_map/ppermute | solution.py:72
  (198 other events, 1947.3 us)
Sparse Core Ops, SparseCore 0:
  27.5 72.0 all-gather.4
  101.7 64.0 all-gather.6
  168.0 64.5 all-gather.8
  330.1 86.9 all-gather.10
  429.2 118.2 reduce-scatter.4
  549.9 77.4 reduce-scatter.6
  651.1 91.4 reduce-scatter.8
  761.9 93.8 reduce-scatter.10

commit v4 on v3

--- a/solution.py
+++ b/solution.py
@@ -413,7 +413,7 @@
         product_rows(gate_late, rows_joined).astype(bf16),
     )
     arrived, (down_terms, gate_terms, mixed) = advance(*jobs, beside=(*work, mixed))
-    down_sum = scatter_units(tie(down_terms, mixed))
+    gate_sum = scatter_units(tie(gate_terms, mixed))
     up_terms = product_rows(tie(grad_up, arrived), rows_joined).astype(bf16)
     _, up_terms = advance(*jobs, beside=up_terms)
     mixed = mixed.astype(f32)
@@ -472,10 +472,10 @@
         scores_back.append(grad_scores)
         grad_keys = grad_keys + product_rows(grad_scores, query_rows) * score_scale
         grad_values = grad_values + product_rows(shares.astype(bf16), grad_rows)
-    _, (grad_keys, grad_values, down_sum) = advance(
-        *out_jobs, beside=(grad_keys.astype(bf16), grad_values.astype(bf16), down_sum)
-    )
-    gate_sum = scatter_units(tie(gate_terms, down_sum))
+    _, (grad_keys, grad_values, gate_sum) = advance(
+        *out_jobs, beside=(grad_keys.astype(bf16), grad_values.astype(bf16), gate_sum)
+    )
+    up_sum = scatter_units(tie(up_terms, gate_sum))
     kv_jobs = [
         Scatter(grad_keys, ("head", low) + upper + mid, row_axes),
         Scatter(grad_values, mid + (low,) + upper + ("head",), row_axes),
@@ -533,15 +533,16 @@
             axis=1,
         ),
     )
-    _, (last, gate_sum) = advance(*query_jobs, beside=(last, gate_sum))
-    up_sum = scatter_units(tie(up_terms, gate_sum))
+    _, (last, up_sum) = advance(*query_jobs, beside=(last, up_sum))
+    down_sum = scatter_units(tie(down_terms, up_sum))
     last_jobs = [scatter_weights(terms, order) for terms, order in zip(last, (backs[0], backs[2]))]
     for _ in range(steps - 1):
         arrived, _ = advance(*query_jobs, *last_jobs)
+    gate_sum, up_sum = tie((gate_sum, up_sum), arrived)
+    gateweight_grad, gateexpand_grad = pair_units(gate_sum, up_sum)
     arrived, _ = advance(*last_jobs)
-    down_sum, gate_sum, up_sum = tie((down_sum, gate_sum, up_sum), arrived)
+    down_sum = tie(down_sum, arrived)
     downweight_grad, downadapt_grad = down_sum[:, :D].astype(f32), down_sum[:, D:].astype(f32)
-    gateweight_grad, gateexpand_grad = pair_units(gate_sum, up_sum)
     advance(*last_jobs)
     kv_grad, expand_grad = last_jobs[0].result(), last_jobs[1].result()
     gains_grad = expand_grad[:, qkv_columns + 2 * D :]

time: 881 us -> 875 us (level)
    unnamed x330 -> x328, local copies, waits for them, and re-layouts: 35.6 us -> 35.5 us
  transfers between devices with their start and end apart: 102 -> 102, of which waited for: 55 -> 52; matrix products, arithmetic and copies ran while one was open for 39% -> 39% of each run, Pallas kernels for 0% -> 1%
where the time goes in v4:
time: 875 us; the launch traced here: 868 us
  waiting for transfers between devices  350 us (40%)
  matrix products  201 us (23%)
  starting transfers between devices  113 us (13%)
  other arithmetic  103 us (12%)
  local copies, waits for them, and re-layouts  75.2 us (9%)
  between operations  17.6 us (2%)
    ppermute x94, waiting for transfers between devices, shift(): return lax.ppermute(values, axes, [(i, i ^ mask) for i in range(size)])  341 us
    ppermute x94, starting transfers between devices, shift(): return lax.ppermute(values, axes, [(i, i ^ mask) for i in range(size)])  111 us
    dot_general x16, matrix products, product_back(): lax.dot_general(former, latter, (((1,), (1,)), ((), ())), preferred_eleme...  76.8 us
    dot_general x14, matrix products, product_rows(): lax.dot_general(former, latter, (((0,), (0,)), ((), ())), preferred_eleme...  62.7 us
    dot_general x17, matrix products, product(): return jnp.dot(former, latter, preferred_element_type=jnp.float32)  61.6 us
    another operation x75, other arithmetic, place(): jnp.stack([jnp.where(first, own, other), jnp.where(first, other, own)], a...  47.3 us
    unnamed x328, local copies, waits for them, and re-layouts  35.5 us
    convert_element_type x38, other arithmetic, finish(): self.value = self.value.astype(jnp.bfloat16)  22.4 us
  transfers between devices with their start and end apart: 102, of which 52 were waited for; matrix products, arithmetic and copies ran while one was open for 39% of the time, Pallas kernels for 1%

profile of v4, /device:TPU:0, one launch (start us, length us, event | category | flops | bytes accessed | tf_op | source)
XLA Modules:
  0.0 868.2 jit_solution(17690142821813970289)
XLA Ops:
  8.2 4.1 collective-permute-start.2
  19.9 4.1 collective-permute-done
  27.5 4.1 copy.56
  38.2 5.3 collective-permute-done.4
  45.2 8.4 collective-permute-done.6
  59.1 11.8 %collective-permute-done.8 = bf16[2,2,64,768]{3,2,1,0:T(8,128)(2,1)} collective-permute-done((bf16[2,2,64,768]{3,2,1,0:T(8,128)(2,1)}, bf16[2,2,64,768]{3,2,1,0:T(8,128)(2,1)}, u32[]{:S(2)}, u32[]{:S(2)}) %collective-permute-start.8) | collective-permute-done | bytes 393248 | tf_op jit(solution)/shard_map/ppermute | solution.py:72
  87.6 27.9 %collective-permute-done.12 = bf16[2,2,2,64,768]{4,3,2,1,0:T(8,128)(2,1)} collective-permute-done((bf16[2,2,2,64,768]{4,3,2,1,0:T(8,128)(2,1)S(1)}, bf16[2,2,2,64,768]{4,3,2,1,0:T(8,128)(2,1)}, u32[]{:S(2)}, u32[]{:S(2)}) %collective-permute-start.12) | collective-permute-done | bytes 786464 | tf_op jit(solution)/shard_map/ppermute | solution.py:72
  115.5 4.5 collective-permute-done.14
  162.2 3.6 all-gather.7.cloned.1.call-done
  174.8 6.1 collective-permute-done.25
  181.6 4.9 collective-permute-done.26
  193.2 13.9 %collective-permute-done.29 = bf16[2,2,128,256]{3,2,1,0:T(8,128)(2,1)S(1)} collective-permute-done((bf16[2,2,128,256]{3,2,1,0:T(8,128)(2,1)S(1)}, bf16[2,2,128,256]{3,2,1,0:T(8,128)(2,1)S(1)}, u32[]{:S(2)}, u32[]{:S(2)}) %collective-permute-start.29) | collective-permute-done | bytes 262176 | tf_op jit(solution)/shard_map/ppermute | solution.py:72
  220.3 31.8 %collective-permute-done.33 = bf16[2,2,2,128,256]{4,3,2,0,1:T(8,128)(2,1)} collective-permute-done((bf16[2,2,2,128,256]{4,3,2,0,1:T(8,128)(2,1)}, bf16[2,2,2,128,256]{4,3,2,0,1:T(8,128)(2,1)}, u32[]{:S(2)}, u32[]{:S(2)}) %collective-permute-start.33) | collective-permute-done | bytes 524320 | tf_op jit(solution)/shard_map/ppermute | solution.py:72
  266.8 3.6 fusion.8
  294.8 19.1 %collective-permute-done.38 = bf16[128,2048]{1,0:T(8,128)(2,1)S(1)} collective-permute-done((bf16[128,2048]{1,0:T(8,128)(2,1)S(1)}, bf16[128,2048]{1,0:T(8,128)(2,1)S(1)}, u32[]{:S(2)}, u32[]{:S(2)}) %collective-permute-start.38) | collective-permute-done | bytes 524320 | tf_op jit(solution)/shard_map/ppermute | solution.py:72
  313.9 16.1 %collective-permute-done.39 = bf16[128,2048]{1,0:T(8,128)(2,1)S(1)} collective-permute-done((bf16[128,2048]{1,0:T(8,128)(2,1)S(1)}, bf16[128,2048]{1,0:T(8,128)(2,1)S(1)}, u32[]{:S(2)}, u32[]{:S(2)}) %collective-permute-start.39) | collective-permute-done | bytes 524320 | tf_op jit(solution)/shard_map/ppermute | solution.py:72
  336.0 9.0 %collective-permute-done.42 = bf16[128,2048]{1,0:T(8,128)(2,1)S(1)} collective-permute-done((bf16[128,2048]{1,0:T(8,128)(2,1)S(1)}, bf16[128,2048]{1,0:T(8,128)(2,1)S(1)}, u32[]{:S(2)}, u32[]{:S(2)}) %collective-permute-start.42) | collective-permute-done | bytes 524320 | tf_op jit(solution)/shard_map/ppermute | solution.py:72
  345.8 16.0 %collective-permute-done.43 = bf16[128,2048]{1,0:T(8,128)(2,1)S(1)} collective-permute-done((bf16[128,2048]{1,0:T(8,128)(2,1)S(1)}, bf16[128,2048]{1,0:T(8,128)(2,1)S(1)}, u32[]{:S(2)}, u32[]{:S(2)}) %collective-permute-start.43) | collective-permute-done | bytes 524320 | tf_op jit(solution)/shard_map/ppermute | solution.py:72
  362.7 7.2 collective-permute-done.44
  370.8 3.9 convolution_convert_fusion.15
  374.7 14.7 %fusion.192 = f32[1024,2048]{1,0:T(8,128)} fusion(bf16[2048,2304]{1,0:T(8,128)(2,1)} %all-gather.7.cloned.1.call-done, bf16[1024,256]{1,0:T(8,128)(2,1)S(1)} %convolution_convert_fusion.15, bf16[1024,2048]{1,0:T(8,128)(2,1)S(1)} %copy-done.111), kind=kOutput, calls=%fused_computation.589 | convolution fusion | flops 9673113600 | bytes 22544384 | tf_op jit(solution)/shard_map/dot_general | solution.py:25
  389.4 19.2 %multiply_convert_fusion.2 = (bf16[1024,2048]{1,0:T(8,128)(2,1)}, f32[1024,2048]{1,0:T(8,128)}) fusion(f32[1024,2048]{1,0:T(8,128)} %fusion.192, bf16[2048,2304]{1,0:T(8,128)(2,1)} %all-gather.9.cloned.1.call-done, bf16[1024,256]{1,0:T(8,128)(2,1)S(1)} %convolution_convert_fusion.15, bf16[1024,2048]{1,0:T(8,128)(2,1)} %constant_dynamic-update-slice_fusion.8), kind=kOutput, calls=%fused_computation.17 | convolution fusion | flops 9694085120 | bytes 35127296 | tf_op jit(solution)/shard_map/dot_general | solution.py:25
  408.7 13.4 %convolution_convert_fusion.4 = bf16[1024,2304]{1,0:T(8,128)(2,1)S(1)} fusion(bf16[1024,2048]{1,0:T(8,128)(2,1)} %get-tuple-element.200, bf16[2048,2304]{1,0:T(8,128)(2,1)} %all-gather.5.cloned.1.call-done), kind=kOutput, calls=%fused_computation.23 | convolution fusion | flops 9666035712 | bytes 18350080 | tf_op jit(solution)/shard_map/dot_general | solution.py:21
  439.2 22.7 %fusion.6 = (bf16[1024,2048]{1,0:T(8,128)(2,1)}, bf16[1024,2048]{1,0:T(8,128)(2,1)}) fusion(f32[1024,2048]{1,0:T(8,128)} %fusion.192, f32[1024,2048]{1,0:T(8,128)} %get-tuple-element.443, bf16[2048,2304]{1,0:T(8,128)(2,1)} %all-gather.5.cloned.1.call-done, bf16[1024,256]{1,0:T(8,128)(2,1)S(1)} %copy.80, bf16[1024,2048]{1,0:T(8,128)(2,1)} %copy-done.114), kind=kOutput, calls=%fused_computation.14 | convolution fusion | flops 9723445248 | bytes 39321600 | tf_op jit(solution)/shard_map/dot_general | solution.py:25
  461.9 13.7 %fusion.218 = f32[1024,2304]{1,0:T(8,128)S(1)} fusion(bf16[1024,2048]{1,0:T(8,128)(2,1)} %get-tuple-element.206, bf16[2048,2304]{1,0:T(8,128)(2,1)} %all-gather.9.cloned.1.call-done), kind=kOutput, calls=%fused_computation.600 | convolution fusion | flops 9663676416 | bytes 23068672 | tf_op jit(solution)/shard_map/dot_general | solution.py:21
  475.6 12.2 %add_convert_fusion = bf16[1024,2304]{1,0:T(8,128)(2,1)S(1)} fusion(f32[1024,2304]{1,0:T(8,128)S(1)} %fusion.218, bf16[1024,2048]{1,0:T(8,128)(2,1)S(1)} %copy-done.134, bf16[2048,2304]{1,0:T(8,128)(2,1)} %all-gather.7.cloned.1.call-done), kind=kOutput, calls=%fused_computation.7 | convolution fusion | flops 9668395008 | bytes 27787264 | tf_op jit(solution)/shard_map/dot_general | solution.py:21
  489.3 17.6 %collective-permute-start.46 = (bf16[2,2,128,1152]{3,2,0,1:T(8,128)(2,1)}, bf16[2,2,128,1152]{3,2,0,1:T(8,128)(2,1)S(1)}, u32[]{:S(2)}, u32[]{:S(2)}) collective-permute-start(bf16[2,2,128,1152]{3,2,0,1:T(8,128)(2,1)} %bitcast.611), channel_id=1, source_target_pairs={{0,2},{2,0},{1,3},{3,1},{4,6},{6,4},{5,7},{7,5},{8,10},{10,8},{9,1... | collective-permute-start | bytes 3538952 | tf_op jit(solution)/shard_map/ppermute | solution.py:72
  508.8 13.0 %convolution_convert_fusion.1 = bf16[2048,2304]{1,0:T(8,128)(2,1)} fusion(bf16[1024,2048]{1,0:T(8,128)(2,1)S(1)} %copy-done.135, bf16[1024,256]{1,0:T(8,128)(2,1)S(1)} %copy-done.132, bf16[1024,2048]{1,0:T(8,128)(2,1)S(1)} %copy-done.112), kind=kOutput, calls=%fused_computation.5 | convolution fusion | flops 9677832192 | bytes 18350080 | tf_op jit(solution)/shard_map/dot_general | solution.py:31
  521.8 15.5 %convolution_convert_fusion.2 = bf16[2048,2304]{1,0:T(8,128)(2,1)} fusion(bf16[1024,2048]{1,0:T(8,128)(2,1)} %get-tuple-element.200, bf16[1024,256]{1,0:T(8,128)(2,1)} %copy-done.86, bf16[1024,2048]{1,0:T(8,128)(2,1)} %copy-done.114), kind=kOutput, calls=%fused_computation.6 | convolution fusion | flops 9677832192 | bytes 18350080 | tf_op jit(solution)/shard_map/dot_general | solution.py:31
  537.4 9.5 %collective-permute-done.46 = bf16[2,2,128,1152]{3,2,0,1:T(8,128)(2,1)S(1)} collective-permute-done((bf16[2,2,128,1152]{3,2,0,1:T(8,128)(2,1)}, bf16[2,2,128,1152]{3,2,0,1:T(8,128)(2,1)S(1)}, u32[]{:S(2)}, u32[]{:S(2)}) %collective-permute-start.46) | collective-permute-done | bytes 1179680 | tf_op jit(solution)/shard_map/ppermute | solution.py:72
  554.6 13.3 %convolution_convert_fusion = bf16[2048,2304]{1,0:T(8,128)(2,1)} fusion(bf16[1024,2048]{1,0:T(8,128)(2,1)S(1)} %copy-done.136, bf16[1024,256]{1,0:T(8,128)(2,1)S(1)} %copy-done.133, bf16[1024,2048]{1,0:T(8,128)(2,1)S(1)} %copy-done.113), kind=kOutput, calls=%fused_computation.4 | convolution fusion | flops 9677832192 | bytes 18350080 | tf_op jit(solution)/shard_map/dot_general | solution.py:31
  567.9 11.5 %collective-permute-done.48 = bf16[2,128,1152]{2,1,0:T(8,128)(2,1)} collective-permute-done((bf16[2,128,1152]{2,1,0:T(8,128)(2,1)}, bf16[2,128,1152]{2,1,0:T(8,128)(2,1)}, u32[]{:S(2)}, u32[]{:S(2)}) %collective-permute-start.48) | collective-permute-done | bytes 589856 | tf_op jit(solution)/shard_map/ppermute | solution.py:72
  588.5 9.5 %collective-permute-done.49 = bf16[128,1152]{1,0:T(8,128)(2,1)S(1)} collective-permute-done((bf16[128,1152]{1,0:T(8,128)(2,1)S(1)}, bf16[128,1152]{1,0:T(8,128)(2,1)S(1)}, u32[]{:S(2)}, u32[]{:S(2)}) %collective-permute-start.49) | collective-permute-done | bytes 294944 | tf_op jit(solution)/shard_map/ppermute | solution.py:72
  631.2 18.8 %collective-permute-done.55 = bf16[2,2,2,64,1024]{4,3,1,0,2:T(8,128)(2,1)S(1)} collective-permute-done((bf16[2,2,2,64,1024]{4,3,1,0,2:T(8,128)(2,1)S(1)}, bf16[2,2,2,64,1024]{4,3,1,0,2:T(8,128)(2,1)S(1)}, u32[]{:S(2)}, u32[]{:S(2)}) %collective-permute-start.55) | collective-permute-done | bytes 1048608 | tf_op jit(solution)/shard_map/ppermute | solution.py:72
  675.9 10.2 %collective-permute-done.58 = bf16[2,2,2,128,256]{4,3,0,1,2:T(8,128)(2,1)S(1)} collective-permute-done((bf16[2,2,2,128,256]{4,3,0,1,2:T(8,128)(2,1)S(1)}, bf16[2,2,2,128,256]{4,3,0,1,2:T(8,128)(2,1)S(1)}, u32[]{:S(2)}, u32[]{:S(2)}) %collective-permute-start.58) | collective-permute-done | bytes 524320 | tf_op jit(solution)/shard_map/ppermute | solution.py:72
  693.9 9.6 %collective-permute-done.66 = bf16[2,64,256]{2,1,0:T(8,128)(2,1)S(1)} collective-permute-done((bf16[2,64,256]{2,1,0:T(8,128)(2,1)S(1)}, bf16[2,64,256]{2,1,0:T(8,128)(2,1)S(1)}, u32[]{:S(2)}, u32[]{:S(2)}) %collective-permute-start.66) | collective-permute-done | bytes 65568 | tf_op jit(solution)/shard_map/ppermute | solution.py:72
  709.8 8.1 collective-permute-done.70
  721.3 3.9 collective-permute-done.67
  748.8 6.6 concatenate.134
  755.4 3.6 convolution_convert_fusion.9
  770.7 11.4 %collective-permute-done.79 = bf16[2,2,64,1024]{3,2,1,0:T(8,128)(2,1)S(1)} collective-permute-done((bf16[2,2,64,1024]{3,2,1,0:T(8,128)(2,1)S(1)}, bf16[2,2,64,1024]{3,2,1,0:T(8,128)(2,1)S(1)}, u32[]{:S(2)}, u32[]{:S(2)}) %collective-permute-start.79) | collective-permute-done | bytes 524320 | tf_op jit(solution)/shard_map/ppermute | solution.py:72
  790.9 10.8 %collective-permute-done.83 = bf16[2,64,1024]{2,1,0:T(8,128)(2,1)S(1)} collective-permute-done((bf16[2,64,1024]{2,1,0:T(8,128)(2,1)S(1)}, bf16[2,64,1024]{2,1,0:T(8,128)(2,1)S(1)}, u32[]{:S(2)}, u32[]{:S(2)}) %collective-permute-start.83) | collective-permute-done | bytes 262176 | tf_op jit(solution)/shard_map/ppermute | solution.py:72
  801.7 7.7 collective-permute-done.82
  818.1 3.9 collective-permute-done.87
  827.1 8.1 collective-permute-done.90
  838.7 8.1 shard_map.287
  851.0 4.3 reduce-scatter.11.cloned.1.call-done
  855.2 4.1 slice_convert_fusion
  (807 shorter events, 340.1 us)
Async XLA Ops:
  7.2 112.9 %all-gather.5.cloned.1.call-start = ((), (), s32[]{:S(2)}) async-start(), calls=%async_computation.4 | async-start | bytes 11796480 | tf_op jit(solution)/shard_map/all_gather | solution.py:250
  27.4 138.4 %all-gather.7.cloned.1.call-start = ((), (), s32[]{:S(2)}) async-start(), calls=%async_computation.5 | async-start | bytes 11796480 | tf_op jit(solution)/shard_map/all_gather | solution.py:250
  32.5 21.1 %collective-permute-start.6 = (bf16[2,64,1024]{2,1,0:T(8,128)(2,1)S(1)}, bf16[2,64,1024]{2,1,0:T(8,128)(2,1)S(1)}, u32[]{:S(2)}, u32[]{:S(2)}) collective-permute-start(bf16[2,64,1024]{2,1,0:T(8,128)(2,1)S(1)} %pad_maximum_fusion.42), channel_id=1, source_target_pairs={{0,8},{8,0},{1,9},{9,1},{2,10},{10,2},{3,11},{11,3},{4,12},{12,4},... | collective-permute-start | bytes 786440 | tf_op jit(solution)/shard_map/ppermute | solution.py:72
  54.5 18.8 %collective-permute-start.11 = (bf16[2,2,64,1024]{3,2,1,0:T(8,128)(2,1)}, bf16[2,2,64,1024]{3,2,1,0:T(8,128)(2,1)S(1)}, u32[]{:S(2)}, u32[]{:S(2)}) collective-permute-start(bf16[2,2,64,1024]{3,2,1,0:T(8,128)(2,1)} %pad_maximum_fusion.33), channel_id=1, source_target_pairs={{0,4},{4,0},{1,5},{5,1},{2,6},{6,2},{3,7},{7,3},{8,12},{12,8},{9,1... | collective-permute-start | bytes 1572872 | tf_op jit(solution)/shard_map/ppermute | solution.py:72
  55.4 19.2 %collective-permute-start.10 = (bf16[2,2,64,1024]{3,2,1,0:T(8,128)(2,1)}, bf16[2,2,64,1024]{3,2,1,0:T(8,128)(2,1)S(1)}, u32[]{:S(2)}, u32[]{:S(2)}) collective-permute-start(bf16[2,2,64,1024]{3,2,1,0:T(8,128)(2,1)} %pad_maximum_fusion.32), channel_id=1, source_target_pairs={{0,2},{2,0},{1,3},{3,1},{4,6},{6,4},{5,7},{7,5},{8,10},{10,8},{9,1... | collective-permute-start | bytes 1572872 | tf_op jit(solution)/shard_map/ppermute | solution.py:72
  75.9 39.6 %collective-permute-start.15 = (bf16[2,2,2,64,1024]{4,3,2,1,0:T(8,128)(2,1)}, bf16[2,2,2,64,1024]{4,3,2,1,0:T(8,128)(2,1)}, u32[]{:S(2)}, u32[]{:S(2)}) collective-permute-start(bf16[2,2,2,64,1024]{4,3,2,1,0:T(8,128)(2,1)} %pad_maximum_fusion.23), channel_id=1, source_target_pairs={{0,1},{1,0},{2,3},{3,2},{4,5},{5,4},{6,7},{7,6},{8,9},{9,8},{10,11... | collective-permute-start | bytes 3145736 | tf_op jit(solution)/shard_map/ppermute | solution.py:72
  78.4 41.6 %collective-permute-start.14 = (bf16[2,2,2,64,1024]{4,3,2,1,0:T(8,128)(2,1)}, bf16[2,2,2,64,1024]{4,3,2,1,0:T(8,128)(2,1)}, u32[]{:S(2)}, u32[]{:S(2)}) collective-permute-start(bf16[2,2,2,64,1024]{4,3,2,1,0:T(8,128)(2,1)} %pad_maximum_fusion.22), channel_id=1, source_target_pairs={{0,1},{1,0},{2,3},{3,2},{4,5},{5,4},{6,7},{7,6},{8,9},{9,8},{10,11... | collective-permute-start | bytes 3145736 | tf_op jit(solution)/shard_map/ppermute | solution.py:72
  80.4 35.1 %collective-permute-start.13 = (bf16[2,2,2,8,6784]{4,3,2,1,0:T(8,128)(2,1)}, bf16[2,2,2,8,6784]{4,3,2,1,0:T(8,128)(2,1)S(1)}, u32[]{:S(2)}, u32[]{:S(2)}) collective-permute-start(bf16[2,2,2,8,6784]{4,3,2,1,0:T(8,128)(2,1)} %pad_maximum_fusion.26), channel_id=1, source_target_pairs={{0,4},{4,0},{1,5},{5,1},{2,6},{6,2},{3,7},{7,3},{8,12},{12,8},{9,1... | collective-permute-start | bytes 2605064 | tf_op jit(solution)/shard_map/ppermute | solution.py:72
  81.6 33.9 %collective-permute-start.12 = (bf16[2,2,2,64,768]{4,3,2,1,0:T(8,128)(2,1)S(1)}, bf16[2,2,2,64,768]{4,3,2,1,0:T(8,128)(2,1)}, u32[]{:S(2)}, u32[]{:S(2)}) collective-permute-start(bf16[2,2,2,64,768]{4,3,2,1,0:T(8,128)(2,1)S(1)} %pad_maximum_fusion.27), channel_id=1, source_target_pairs={{0,2},{2,0},{1,3},{3,1},{4,6},{6,4},{5,7},{7,5},{8,10},{10,8},{9,1... | collective-permute-start | bytes 2359304 | tf_op jit(solution)/shard_map/ppermute | solution.py:72
  82.3 172.8 %all-gather.9.cloned.1.call-start = ((), (), s32[]{:S(2)}) async-start(), calls=%async_computation.6 | async-start | bytes 11796480 | tf_op jit(solution)/shard_map/all_gather | solution.py:250
  85.0 77.2 %collective-permute-start.20 = (bf16[64,1280]{1,0:T(8,128)(2,1)}, bf16[64,1280]{1,0:T(8,128)(2,1)}, u32[]{:S(2)}, u32[]{:S(2)}) collective-permute-start(bf16[64,1280]{1,0:T(8,128)(2,1)} %pad_maximum_fusion.48), channel_id=1, source_target_pairs={{0,8},{8,0},{1,9},{9,1},{2,10},{10,2},{3,11},{11,3},{4,12},{12,4},... | collective-permute-start | bytes 491528 | tf_op jit(solution)/shard_map/ppermute | solution.py:72
  127.0 35.2 %collective-permute-start.21 = (bf16[64,1280]{1,0:T(8,128)(2,1)}, bf16[64,1280]{1,0:T(8,128)(2,1)}, u32[]{:S(2)}, u32[]{:S(2)}) collective-permute-start(bf16[64,1280]{1,0:T(8,128)(2,1)} %pad_maximum_fusion.49), channel_id=1, source_target_pairs={{0,4},{4,0},{1,5},{5,1},{2,6},{6,2},{3,7},{7,3},{8,12},{12,8},{9,1... | collective-permute-start | bytes 491528 | tf_op jit(solution)/shard_map/ppermute | solution.py:72
  131.1 19.9 %collective-permute-start.23 = (bf16[2,2,2,2,64,1024]{5,4,3,2,1,0:T(8,128)(2,1)}, bf16[2,2,2,2,64,1024]{5,4,3,2,1,0:T(8,128)(2,1)}, u32[]{:S(2)}, u32[]{:S(2)}) collective-permute-start(bf16[2,2,2,2,64,1024]{5,4,3,2,1,0:T(8,128)(2,1)} %pad_maximum_fusion.16), channel_id=1, source_target_pairs={{0,16},{16,0},{1,17},{17,1},{2,18},{18,2},{3,19},{19,3},{4,20},{20... | collective-permute-start | bytes 6291464 | tf_op jit(solution)/shard_map/ppermute | solution.py:72
  165.9 263.2 %all-gather.11.cloned.1.call-start = ((), (), s32[]{:S(2)}) async-start(), calls=%async_computation.7 | async-start | bytes 4718592 | tf_op jit(solution)/shard_map/all_gather | solution.py:382
  186.6 23.0 %collective-permute-start.31 = (bf16[2,2,64,1280]{3,2,1,0:T(8,128)(2,1)S(1)}, bf16[2,2,64,1280]{3,2,1,0:T(8,128)(2,1)S(1)}, u32[]{:S(2)}, u32[]{:S(2)}) collective-permute-start(bf16[2,2,64,1280]{3,2,1,0:T(8,128)(2,1)S(1)} %pad_maximum_fusion.29), channel_id=1, source_target_pairs={{0,2},{2,0},{1,3},{3,1},{4,6},{6,4},{5,7},{7,5},{8,10},{10,8},{9,1... | collective-permute-start | bytes 1966088 | tf_op jit(solution)/shard_map/ppermute | solution.py:72
  187.5 22.1 %collective-permute-start.30 = (bf16[2,2,64,1280]{3,2,1,0:T(8,128)(2,1)S(1)}, bf16[2,2,64,1280]{3,2,1,0:T(8,128)(2,1)S(1)}, u32[]{:S(2)}, u32[]{:S(2)}) collective-permute-start(bf16[2,2,64,1280]{3,2,1,0:T(8,128)(2,1)S(1)} %pad_maximum_fusion.28), channel_id=1, source_target_pairs={{0,1},{1,0},{2,3},{3,2},{4,5},{5,4},{6,7},{7,6},{8,9},{9,8},{10,11... | collective-permute-start | bytes 1966088 | tf_op jit(solution)/shard_map/ppermute | solution.py:72
  210.9 43.4 %collective-permute-start.35 = (bf16[2,2,2,64,1280]{4,3,2,1,0:T(8,128)(2,1)}, bf16[2,2,2,64,1280]{4,3,2,1,0:T(8,128)(2,1)}, u32[]{:S(2)}, u32[]{:S(2)}) collective-permute-start(bf16[2,2,2,64,1280]{4,3,2,1,0:T(8,128)(2,1)} %pad_maximum_fusion.20), channel_id=1, source_target_pairs={{0,1},{1,0},{2,3},{3,2},{4,5},{5,4},{6,7},{7,6},{8,9},{9,8},{10,11... | collective-permute-start | bytes 3932168 | tf_op jit(solution)/shard_map/ppermute | solution.py:72
  213.6 41.4 %collective-permute-start.34 = (bf16[2,2,2,64,1280]{4,3,2,1,0:T(8,128)(2,1)}, bf16[2,2,2,64,1280]{4,3,2,1,0:T(8,128)(2,1)}, u32[]{:S(2)}, u32[]{:S(2)}) collective-permute-start(bf16[2,2,2,64,1280]{4,3,2,1,0:T(8,128)(2,1)} %pad_maximum_fusion.19), channel_id=1, source_target_pairs={{0,2},{2,0},{1,3},{3,1},{4,6},{6,4},{5,7},{7,5},{8,10},{10,8},{9,1... | collective-permute-start | bytes 3932168 | tf_op jit(solution)/shard_map/ppermute | solution.py:72
  216.4 35.7 %collective-permute-start.33 = (bf16[2,2,2,128,256]{4,3,2,0,1:T(8,128)(2,1)}, bf16[2,2,2,128,256]{4,3,2,0,1:T(8,128)(2,1)}, u32[]{:S(2)}, u32[]{:S(2)}) collective-permute-start(bf16[2,2,2,128,256]{4,3,2,0,1:T(8,128)(2,1)} %pad_maximum_fusion.36), channel_id=1, source_target_pairs={{0,1},{1,0},{2,3},{3,2},{4,5},{5,4},{6,7},{7,6},{8,9},{9,8},{10,11... | collective-permute-start | bytes 1572872 | tf_op jit(solution)/shard_map/ppermute | solution.py:72
  217.9 36.4 %collective-permute-start.32 = (bf16[2,2,2,128,256]{4,3,0,1,2:T(8,128)(2,1)}, bf16[2,2,2,128,256]{4,3,0,1,2:T(8,128)(2,1)}, u32[]{:S(2)}, u32[]{:S(2)}) collective-permute-start(bf16[2,2,2,128,256]{4,3,0,1,2:T(8,128)(2,1)} %pad_maximum_fusion.35), channel_id=1, source_target_pairs={{0,4},{4,0},{1,5},{5,1},{2,6},{6,2},{3,7},{7,3},{8,12},{12,8},{9,1... | collective-permute-start | bytes 1572872 | tf_op jit(solution)/shard_map/ppermute | solution.py:72
  288.9 25.0 %collective-permute-start.38 = (bf16[128,2048]{1,0:T(8,128)(2,1)S(1)}, bf16[128,2048]{1,0:T(8,128)(2,1)S(1)}, u32[]{:S(2)}, u32[]{:S(2)}) collective-permute-start(bf16[128,2048]{1,0:T(8,128)(2,1)S(1)} %get-tuple-element.304), channel_id=1, source_target_pairs={{0,2},{2,0},{4,6},{6,4},{1,3},{3,1},{5,7},{7,5},{8,10},{10,8},{12,... | collective-permute-start | bytes 1572872 | tf_op jit(solution)/shard_map/ppermute | solution.py:72
  291.8 38.2 %collective-permute-start.39 = (bf16[128,2048]{1,0:T(8,128)(2,1)S(1)}, bf16[128,2048]{1,0:T(8,128)(2,1)S(1)}, u32[]{:S(2)}, u32[]{:S(2)}) collective-permute-start(bf16[128,2048]{1,0:T(8,128)(2,1)S(1)} %get-tuple-element.304), channel_id=1, source_target_pairs={{0,4},{2,6},{4,0},{6,2},{1,5},{3,7},{5,1},{7,3},{8,12},{10,14},{12... | collective-permute-start | bytes 1572872 | tf_op jit(solution)/shard_map/ppermute | solution.py:72
  292.4 37.6 %collective-permute-start.40 = (bf16[128,2048]{1,0:T(8,128)(2,1)S(1)}, bf16[128,2048]{1,0:T(8,128)(2,1)S(1)}, u32[]{:S(2)}, u32[]{:S(2)}) collective-permute-start(bf16[128,2048]{1,0:T(8,128)(2,1)S(1)} %get-tuple-element.304), channel_id=1, source_target_pairs={{0,6},{2,4},{4,2},{6,0},{1,7},{3,5},{5,3},{7,1},{8,14},{10,12},{12... | collective-permute-start | bytes 1572872 | tf_op jit(solution)/shard_map/ppermute | solution.py:72
  294.2 41.0 %collective-permute-start.41 = (bf16[128,2048]{1,0:T(8,128)(2,1)S(1)}, bf16[128,2048]{1,0:T(8,128)(2,1)S(1)}, u32[]{:S(2)}, u32[]{:S(2)}) collective-permute-start(bf16[128,2048]{1,0:T(8,128)(2,1)S(1)} %get-tuple-element.304), channel_id=1, source_target_pairs={{0,1},{1,0},{2,3},{3,2},{4,5},{5,4},{6,7},{7,6},{8,9},{9,8},{10,11... | collective-permute-start | bytes 1572872 | tf_op jit(solution)/shard_map/ppermute | solution.py:72
  330.0 217.6 %reduce-scatter.5.cloned.1.call-start = ((), (), s32[]{:S(2)}) async-start(), calls=%async_computation.8 | async-start | bytes 5308416 | tf_op jit(solution)/shard_map/reduce_scatter | solution.py:391
  330.7 31.2 %collective-permute-start.43 = (bf16[128,2048]{1,0:T(8,128)(2,1)S(1)}, bf16[128,2048]{1,0:T(8,128)(2,1)S(1)}, u32[]{:S(2)}, u32[]{:S(2)}) collective-permute-start(bf16[128,2048]{1,0:T(8,128)(2,1)S(1)} %collective-permute-done.39), channel_id=1, source_target_pairs={{0,1},{1,0},{2,3},{3,2},{4,5},{5,4},{6,7},{7,6},{8,9},{9,8},{10,11... | collective-permute-start | bytes 1572872 | tf_op jit(solution)/shard_map/ppermute | solution.py:72
  332.2 37.8 %collective-permute-start.44 = (bf16[128,2048]{1,0:T(8,128)(2,1)S(1)}, bf16[128,2048]{1,0:T(8,128)(2,1)S(1)}, u32[]{:S(2)}, u32[]{:S(2)}) collective-permute-start(bf16[128,2048]{1,0:T(8,128)(2,1)S(1)} %collective-permute-done.40), channel_id=1, source_target_pairs={{0,1},{1,0},{2,3},{3,2},{4,5},{5,4},{6,7},{7,6},{8,9},{9,8},{10,11... | collective-permute-start | bytes 1572872 | tf_op jit(solution)/shard_map/ppermute | solution.py:72
  429.1 221.9 %reduce-scatter.7.cloned.1.call-start = ((), (), s32[]{:S(2)}) async-start(), calls=%async_computation.9 | async-start | bytes 11796480 | tf_op jit(solution)/shard_map/reduce_scatter | solution.py:408
  489.3 57.5 %collective-permute-start.46 = (bf16[2,2,128,1152]{3,2,0,1:T(8,128)(2,1)}, bf16[2,2,128,1152]{3,2,0,1:T(8,128)(2,1)S(1)}, u32[]{:S(2)}, u32[]{:S(2)}) collective-permute-start(bf16[2,2,128,1152]{3,2,0,1:T(8,128)(2,1)} %bitcast.611), channel_id=1, source_target_pairs={{0,2},{2,0},{1,3},{3,1},{4,6},{6,4},{5,7},{7,5},{8,10},{10,8},{9,1... | collective-permute-start | bytes 3538952 | tf_op jit(solution)/shard_map/ppermute | solution.py:72
  508.2 38.6 %collective-permute-start.45 = (bf16[2,2,128,1152]{3,2,0,1:T(8,128)(2,1)}, bf16[2,2,128,1152]{3,2,0,1:T(8,128)(2,1)}, u32[]{:S(2)}, u32[]{:S(2)}) collective-permute-start(bf16[2,2,128,1152]{3,2,0,1:T(8,128)(2,1)} %copy.81), channel_id=1, source_target_pairs={{0,1},{1,0},{2,3},{3,2},{4,5},{5,4},{6,7},{7,6},{8,9},{9,8},{10,11... | collective-permute-start | bytes 3538952 | tf_op jit(solution)/shard_map/ppermute | solution.py:72
  547.9 213.8 %reduce-scatter.9.cloned.1.call-start = ((), (), s32[]{:S(2)}) async-start(), calls=%async_computation.10 | async-start | bytes 11796480 | tf_op jit(solution)/shard_map/reduce_scatter | solution.py:408
  550.5 28.9 %collective-permute-start.48 = (bf16[2,128,1152]{2,1,0:T(8,128)(2,1)}, bf16[2,128,1152]{2,1,0:T(8,128)(2,1)}, u32[]{:S(2)}, u32[]{:S(2)}) collective-permute-start(bf16[2,128,1152]{2,1,0:T(8,128)(2,1)} %slice_bitcast_fusion.3), channel_id=1, source_target_pairs={{0,4},{4,0},{1,5},{5,1},{2,6},{6,2},{3,7},{7,3},{8,12},{12,8},{9,1... | collective-permute-start | bytes 1769480 | tf_op jit(solution)/shard_map/ppermute | solution.py:72
  554.1 26.0 %collective-permute-start.47 = (bf16[2,128,1152]{2,1,0:T(8,128)(2,1)S(1)}, bf16[2,128,1152]{2,1,0:T(8,128)(2,1)}, u32[]{:S(2)}, u32[]{:S(2)}) collective-permute-start(bf16[2,128,1152]{2,1,0:T(8,128)(2,1)S(1)} %slice_bitcast_fusion.4), channel_id=1, source_target_pairs={{0,2},{2,0},{1,3},{3,1},{4,6},{6,4},{5,7},{7,5},{8,10},{10,8},{9,1... | collective-permute-start | bytes 1769480 | tf_op jit(solution)/shard_map/ppermute | solution.py:72
  619.5 31.6 %collective-permute-start.54 = (bf16[2,2,2,64,1280]{4,3,0,1,2:T(8,128)(2,1)S(1)}, bf16[2,2,2,64,1280]{4,3,0,1,2:T(8,128)(2,1)}, u32[]{:S(2)}, u32[]{:S(2)}) collective-permute-start(bf16[2,2,2,64,1280]{4,3,0,1,2:T(8,128)(2,1)S(1)} %dynamic-slice_bitcast_fusion), channel_id=1, source_target_pairs={{0,2},{2,0},{1,3},{3,1},{4,6},{6,4},{5,7},{7,5},{8,10},{10,8},{9,1... | collective-permute-start | bytes 3932168 | tf_op jit(solution)/shard_map/ppermute | solution.py:72
  625.0 25.0 %collective-permute-start.55 = (bf16[2,2,2,64,1024]{4,3,1,0,2:T(8,128)(2,1)S(1)}, bf16[2,2,2,64,1024]{4,3,1,0,2:T(8,128)(2,1)S(1)}, u32[]{:S(2)}, u32[]{:S(2)}) collective-permute-start(bf16[2,2,2,64,1024]{4,3,1,0,2:T(8,128)(2,1)S(1)} %dynamic-slice_bitcast_fusion.3), channel_id=1, source_target_pairs={{0,1},{1,0},{2,3},{3,2},{4,5},{5,4},{6,7},{7,6},{8,9},{9,8},{10,11... | collective-permute-start | bytes 3145736 | tf_op jit(solution)/shard_map/ppermute | solution.py:72
  651.1 204.2 %reduce-scatter.11.cloned.1.call-start = ((), (), s32[]{:S(2)}) async-start(), calls=%async_computation.11 | async-start | bytes 11796480 | tf_op jit(solution)/shard_map/reduce_scatter | solution.py:408
  665.1 21.1 %collective-permute-start.59 = (bf16[2,2,64,1280]{3,2,0,1:T(8,128)(2,1)S(1)}, bf16[2,2,64,1280]{3,2,0,1:T(8,128)(2,1)S(1)}, u32[]{:S(2)}, u32[]{:S(2)}) collective-permute-start(bf16[2,2,64,1280]{3,2,0,1:T(8,128)(2,1)S(1)} %dynamic-slice_bitcast_fusion.6), channel_id=1, source_target_pairs={{0,1},{1,0},{2,3},{3,2},{4,5},{5,4},{6,7},{7,6},{8,9},{9,8},{10,11... | collective-permute-start | bytes 1966088 | tf_op jit(solution)/shard_map/ppermute | solution.py:72
  665.5 20.7 %collective-permute-start.58 = (bf16[2,2,2,128,256]{4,3,0,1,2:T(8,128)(2,1)S(1)}, bf16[2,2,2,128,256]{4,3,0,1,2:T(8,128)(2,1)S(1)}, u32[]{:S(2)}, u32[]{:S(2)}) collective-permute-start(bf16[2,2,2,128,256]{4,3,0,1,2:T(8,128)(2,1)S(1)} %bitcast.670), channel_id=1, source_target_pairs={{0,2},{2,0},{1,3},{3,1},{4,6},{6,4},{5,7},{7,5},{8,10},{10,8},{9,1... | collective-permute-start | bytes 1572872 | tf_op jit(solution)/shard_map/ppermute | solution.py:72
  665.9 20.3 %collective-permute-start.57 = (bf16[2,2,2,128,256]{4,3,1,0,2:T(8,128)(2,1)S(1)}, bf16[2,2,2,128,256]{4,3,1,0,2:T(8,128)(2,1)S(1)}, u32[]{:S(2)}, u32[]{:S(2)}) collective-permute-start(bf16[2,2,2,128,256]{4,3,1,0,2:T(8,128)(2,1)S(1)} %bitcast.671), channel_id=1, source_target_pairs={{0,8},{8,0},{1,9},{9,1},{2,10},{10,2},{3,11},{11,3},{4,12},{12,4},... | collective-permute-start | bytes 1572872 | tf_op jit(solution)/shard_map/ppermute | solution.py:72
  703.5 28.3 %collective-permute-start.74 = (bf16[2,2,2,2,64,1024]{5,4,0,1,3,2:T(8,128)(2,1)S(1)}, bf16[2,2,2,2,64,1024]{5,4,0,1,3,2:T(8,128)(2,1)S(1)}, u32[]{:S(2)}, u32[]{:S(2)}) collective-permute-start(bf16[2,2,2,2,64,1024]{5,4,0,1,3,2:T(8,128)(2,1)S(1)} %bitcast.663), channel_id=1, source_target_pairs={{0,16},{16,0},{1,17},{17,1},{2,18},{18,2},{3,19},{19,3},{4,20},{20... | collective-permute-start | bytes 6291464 | tf_op jit(solution)/shard_map/ppermute | solution.py:72
  703.5 28.3 %collective-permute-start.75 = (bf16[2,2,2,2,64,1024]{5,4,1,0,2,3:T(8,128)(2,1)S(1)}, bf16[2,2,2,2,64,1024]{5,4,1,0,2,3:T(8,128)(2,1)S(1)}, u32[]{:S(2)}, u32[]{:S(2)}) collective-permute-start(bf16[2,2,2,2,64,1024]{5,4,1,0,2,3:T(8,128)(2,1)S(1)} %bitcast.662), channel_id=1, source_target_pairs={{0,16},{16,0},{1,17},{17,1},{2,18},{18,2},{3,19},{19,3},{4,20},{20... | collective-permute-start | bytes 6291464 | tf_op jit(solution)/shard_map/ppermute | solution.py:72
  734.1 24.9 %collective-permute-start.77 = (bf16[2,2,2,64,1024]{4,3,1,0,2:T(8,128)(2,1)}, bf16[2,2,2,64,1024]{4,3,1,0,2:T(8,128)(2,1)}, u32[]{:S(2)}, u32[]{:S(2)}) collective-permute-start(bf16[2,2,2,64,1024]{4,3,1,0,2:T(8,128)(2,1)} %dynamic-slice_bitcast_fusion.1), channel_id=1, source_target_pairs={{0,1},{1,0},{2,3},{3,2},{4,5},{5,4},{6,7},{7,6},{8,9},{9,8},{10,11... | collective-permute-start | bytes 3145736 | tf_op jit(solution)/shard_map/ppermute | solution.py:72
  738.2 23.5 %collective-permute-start.76 = (bf16[2,2,2,64,1024]{4,3,0,1,2:T(8,128)(2,1)}, bf16[2,2,2,64,1024]{4,3,0,1,2:T(8,128)(2,1)}, u32[]{:S(2)}, u32[]{:S(2)}) collective-permute-start(bf16[2,2,2,64,1024]{4,3,0,1,2:T(8,128)(2,1)} %dynamic-slice_bitcast_fusion.2), channel_id=1, source_target_pairs={{0,2},{2,0},{1,3},{3,1},{4,6},{6,4},{5,7},{7,5},{8,10},{10,8},{9,1... | collective-permute-start | bytes 3145736 | tf_op jit(solution)/shard_map/ppermute | solution.py:72
  764.2 19.7 %collective-permute-start.81 = (bf16[2,2,2,2,8,6784]{5,4,1,0,2,3:T(8,128)(2,1)S(1)}, bf16[2,2,2,2,8,6784]{5,4,1,0,2,3:T(8,128)(2,1)S(1)}, u32[]{:S(2)}, u32[]{:S(2)}) collective-permute-start(bf16[2,2,2,2,8,6784]{5,4,1,0,2,3:T(8,128)(2,1)S(1)} %bitcast.665), channel_id=1, source_target_pairs={{0,16},{16,0},{1,17},{17,1},{2,18},{18,2},{3,19},{19,3},{4,20},{20... | collective-permute-start | bytes 5210120 | tf_op jit(solution)/shard_map/ppermute | solution.py:72
  765.2 18.8 %collective-permute-start.80 = (bf16[2,2,2,2,64,768]{5,4,0,1,3,2:T(8,128)(2,1)S(1)}, bf16[2,2,2,2,64,768]{5,4,0,1,3,2:T(8,128)(2,1)S(1)}, u32[]{:S(2)}, u32[]{:S(2)}) collective-permute-start(bf16[2,2,2,2,64,768]{5,4,0,1,3,2:T(8,128)(2,1)S(1)} %bitcast.666), channel_id=1, source_target_pairs={{0,16},{16,0},{1,17},{17,1},{2,18},{18,2},{3,19},{19,3},{4,20},{20... | collective-permute-start | bytes 4718600 | tf_op jit(solution)/shard_map/ppermute | solution.py:72
  784.4 25.8 %collective-permute-start.85 = (bf16[2,2,2,8,6784]{4,3,1,0,2:T(8,128)(2,1)S(1)}, bf16[2,2,2,8,6784]{4,3,1,0,2:T(8,128)(2,1)S(1)}, u32[]{:S(2)}, u32[]{:S(2)}) collective-permute-start(bf16[2,2,2,8,6784]{4,3,1,0,2:T(8,128)(2,1)S(1)} %dynamic-slice_bitcast_fusion.4), channel_id=1, source_target_pairs={{0,1},{1,0},{2,3},{3,2},{4,5},{5,4},{6,7},{7,6},{8,9},{9,8},{10,11... | collective-permute-start | bytes 2605064 | tf_op jit(solution)/shard_map/ppermute | solution.py:72
  785.3 24.9 %collective-permute-start.84 = (bf16[2,2,2,64,768]{4,3,0,1,2:T(8,128)(2,1)S(1)}, bf16[2,2,2,64,768]{4,3,0,1,2:T(8,128)(2,1)S(1)}, u32[]{:S(2)}, u32[]{:S(2)}) collective-permute-start(bf16[2,2,2,64,768]{4,3,0,1,2:T(8,128)(2,1)S(1)} %dynamic-slice_bitcast_fusion.5), channel_id=1, source_target_pairs={{0,2},{2,0},{1,3},{3,1},{4,6},{6,4},{5,7},{7,5},{8,10},{10,8},{9,1... | collective-permute-start | bytes 2359304 | tf_op jit(solution)/shard_map/ppermute | solution.py:72
  789.3 20.1 %collective-permute-start.82 = (bf16[2,64,1024]{2,1,0:T(8,128)(2,1)S(1)}, bf16[2,64,1024]{2,1,0:T(8,128)(2,1)S(1)}, u32[]{:S(2)}, u32[]{:S(2)}) collective-permute-start(bf16[2,64,1024]{2,1,0:T(8,128)(2,1)S(1)} %dynamic-slice_bitcast_fusion.14), channel_id=1, source_target_pairs={{0,4},{4,0},{1,5},{5,1},{2,6},{6,2},{3,7},{7,3},{8,12},{12,8},{9,1... | collective-permute-start | bytes 786440 | tf_op jit(solution)/shard_map/ppermute | solution.py:72
  (197 other events, 1930.0 us)
Sparse Core Ops, SparseCore 0:
  27.5 72.0 all-gather.4
  101.7 64.0 all-gather.6
  168.0 64.5 all-gather.8
  330.1 86.9 all-gather.10
  429.2 118.3 reduce-scatter.4
  550.0 77.2 reduce-scatter.6
  651.2 91.2 reduce-scatter.8
  761.9 93.3 reduce-scatter.10

commit v5 on v4

--- a/solution.py
+++ b/solution.py
@@ -536,7 +536,9 @@
     _, (last, up_sum) = advance(*query_jobs, beside=(last, up_sum))
     down_sum = scatter_units(tie(down_terms, up_sum))
     last_jobs = [scatter_weights(terms, order) for terms, order in zip(last, (backs[0], backs[2]))]
-    for _ in range(steps - 1):
+    advance(*last_jobs)
+    advance(*query_jobs)
+    for _ in range(steps - 2):
         arrived, _ = advance(*query_jobs, *last_jobs)
     gate_sum, up_sum = tie((gate_sum, up_sum), arrived)
     gateweight_grad, gateexpand_grad = pair_units(gate_sum, up_sum)

time: 875 us -> 874 us (level)
  no operation moved by 1% of the time
where the time goes in v5:
time: 874 us; the launch traced here: 867 us
  waiting for transfers between devices  350 us (40%)
  matrix products  201 us (23%)
  starting transfers between devices  112 us (13%)
  other arithmetic  103 us (12%)
  local copies, waits for them, and re-layouts  75.2 us (9%)
  between operations  17.6 us (2%)
    ppermute x94, waiting for transfers between devices, shift(): return lax.ppermute(values, axes, [(i, i ^ mask) for i in range(size)])  343 us
    ppermute x94, starting transfers between devices, shift(): return lax.ppermute(values, axes, [(i, i ^ mask) for i in range(size)])  110 us
    dot_general x16, matrix products, product_back(): lax.dot_general(former, latter, (((1,), (1,)), ((), ())), preferred_eleme...  76.8 us
    dot_general x14, matrix products, product_rows(): lax.dot_general(former, latter, (((0,), (0,)), ((), ())), preferred_eleme...  62.7 us
    dot_general x17, matrix products, product(): return jnp.dot(former, latter, preferred_element_type=jnp.float32)  61.6 us
    another operation x75, other arithmetic, place(): jnp.stack([jnp.where(first, own, other), jnp.where(first, other, own)], a...  47.3 us
    unnamed x328, local copies, waits for them, and re-layouts  35.5 us
    convert_element_type x38, other arithmetic, finish(): self.value = self.value.astype(jnp.bfloat16)  22.4 us
  transfers between devices with their start and end apart: 102, of which 52 were waited for; matrix products, arithmetic and copies ran while one was open for 39% of the time, Pallas kernels for 1%

profile of v5, /device:TPU:0, one launch (start us, length us, event | category | flops | bytes accessed | tf_op | source)
XLA Modules:
  0.0 866.8 jit_solution(7219765456647727664)
XLA Ops:
  8.2 4.1 collective-permute-start.2
  19.9 4.1 collective-permute-done
  27.5 4.1 copy.56
  38.2 5.3 collective-permute-done.4
  45.2 8.4 collective-permute-done.6
  59.1 11.8 %collective-permute-done.8 = bf16[2,2,64,768]{3,2,1,0:T(8,128)(2,1)} collective-permute-done((bf16[2,2,64,768]{3,2,1,0:T(8,128)(2,1)}, bf16[2,2,64,768]{3,2,1,0:T(8,128)(2,1)}, u32[]{:S(2)}, u32[]{:S(2)}) %collective-permute-start.8) | collective-permute-done | bytes 393248 | tf_op jit(solution)/shard_map/ppermute | solution.py:72
  87.6 27.9 %collective-permute-done.12 = bf16[2,2,2,64,768]{4,3,2,1,0:T(8,128)(2,1)} collective-permute-done((bf16[2,2,2,64,768]{4,3,2,1,0:T(8,128)(2,1)S(1)}, bf16[2,2,2,64,768]{4,3,2,1,0:T(8,128)(2,1)}, u32[]{:S(2)}, u32[]{:S(2)}) %collective-permute-start.12) | collective-permute-done | bytes 786464 | tf_op jit(solution)/shard_map/ppermute | solution.py:72
  115.5 4.5 collective-permute-done.14
  162.2 3.6 all-gather.7.cloned.1.call-done
  174.8 6.1 collective-permute-done.25
  181.6 4.9 collective-permute-done.26
  193.2 13.9 %collective-permute-done.29 = bf16[2,2,128,256]{3,2,1,0:T(8,128)(2,1)S(1)} collective-permute-done((bf16[2,2,128,256]{3,2,1,0:T(8,128)(2,1)S(1)}, bf16[2,2,128,256]{3,2,1,0:T(8,128)(2,1)S(1)}, u32[]{:S(2)}, u32[]{:S(2)}) %collective-permute-start.29) | collective-permute-done | bytes 262176 | tf_op jit(solution)/shard_map/ppermute | solution.py:72
  220.3 31.8 %collective-permute-done.33 = bf16[2,2,2,128,256]{4,3,2,0,1:T(8,128)(2,1)} collective-permute-done((bf16[2,2,2,128,256]{4,3,2,0,1:T(8,128)(2,1)}, bf16[2,2,2,128,256]{4,3,2,0,1:T(8,128)(2,1)}, u32[]{:S(2)}, u32[]{:S(2)}) %collective-permute-start.33) | collective-permute-done | bytes 524320 | tf_op jit(solution)/shard_map/ppermute | solution.py:72
  266.8 3.6 fusion.8
  294.8 19.1 %collective-permute-done.38 = bf16[128,2048]{1,0:T(8,128)(2,1)S(1)} collective-permute-done((bf16[128,2048]{1,0:T(8,128)(2,1)S(1)}, bf16[128,2048]{1,0:T(8,128)(2,1)S(1)}, u32[]{:S(2)}, u32[]{:S(2)}) %collective-permute-start.38) | collective-permute-done | bytes 524320 | tf_op jit(solution)/shard_map/ppermute | solution.py:72
  313.9 16.1 %collective-permute-done.39 = bf16[128,2048]{1,0:T(8,128)(2,1)S(1)} collective-permute-done((bf16[128,2048]{1,0:T(8,128)(2,1)S(1)}, bf16[128,2048]{1,0:T(8,128)(2,1)S(1)}, u32[]{:S(2)}, u32[]{:S(2)}) %collective-permute-start.39) | collective-permute-done | bytes 524320 | tf_op jit(solution)/shard_map/ppermute | solution.py:72
  336.0 9.0 %collective-permute-done.42 = bf16[128,2048]{1,0:T(8,128)(2,1)S(1)} collective-permute-done((bf16[128,2048]{1,0:T(8,128)(2,1)S(1)}, bf16[128,2048]{1,0:T(8,128)(2,1)S(1)}, u32[]{:S(2)}, u32[]{:S(2)}) %collective-permute-start.42) | collective-permute-done | bytes 524320 | tf_op jit(solution)/shard_map/ppermute | solution.py:72
  345.8 16.0 %collective-permute-done.43 = bf16[128,2048]{1,0:T(8,128)(2,1)S(1)} collective-permute-done((bf16[128,2048]{1,0:T(8,128)(2,1)S(1)}, bf16[128,2048]{1,0:T(8,128)(2,1)S(1)}, u32[]{:S(2)}, u32[]{:S(2)}) %collective-permute-start.43) | collective-permute-done | bytes 524320 | tf_op jit(solution)/shard_map/ppermute | solution.py:72
  362.7 7.2 collective-permute-done.44
  370.8 3.9 convolution_convert_fusion.15
  374.7 14.7 %fusion.192 = f32[1024,2048]{1,0:T(8,128)} fusion(bf16[2048,2304]{1,0:T(8,128)(2,1)} %all-gather.7.cloned.1.call-done, bf16[1024,256]{1,0:T(8,128)(2,1)S(1)} %convolution_convert_fusion.15, bf16[1024,2048]{1,0:T(8,128)(2,1)S(1)} %copy-done.111), kind=kOutput, calls=%fused_computation.589 | convolution fusion | flops 9673113600 | bytes 22544384 | tf_op jit(solution)/shard_map/dot_general | solution.py:25
  389.4 19.2 %multiply_convert_fusion.2 = (bf16[1024,2048]{1,0:T(8,128)(2,1)}, f32[1024,2048]{1,0:T(8,128)}) fusion(f32[1024,2048]{1,0:T(8,128)} %fusion.192, bf16[2048,2304]{1,0:T(8,128)(2,1)} %all-gather.9.cloned.1.call-done, bf16[1024,256]{1,0:T(8,128)(2,1)S(1)} %convolution_convert_fusion.15, bf16[1024,2048]{1,0:T(8,128)(2,1)} %constant_dynamic-update-slice_fusion.8), kind=kOutput, calls=%fused_computation.17 | convolution fusion | flops 9694085120 | bytes 35127296 | tf_op jit(solution)/shard_map/dot_general | solution.py:25
  408.7 13.4 %convolution_convert_fusion.4 = bf16[1024,2304]{1,0:T(8,128)(2,1)S(1)} fusion(bf16[1024,2048]{1,0:T(8,128)(2,1)} %get-tuple-element.200, bf16[2048,2304]{1,0:T(8,128)(2,1)} %all-gather.5.cloned.1.call-done), kind=kOutput, calls=%fused_computation.23 | convolution fusion | flops 9666035712 | bytes 18350080 | tf_op jit(solution)/shard_map/dot_general | solution.py:21
  439.2 22.7 %fusion.6 = (bf16[1024,2048]{1,0:T(8,128)(2,1)}, bf16[1024,2048]{1,0:T(8,128)(2,1)}) fusion(f32[1024,2048]{1,0:T(8,128)} %fusion.192, f32[1024,2048]{1,0:T(8,128)} %get-tuple-element.443, bf16[2048,2304]{1,0:T(8,128)(2,1)} %all-gather.5.cloned.1.call-done, bf16[1024,256]{1,0:T(8,128)(2,1)S(1)} %copy.80, bf16[1024,2048]{1,0:T(8,128)(2,1)} %copy-done.114), kind=kOutput, calls=%fused_computation.14 | convolution fusion | flops 9723445248 | bytes 39321600 | tf_op jit(solution)/shard_map/dot_general | solution.py:25
  461.9 13.7 %fusion.218 = f32[1024,2304]{1,0:T(8,128)S(1)} fusion(bf16[1024,2048]{1,0:T(8,128)(2,1)} %get-tuple-element.206, bf16[2048,2304]{1,0:T(8,128)(2,1)} %all-gather.9.cloned.1.call-done), kind=kOutput, calls=%fused_computation.600 | convolution fusion | flops 9663676416 | bytes 23068672 | tf_op jit(solution)/shard_map/dot_general | solution.py:21
  475.6 12.2 %add_convert_fusion = bf16[1024,2304]{1,0:T(8,128)(2,1)S(1)} fusion(f32[1024,2304]{1,0:T(8,128)S(1)} %fusion.218, bf16[1024,2048]{1,0:T(8,128)(2,1)S(1)} %copy-done.134, bf16[2048,2304]{1,0:T(8,128)(2,1)} %all-gather.7.cloned.1.call-done), kind=kOutput, calls=%fused_computation.7 | convolution fusion | flops 9668395008 | bytes 27787264 | tf_op jit(solution)/shard_map/dot_general | solution.py:21
  489.3 17.6 %collective-permute-start.46 = (bf16[2,2,128,1152]{3,2,0,1:T(8,128)(2,1)}, bf16[2,2,128,1152]{3,2,0,1:T(8,128)(2,1)S(1)}, u32[]{:S(2)}, u32[]{:S(2)}) collective-permute-start(bf16[2,2,128,1152]{3,2,0,1:T(8,128)(2,1)} %bitcast.611), channel_id=1, source_target_pairs={{0,2},{2,0},{1,3},{3,1},{4,6},{6,4},{5,7},{7,5},{8,10},{10,8},{9,1... | collective-permute-start | bytes 3538952 | tf_op jit(solution)/shard_map/ppermute | solution.py:72
  508.8 13.0 %convolution_convert_fusion.1 = bf16[2048,2304]{1,0:T(8,128)(2,1)} fusion(bf16[1024,2048]{1,0:T(8,128)(2,1)S(1)} %copy-done.135, bf16[1024,256]{1,0:T(8,128)(2,1)S(1)} %copy-done.132, bf16[1024,2048]{1,0:T(8,128)(2,1)S(1)} %copy-done.112), kind=kOutput, calls=%fused_computation.5 | convolution fusion | flops 9677832192 | bytes 18350080 | tf_op jit(solution)/shard_map/dot_general | solution.py:31
  521.8 15.5 %convolution_convert_fusion.2 = bf16[2048,2304]{1,0:T(8,128)(2,1)} fusion(bf16[1024,2048]{1,0:T(8,128)(2,1)} %get-tuple-element.200, bf16[1024,256]{1,0:T(8,128)(2,1)} %copy-done.86, bf16[1024,2048]{1,0:T(8,128)(2,1)} %copy-done.114), kind=kOutput, calls=%fused_computation.6 | convolution fusion | flops 9677832192 | bytes 18350080 | tf_op jit(solution)/shard_map/dot_general | solution.py:31
  537.4 9.5 %collective-permute-done.46 = bf16[2,2,128,1152]{3,2,0,1:T(8,128)(2,1)S(1)} collective-permute-done((bf16[2,2,128,1152]{3,2,0,1:T(8,128)(2,1)}, bf16[2,2,128,1152]{3,2,0,1:T(8,128)(2,1)S(1)}, u32[]{:S(2)}, u32[]{:S(2)}) %collective-permute-start.46) | collective-permute-done | bytes 1179680 | tf_op jit(solution)/shard_map/ppermute | solution.py:72
  554.6 13.3 %convolution_convert_fusion = bf16[2048,2304]{1,0:T(8,128)(2,1)} fusion(bf16[1024,2048]{1,0:T(8,128)(2,1)S(1)} %copy-done.136, bf16[1024,256]{1,0:T(8,128)(2,1)S(1)} %copy-done.133, bf16[1024,2048]{1,0:T(8,128)(2,1)S(1)} %copy-done.113), kind=kOutput, calls=%fused_computation.4 | convolution fusion | flops 9677832192 | bytes 18350080 | tf_op jit(solution)/shard_map/dot_general | solution.py:31
  567.9 11.5 %collective-permute-done.48 = bf16[2,128,1152]{2,1,0:T(8,128)(2,1)} collective-permute-done((bf16[2,128,1152]{2,1,0:T(8,128)(2,1)}, bf16[2,128,1152]{2,1,0:T(8,128)(2,1)}, u32[]{:S(2)}, u32[]{:S(2)}) %collective-permute-start.48) | collective-permute-done | bytes 589856 | tf_op jit(solution)/shard_map/ppermute | solution.py:72
  585.0 3.6 collective-permute-done.50
  588.5 9.5 %collective-permute-done.49 = bf16[128,1152]{1,0:T(8,128)(2,1)S(1)} collective-permute-done((bf16[128,1152]{1,0:T(8,128)(2,1)S(1)}, bf16[128,1152]{1,0:T(8,128)(2,1)S(1)}, u32[]{:S(2)}, u32[]{:S(2)}) %collective-permute-start.49) | collective-permute-done | bytes 294944 | tf_op jit(solution)/shard_map/ppermute | solution.py:72
  631.2 18.8 %collective-permute-done.55 = bf16[2,2,2,64,1024]{4,3,1,0,2:T(8,128)(2,1)S(1)} collective-permute-done((bf16[2,2,2,64,1024]{4,3,1,0,2:T(8,128)(2,1)S(1)}, bf16[2,2,2,64,1024]{4,3,1,0,2:T(8,128)(2,1)S(1)}, u32[]{:S(2)}, u32[]{:S(2)}) %collective-permute-start.55) | collective-permute-done | bytes 1048608 | tf_op jit(solution)/shard_map/ppermute | solution.py:72
  675.9 10.2 %collective-permute-done.58 = bf16[2,2,2,128,256]{4,3,0,1,2:T(8,128)(2,1)S(1)} collective-permute-done((bf16[2,2,2,128,256]{4,3,0,1,2:T(8,128)(2,1)S(1)}, bf16[2,2,2,128,256]{4,3,0,1,2:T(8,128)(2,1)S(1)}, u32[]{:S(2)}, u32[]{:S(2)}) %collective-permute-start.58) | collective-permute-done | bytes 524320 | tf_op jit(solution)/shard_map/ppermute | solution.py:72
  693.9 9.6 %collective-permute-done.66 = bf16[2,64,256]{2,1,0:T(8,128)(2,1)S(1)} collective-permute-done((bf16[2,64,256]{2,1,0:T(8,128)(2,1)S(1)}, bf16[2,64,256]{2,1,0:T(8,128)(2,1)S(1)}, u32[]{:S(2)}, u32[]{:S(2)}) %collective-permute-start.66) | collective-permute-done | bytes 65568 | tf_op jit(solution)/shard_map/ppermute | solution.py:72
  709.8 8.1 collective-permute-done.70
  721.3 3.9 collective-permute-done.67
  748.8 6.6 concatenate.134
  755.4 3.6 convolution_convert_fusion.9
  770.7 11.4 %collective-permute-done.81 = bf16[2,2,64,1024]{3,2,1,0:T(8,128)(2,1)S(1)} collective-permute-done((bf16[2,2,64,1024]{3,2,1,0:T(8,128)(2,1)S(1)}, bf16[2,2,64,1024]{3,2,1,0:T(8,128)(2,1)S(1)}, u32[]{:S(2)}, u32[]{:S(2)}) %collective-permute-start.81) | collective-permute-done | bytes 524320 | tf_op jit(solution)/shard_map/ppermute | solution.py:72
  790.9 6.7 collective-permute-done.83
  797.6 13.1 %collective-permute-done.82 = bf16[2,64,1024]{2,1,0:T(8,128)(2,1)S(1)} collective-permute-done((bf16[2,64,1024]{2,1,0:T(8,128)(2,1)S(1)}, bf16[2,64,1024]{2,1,0:T(8,128)(2,1)S(1)}, u32[]{:S(2)}, u32[]{:S(2)}) %collective-permute-start.82) | collective-permute-done | bytes 262176 | tf_op jit(solution)/shard_map/ppermute | solution.py:72
  819.1 3.9 collective-permute-done.87
  827.6 8.1 collective-permute-done.90
  839.1 8.2 shard_map.287
  853.8 4.1 slice_convert_fusion
  (807 shorter events, 337.9 us)
Async XLA Ops:
  7.2 112.9 %all-gather.5.cloned.1.call-start = ((), (), s32[]{:S(2)}) async-start(), calls=%async_computation.4 | async-start | bytes 11796480 | tf_op jit(solution)/shard_map/all_gather | solution.py:250
  27.4 138.4 %all-gather.7.cloned.1.call-start = ((), (), s32[]{:S(2)}) async-start(), calls=%async_computation.5 | async-start | bytes 11796480 | tf_op jit(solution)/shard_map/all_gather | solution.py:250
  32.5 21.1 %collective-permute-start.6 = (bf16[2,64,1024]{2,1,0:T(8,128)(2,1)S(1)}, bf16[2,64,1024]{2,1,0:T(8,128)(2,1)S(1)}, u32[]{:S(2)}, u32[]{:S(2)}) collective-permute-start(bf16[2,64,1024]{2,1,0:T(8,128)(2,1)S(1)} %pad_maximum_fusion.42), channel_id=1, source_target_pairs={{0,8},{8,0},{1,9},{9,1},{2,10},{10,2},{3,11},{11,3},{4,12},{12,4},... | collective-permute-start | bytes 786440 | tf_op jit(solution)/shard_map/ppermute | solution.py:72
  54.5 18.8 %collective-permute-start.11 = (bf16[2,2,64,1024]{3,2,1,0:T(8,128)(2,1)}, bf16[2,2,64,1024]{3,2,1,0:T(8,128)(2,1)S(1)}, u32[]{:S(2)}, u32[]{:S(2)}) collective-permute-start(bf16[2,2,64,1024]{3,2,1,0:T(8,128)(2,1)} %pad_maximum_fusion.33), channel_id=1, source_target_pairs={{0,4},{4,0},{1,5},{5,1},{2,6},{6,2},{3,7},{7,3},{8,12},{12,8},{9,1... | collective-permute-start | bytes 1572872 | tf_op jit(solution)/shard_map/ppermute | solution.py:72
  55.4 19.2 %collective-permute-start.10 = (bf16[2,2,64,1024]{3,2,1,0:T(8,128)(2,1)}, bf16[2,2,64,1024]{3,2,1,0:T(8,128)(2,1)S(1)}, u32[]{:S(2)}, u32[]{:S(2)}) collective-permute-start(bf16[2,2,64,1024]{3,2,1,0:T(8,128)(2,1)} %pad_maximum_fusion.32), channel_id=1, source_target_pairs={{0,2},{2,0},{1,3},{3,1},{4,6},{6,4},{5,7},{7,5},{8,10},{10,8},{9,1... | collective-permute-start | bytes 1572872 | tf_op jit(solution)/shard_map/ppermute | solution.py:72
  75.9 39.6 %collective-permute-start.15 = (bf16[2,2,2,64,1024]{4,3,2,1,0:T(8,128)(2,1)}, bf16[2,2,2,64,1024]{4,3,2,1,0:T(8,128)(2,1)}, u32[]{:S(2)}, u32[]{:S(2)}) collective-permute-start(bf16[2,2,2,64,1024]{4,3,2,1,0:T(8,128)(2,1)} %pad_maximum_fusion.23), channel_id=1, source_target_pairs={{0,1},{1,0},{2,3},{3,2},{4,5},{5,4},{6,7},{7,6},{8,9},{9,8},{10,11... | collective-permute-start | bytes 3145736 | tf_op jit(solution)/shard_map/ppermute | solution.py:72
  78.4 41.6 %collective-permute-start.14 = (bf16[2,2,2,64,1024]{4,3,2,1,0:T(8,128)(2,1)}, bf16[2,2,2,64,1024]{4,3,2,1,0:T(8,128)(2,1)}, u32[]{:S(2)}, u32[]{:S(2)}) collective-permute-start(bf16[2,2,2,64,1024]{4,3,2,1,0:T(8,128)(2,1)} %pad_maximum_fusion.22), channel_id=1, source_target_pairs={{0,1},{1,0},{2,3},{3,2},{4,5},{5,4},{6,7},{7,6},{8,9},{9,8},{10,11... | collective-permute-start | bytes 3145736 | tf_op jit(solution)/shard_map/ppermute | solution.py:72
  80.4 35.1 %collective-permute-start.13 = (bf16[2,2,2,8,6784]{4,3,2,1,0:T(8,128)(2,1)}, bf16[2,2,2,8,6784]{4,3,2,1,0:T(8,128)(2,1)S(1)}, u32[]{:S(2)}, u32[]{:S(2)}) collective-permute-start(bf16[2,2,2,8,6784]{4,3,2,1,0:T(8,128)(2,1)} %pad_maximum_fusion.26), channel_id=1, source_target_pairs={{0,4},{4,0},{1,5},{5,1},{2,6},{6,2},{3,7},{7,3},{8,12},{12,8},{9,1... | collective-permute-start | bytes 2605064 | tf_op jit(solution)/shard_map/ppermute | solution.py:72
  81.6 33.9 %collective-permute-start.12 = (bf16[2,2,2,64,768]{4,3,2,1,0:T(8,128)(2,1)S(1)}, bf16[2,2,2,64,768]{4,3,2,1,0:T(8,128)(2,1)}, u32[]{:S(2)}, u32[]{:S(2)}) collective-permute-start(bf16[2,2,2,64,768]{4,3,2,1,0:T(8,128)(2,1)S(1)} %pad_maximum_fusion.27), channel_id=1, source_target_pairs={{0,2},{2,0},{1,3},{3,1},{4,6},{6,4},{5,7},{7,5},{8,10},{10,8},{9,1... | collective-permute-start | bytes 2359304 | tf_op jit(solution)/shard_map/ppermute | solution.py:72
  82.3 172.8 %all-gather.9.cloned.1.call-start = ((), (), s32[]{:S(2)}) async-start(), calls=%async_computation.6 | async-start | bytes 11796480 | tf_op jit(solution)/shard_map/all_gather | solution.py:250
  85.0 77.2 %collective-permute-start.20 = (bf16[64,1280]{1,0:T(8,128)(2,1)}, bf16[64,1280]{1,0:T(8,128)(2,1)}, u32[]{:S(2)}, u32[]{:S(2)}) collective-permute-start(bf16[64,1280]{1,0:T(8,128)(2,1)} %pad_maximum_fusion.48), channel_id=1, source_target_pairs={{0,8},{8,0},{1,9},{9,1},{2,10},{10,2},{3,11},{11,3},{4,12},{12,4},... | collective-permute-start | bytes 491528 | tf_op jit(solution)/shard_map/ppermute | solution.py:72
  127.0 35.2 %collective-permute-start.21 = (bf16[64,1280]{1,0:T(8,128)(2,1)}, bf16[64,1280]{1,0:T(8,128)(2,1)}, u32[]{:S(2)}, u32[]{:S(2)}) collective-permute-start(bf16[64,1280]{1,0:T(8,128)(2,1)} %pad_maximum_fusion.49), channel_id=1, source_target_pairs={{0,4},{4,0},{1,5},{5,1},{2,6},{6,2},{3,7},{7,3},{8,12},{12,8},{9,1... | collective-permute-start | bytes 491528 | tf_op jit(solution)/shard_map/ppermute | solution.py:72
  131.1 19.9 %collective-permute-start.23 = (bf16[2,2,2,2,64,1024]{5,4,3,2,1,0:T(8,128)(2,1)}, bf16[2,2,2,2,64,1024]{5,4,3,2,1,0:T(8,128)(2,1)}, u32[]{:S(2)}, u32[]{:S(2)}) collective-permute-start(bf16[2,2,2,2,64,1024]{5,4,3,2,1,0:T(8,128)(2,1)} %pad_maximum_fusion.16), channel_id=1, source_target_pairs={{0,16},{16,0},{1,17},{17,1},{2,18},{18,2},{3,19},{19,3},{4,20},{20... | collective-permute-start | bytes 6291464 | tf_op jit(solution)/shard_map/ppermute | solution.py:72
  165.9 263.2 %all-gather.11.cloned.1.call-start = ((), (), s32[]{:S(2)}) async-start(), calls=%async_computation.7 | async-start | bytes 4718592 | tf_op jit(solution)/shard_map/all_gather | solution.py:382
  186.6 23.0 %collective-permute-start.31 = (bf16[2,2,64,1280]{3,2,1,0:T(8,128)(2,1)S(1)}, bf16[2,2,64,1280]{3,2,1,0:T(8,128)(2,1)S(1)}, u32[]{:S(2)}, u32[]{:S(2)}) collective-permute-start(bf16[2,2,64,1280]{3,2,1,0:T(8,128)(2,1)S(1)} %pad_maximum_fusion.29), channel_id=1, source_target_pairs={{0,2},{2,0},{1,3},{3,1},{4,6},{6,4},{5,7},{7,5},{8,10},{10,8},{9,1... | collective-permute-start | bytes 1966088 | tf_op jit(solution)/shard_map/ppermute | solution.py:72
  187.5 22.1 %collective-permute-start.30 = (bf16[2,2,64,1280]{3,2,1,0:T(8,128)(2,1)S(1)}, bf16[2,2,64,1280]{3,2,1,0:T(8,128)(2,1)S(1)}, u32[]{:S(2)}, u32[]{:S(2)}) collective-permute-start(bf16[2,2,64,1280]{3,2,1,0:T(8,128)(2,1)S(1)} %pad_maximum_fusion.28), channel_id=1, source_target_pairs={{0,1},{1,0},{2,3},{3,2},{4,5},{5,4},{6,7},{7,6},{8,9},{9,8},{10,11... | collective-permute-start | bytes 1966088 | tf_op jit(solution)/shard_map/ppermute | solution.py:72
  210.9 43.4 %collective-permute-start.35 = (bf16[2,2,2,64,1280]{4,3,2,1,0:T(8,128)(2,1)}, bf16[2,2,2,64,1280]{4,3,2,1,0:T(8,128)(2,1)}, u32[]{:S(2)}, u32[]{:S(2)}) collective-permute-start(bf16[2,2,2,64,1280]{4,3,2,1,0:T(8,128)(2,1)} %pad_maximum_fusion.20), channel_id=1, source_target_pairs={{0,1},{1,0},{2,3},{3,2},{4,5},{5,4},{6,7},{7,6},{8,9},{9,8},{10,11... | collective-permute-start | bytes 3932168 | tf_op jit(solution)/shard_map/ppermute | solution.py:72
  213.6 41.4 %collective-permute-start.34 = (bf16[2,2,2,64,1280]{4,3,2,1,0:T(8,128)(2,1)}, bf16[2,2,2,64,1280]{4,3,2,1,0:T(8,128)(2,1)}, u32[]{:S(2)}, u32[]{:S(2)}) collective-permute-start(bf16[2,2,2,64,1280]{4,3,2,1,0:T(8,128)(2,1)} %pad_maximum_fusion.19), channel_id=1, source_target_pairs={{0,2},{2,0},{1,3},{3,1},{4,6},{6,4},{5,7},{7,5},{8,10},{10,8},{9,1... | collective-permute-start | bytes 3932168 | tf_op jit(solution)/shard_map/ppermute | solution.py:72
  216.4 35.7 %collective-permute-start.33 = (bf16[2,2,2,128,256]{4,3,2,0,1:T(8,128)(2,1)}, bf16[2,2,2,128,256]{4,3,2,0,1:T(8,128)(2,1)}, u32[]{:S(2)}, u32[]{:S(2)}) collective-permute-start(bf16[2,2,2,128,256]{4,3,2,0,1:T(8,128)(2,1)} %pad_maximum_fusion.36), channel_id=1, source_target_pairs={{0,1},{1,0},{2,3},{3,2},{4,5},{5,4},{6,7},{7,6},{8,9},{9,8},{10,11... | collective-permute-start | bytes 1572872 | tf_op jit(solution)/shard_map/ppermute | solution.py:72
  217.9 36.4 %collective-permute-start.32 = (bf16[2,2,2,128,256]{4,3,0,1,2:T(8,128)(2,1)}, bf16[2,2,2,128,256]{4,3,0,1,2:T(8,128)(2,1)}, u32[]{:S(2)}, u32[]{:S(2)}) collective-permute-start(bf16[2,2,2,128,256]{4,3,0,1,2:T(8,128)(2,1)} %pad_maximum_fusion.35), channel_id=1, source_target_pairs={{0,4},{4,0},{1,5},{5,1},{2,6},{6,2},{3,7},{7,3},{8,12},{12,8},{9,1... | collective-permute-start | bytes 1572872 | tf_op jit(solution)/shard_map/ppermute | solution.py:72
  288.9 25.0 %collective-permute-start.38 = (bf16[128,2048]{1,0:T(8,128)(2,1)S(1)}, bf16[128,2048]{1,0:T(8,128)(2,1)S(1)}, u32[]{:S(2)}, u32[]{:S(2)}) collective-permute-start(bf16[128,2048]{1,0:T(8,128)(2,1)S(1)} %get-tuple-element.304), channel_id=1, source_target_pairs={{0,2},{2,0},{4,6},{6,4},{1,3},{3,1},{5,7},{7,5},{8,10},{10,8},{12,... | collective-permute-start | bytes 1572872 | tf_op jit(solution)/shard_map/ppermute | solution.py:72
  291.8 38.2 %collective-permute-start.39 = (bf16[128,2048]{1,0:T(8,128)(2,1)S(1)}, bf16[128,2048]{1,0:T(8,128)(2,1)S(1)}, u32[]{:S(2)}, u32[]{:S(2)}) collective-permute-start(bf16[128,2048]{1,0:T(8,128)(2,1)S(1)} %get-tuple-element.304), channel_id=1, source_target_pairs={{0,4},{2,6},{4,0},{6,2},{1,5},{3,7},{5,1},{7,3},{8,12},{10,14},{12... | collective-permute-start | bytes 1572872 | tf_op jit(solution)/shard_map/ppermute | solution.py:72
  292.4 37.6 %collective-permute-start.40 = (bf16[128,2048]{1,0:T(8,128)(2,1)S(1)}, bf16[128,2048]{1,0:T(8,128)(2,1)S(1)}, u32[]{:S(2)}, u32[]{:S(2)}) collective-permute-start(bf16[128,2048]{1,0:T(8,128)(2,1)S(1)} %get-tuple-element.304), channel_id=1, source_target_pairs={{0,6},{2,4},{4,2},{6,0},{1,7},{3,5},{5,3},{7,1},{8,14},{10,12},{12... | collective-permute-start | bytes 1572872 | tf_op jit(solution)/shard_map/ppermute | solution.py:72
  294.2 41.0 %collective-permute-start.41 = (bf16[128,2048]{1,0:T(8,128)(2,1)S(1)}, bf16[128,2048]{1,0:T(8,128)(2,1)S(1)}, u32[]{:S(2)}, u32[]{:S(2)}) collective-permute-start(bf16[128,2048]{1,0:T(8,128)(2,1)S(1)} %get-tuple-element.304), channel_id=1, source_target_pairs={{0,1},{1,0},{2,3},{3,2},{4,5},{5,4},{6,7},{7,6},{8,9},{9,8},{10,11... | collective-permute-start | bytes 1572872 | tf_op jit(solution)/shard_map/ppermute | solution.py:72
  330.0 217.6 %reduce-scatter.5.cloned.1.call-start = ((), (), s32[]{:S(2)}) async-start(), calls=%async_computation.8 | async-start | bytes 5308416 | tf_op jit(solution)/shard_map/reduce_scatter | solution.py:391
  330.7 31.2 %collective-permute-start.43 = (bf16[128,2048]{1,0:T(8,128)(2,1)S(1)}, bf16[128,2048]{1,0:T(8,128)(2,1)S(1)}, u32[]{:S(2)}, u32[]{:S(2)}) collective-permute-start(bf16[128,2048]{1,0:T(8,128)(2,1)S(1)} %collective-permute-done.39), channel_id=1, source_target_pairs={{0,1},{1,0},{2,3},{3,2},{4,5},{5,4},{6,7},{7,6},{8,9},{9,8},{10,11... | collective-permute-start | bytes 1572872 | tf_op jit(solution)/shard_map/ppermute | solution.py:72
  332.2 37.8 %collective-permute-start.44 = (bf16[128,2048]{1,0:T(8,128)(2,1)S(1)}, bf16[128,2048]{1,0:T(8,128)(2,1)S(1)}, u32[]{:S(2)}, u32[]{:S(2)}) collective-permute-start(bf16[128,2048]{1,0:T(8,128)(2,1)S(1)} %collective-permute-done.40), channel_id=1, source_target_pairs={{0,1},{1,0},{2,3},{3,2},{4,5},{5,4},{6,7},{7,6},{8,9},{9,8},{10,11... | collective-permute-start | bytes 1572872 | tf_op jit(solution)/shard_map/ppermute | solution.py:72
  429.1 221.9 %reduce-scatter.7.cloned.1.call-start = ((), (), s32[]{:S(2)}) async-start(), calls=%async_computation.9 | async-start | bytes 11796480 | tf_op jit(solution)/shard_map/reduce_scatter | solution.py:408
  489.3 57.5 %collective-permute-start.46 = (bf16[2,2,128,1152]{3,2,0,1:T(8,128)(2,1)}, bf16[2,2,128,1152]{3,2,0,1:T(8,128)(2,1)S(1)}, u32[]{:S(2)}, u32[]{:S(2)}) collective-permute-start(bf16[2,2,128,1152]{3,2,0,1:T(8,128)(2,1)} %bitcast.611), channel_id=1, source_target_pairs={{0,2},{2,0},{1,3},{3,1},{4,6},{6,4},{5,7},{7,5},{8,10},{10,8},{9,1... | collective-permute-start | bytes 3538952 | tf_op jit(solution)/shard_map/ppermute | solution.py:72
  508.2 38.6 %collective-permute-start.45 = (bf16[2,2,128,1152]{3,2,0,1:T(8,128)(2,1)}, bf16[2,2,128,1152]{3,2,0,1:T(8,128)(2,1)}, u32[]{:S(2)}, u32[]{:S(2)}) collective-permute-start(bf16[2,2,128,1152]{3,2,0,1:T(8,128)(2,1)} %copy.81), channel_id=1, source_target_pairs={{0,1},{1,0},{2,3},{3,2},{4,5},{5,4},{6,7},{7,6},{8,9},{9,8},{10,11... | collective-permute-start | bytes 3538952 | tf_op jit(solution)/shard_map/ppermute | solution.py:72
  547.9 213.8 %reduce-scatter.9.cloned.1.call-start = ((), (), s32[]{:S(2)}) async-start(), calls=%async_computation.10 | async-start | bytes 11796480 | tf_op jit(solution)/shard_map/reduce_scatter | solution.py:408
  550.5 28.9 %collective-permute-start.48 = (bf16[2,128,1152]{2,1,0:T(8,128)(2,1)}, bf16[2,128,1152]{2,1,0:T(8,128)(2,1)}, u32[]{:S(2)}, u32[]{:S(2)}) collective-permute-start(bf16[2,128,1152]{2,1,0:T(8,128)(2,1)} %slice_bitcast_fusion.3), channel_id=1, source_target_pairs={{0,4},{4,0},{1,5},{5,1},{2,6},{6,2},{3,7},{7,3},{8,12},{12,8},{9,1... | collective-permute-start | bytes 1769480 | tf_op jit(solution)/shard_map/ppermute | solution.py:72
  554.1 26.0 %collective-permute-start.47 = (bf16[2,128,1152]{2,1,0:T(8,128)(2,1)S(1)}, bf16[2,128,1152]{2,1,0:T(8,128)(2,1)}, u32[]{:S(2)}, u32[]{:S(2)}) collective-permute-start(bf16[2,128,1152]{2,1,0:T(8,128)(2,1)S(1)} %slice_bitcast_fusion.4), channel_id=1, source_target_pairs={{0,2},{2,0},{1,3},{3,1},{4,6},{6,4},{5,7},{7,5},{8,10},{10,8},{9,1... | collective-permute-start | bytes 1769480 | tf_op jit(solution)/shard_map/ppermute | solution.py:72
  619.5 31.6 %collective-permute-start.54 = (bf16[2,2,2,64,1280]{4,3,0,1,2:T(8,128)(2,1)S(1)}, bf16[2,2,2,64,1280]{4,3,0,1,2:T(8,128)(2,1)}, u32[]{:S(2)}, u32[]{:S(2)}) collective-permute-start(bf16[2,2,2,64,1280]{4,3,0,1,2:T(8,128)(2,1)S(1)} %dynamic-slice_bitcast_fusion), channel_id=1, source_target_pairs={{0,2},{2,0},{1,3},{3,1},{4,6},{6,4},{5,7},{7,5},{8,10},{10,8},{9,1... | collective-permute-start | bytes 3932168 | tf_op jit(solution)/shard_map/ppermute | solution.py:72
  625.0 25.0 %collective-permute-start.55 = (bf16[2,2,2,64,1024]{4,3,1,0,2:T(8,128)(2,1)S(1)}, bf16[2,2,2,64,1024]{4,3,1,0,2:T(8,128)(2,1)S(1)}, u32[]{:S(2)}, u32[]{:S(2)}) collective-permute-start(bf16[2,2,2,64,1024]{4,3,1,0,2:T(8,128)(2,1)S(1)} %dynamic-slice_bitcast_fusion.3), channel_id=1, source_target_pairs={{0,1},{1,0},{2,3},{3,2},{4,5},{5,4},{6,7},{7,6},{8,9},{9,8},{10,11... | collective-permute-start | bytes 3145736 | tf_op jit(solution)/shard_map/ppermute | solution.py:72
  651.1 202.8 %reduce-scatter.11.cloned.1.call-start = ((), (), s32[]{:S(2)}) async-start(), calls=%async_computation.11 | async-start | bytes 11796480 | tf_op jit(solution)/shard_map/reduce_scatter | solution.py:408
  665.1 21.1 %collective-permute-start.59 = (bf16[2,2,64,1280]{3,2,0,1:T(8,128)(2,1)S(1)}, bf16[2,2,64,1280]{3,2,0,1:T(8,128)(2,1)S(1)}, u32[]{:S(2)}, u32[]{:S(2)}) collective-permute-start(bf16[2,2,64,1280]{3,2,0,1:T(8,128)(2,1)S(1)} %dynamic-slice_bitcast_fusion.6), channel_id=1, source_target_pairs={{0,1},{1,0},{2,3},{3,2},{4,5},{5,4},{6,7},{7,6},{8,9},{9,8},{10,11... | collective-permute-start | bytes 1966088 | tf_op jit(solution)/shard_map/ppermute | solution.py:72
  665.5 20.7 %collective-permute-start.58 = (bf16[2,2,2,128,256]{4,3,0,1,2:T(8,128)(2,1)S(1)}, bf16[2,2,2,128,256]{4,3,0,1,2:T(8,128)(2,1)S(1)}, u32[]{:S(2)}, u32[]{:S(2)}) collective-permute-start(bf16[2,2,2,128,256]{4,3,0,1,2:T(8,128)(2,1)S(1)} %bitcast.670), channel_id=1, source_target_pairs={{0,2},{2,0},{1,3},{3,1},{4,6},{6,4},{5,7},{7,5},{8,10},{10,8},{9,1... | collective-permute-start | bytes 1572872 | tf_op jit(solution)/shard_map/ppermute | solution.py:72
  665.9 20.3 %collective-permute-start.57 = (bf16[2,2,2,128,256]{4,3,1,0,2:T(8,128)(2,1)S(1)}, bf16[2,2,2,128,256]{4,3,1,0,2:T(8,128)(2,1)S(1)}, u32[]{:S(2)}, u32[]{:S(2)}) collective-permute-start(bf16[2,2,2,128,256]{4,3,1,0,2:T(8,128)(2,1)S(1)} %bitcast.671), channel_id=1, source_target_pairs={{0,8},{8,0},{1,9},{9,1},{2,10},{10,2},{3,11},{11,3},{4,12},{12,4},... | collective-permute-start | bytes 1572872 | tf_op jit(solution)/shard_map/ppermute | solution.py:72
  703.5 28.3 %collective-permute-start.74 = (bf16[2,2,2,2,64,1024]{5,4,0,1,3,2:T(8,128)(2,1)S(1)}, bf16[2,2,2,2,64,1024]{5,4,0,1,3,2:T(8,128)(2,1)S(1)}, u32[]{:S(2)}, u32[]{:S(2)}) collective-permute-start(bf16[2,2,2,2,64,1024]{5,4,0,1,3,2:T(8,128)(2,1)S(1)} %bitcast.663), channel_id=1, source_target_pairs={{0,16},{16,0},{1,17},{17,1},{2,18},{18,2},{3,19},{19,3},{4,20},{20... | collective-permute-start | bytes 6291464 | tf_op jit(solution)/shard_map/ppermute | solution.py:72
  703.5 28.3 %collective-permute-start.75 = (bf16[2,2,2,2,64,1024]{5,4,1,0,2,3:T(8,128)(2,1)S(1)}, bf16[2,2,2,2,64,1024]{5,4,1,0,2,3:T(8,128)(2,1)S(1)}, u32[]{:S(2)}, u32[]{:S(2)}) collective-permute-start(bf16[2,2,2,2,64,1024]{5,4,1,0,2,3:T(8,128)(2,1)S(1)} %bitcast.662), channel_id=1, source_target_pairs={{0,16},{16,0},{1,17},{17,1},{2,18},{18,2},{3,19},{19,3},{4,20},{20... | collective-permute-start | bytes 6291464 | tf_op jit(solution)/shard_map/ppermute | solution.py:72
  734.1 24.9 %collective-permute-start.77 = (bf16[2,2,2,64,1024]{4,3,1,0,2:T(8,128)(2,1)}, bf16[2,2,2,64,1024]{4,3,1,0,2:T(8,128)(2,1)}, u32[]{:S(2)}, u32[]{:S(2)}) collective-permute-start(bf16[2,2,2,64,1024]{4,3,1,0,2:T(8,128)(2,1)} %dynamic-slice_bitcast_fusion.1), channel_id=1, source_target_pairs={{0,1},{1,0},{2,3},{3,2},{4,5},{5,4},{6,7},{7,6},{8,9},{9,8},{10,11... | collective-permute-start | bytes 3145736 | tf_op jit(solution)/shard_map/ppermute | solution.py:72
  738.2 23.5 %collective-permute-start.76 = (bf16[2,2,2,64,1024]{4,3,0,1,2:T(8,128)(2,1)}, bf16[2,2,2,64,1024]{4,3,0,1,2:T(8,128)(2,1)}, u32[]{:S(2)}, u32[]{:S(2)}) collective-permute-start(bf16[2,2,2,64,1024]{4,3,0,1,2:T(8,128)(2,1)} %dynamic-slice_bitcast_fusion.2), channel_id=1, source_target_pairs={{0,2},{2,0},{1,3},{3,1},{4,6},{6,4},{5,7},{7,5},{8,10},{10,8},{9,1... | collective-permute-start | bytes 3145736 | tf_op jit(solution)/shard_map/ppermute | solution.py:72
  764.2 21.5 %collective-permute-start.79 = (bf16[2,2,2,2,8,6784]{5,4,1,0,2,3:T(8,128)(2,1)S(1)}, bf16[2,2,2,2,8,6784]{5,4,1,0,2,3:T(8,128)(2,1)S(1)}, u32[]{:S(2)}, u32[]{:S(2)}) collective-permute-start(bf16[2,2,2,2,8,6784]{5,4,1,0,2,3:T(8,128)(2,1)S(1)} %bitcast.665), channel_id=1, source_target_pairs={{0,16},{16,0},{1,17},{17,1},{2,18},{18,2},{3,19},{19,3},{4,20},{20... | collective-permute-start | bytes 5210120 | tf_op jit(solution)/shard_map/ppermute | solution.py:72
  765.2 20.6 %collective-permute-start.78 = (bf16[2,2,2,2,64,768]{5,4,0,1,3,2:T(8,128)(2,1)S(1)}, bf16[2,2,2,2,64,768]{5,4,0,1,3,2:T(8,128)(2,1)S(1)}, u32[]{:S(2)}, u32[]{:S(2)}) collective-permute-start(bf16[2,2,2,2,64,768]{5,4,0,1,3,2:T(8,128)(2,1)S(1)} %bitcast.666), channel_id=1, source_target_pairs={{0,16},{16,0},{1,17},{17,1},{2,18},{18,2},{3,19},{19,3},{4,20},{20... | collective-permute-start | bytes 4718600 | tf_op jit(solution)/shard_map/ppermute | solution.py:72
  786.2 25.3 %collective-permute-start.85 = (bf16[2,2,2,8,6784]{4,3,1,0,2:T(8,128)(2,1)S(1)}, bf16[2,2,2,8,6784]{4,3,1,0,2:T(8,128)(2,1)S(1)}, u32[]{:S(2)}, u32[]{:S(2)}) collective-permute-start(bf16[2,2,2,8,6784]{4,3,1,0,2:T(8,128)(2,1)S(1)} %dynamic-slice_bitcast_fusion.4), channel_id=1, source_target_pairs={{0,1},{1,0},{2,3},{3,2},{4,5},{5,4},{6,7},{7,6},{8,9},{9,8},{10,11... | collective-permute-start | bytes 2605064 | tf_op jit(solution)/shard_map/ppermute | solution.py:72
  787.1 24.4 %collective-permute-start.84 = (bf16[2,2,2,64,768]{4,3,0,1,2:T(8,128)(2,1)S(1)}, bf16[2,2,2,64,768]{4,3,0,1,2:T(8,128)(2,1)S(1)}, u32[]{:S(2)}, u32[]{:S(2)}) collective-permute-start(bf16[2,2,2,64,768]{4,3,0,1,2:T(8,128)(2,1)S(1)} %dynamic-slice_bitcast_fusion.5), channel_id=1, source_target_pairs={{0,2},{2,0},{1,3},{3,1},{4,6},{6,4},{5,7},{7,5},{8,10},{10,8},{9,1... | collective-permute-start | bytes 2359304 | tf_op jit(solution)/shard_map/ppermute | solution.py:72
  789.3 21.4 %collective-permute-start.82 = (bf16[2,64,1024]{2,1,0:T(8,128)(2,1)S(1)}, bf16[2,64,1024]{2,1,0:T(8,128)(2,1)S(1)}, u32[]{:S(2)}, u32[]{:S(2)}) collective-permute-start(bf16[2,64,1024]{2,1,0:T(8,128)(2,1)S(1)} %dynamic-slice_bitcast_fusion.14), channel_id=1, source_target_pairs={{0,4},{4,0},{1,5},{5,1},{2,6},{6,2},{3,7},{7,3},{8,12},{12,8},{9,1... | collective-permute-start | bytes 786440 | tf_op jit(solution)/shard_map/ppermute | solution.py:72
  (197 other events, 1927.6 us)
Sparse Core Ops, SparseCore 0:
  27.5 72.0 all-gather.4
  101.7 64.0 all-gather.6
  168.0 64.5 all-gather.8
  330.1 86.9 all-gather.10
  429.2 118.3 reduce-scatter.4
  550.0 77.2 reduce-scatter.6
  651.2 91.2 reduce-scatter.8
  761.9 91.9 reduce-scatter.10
